TPU v7x, 32 devices: a whole 2x2x4 slice. The times are simulated.
32 devices in a mesh: seq: 16 (over z, x, core), head: 2 (over y).
Axes of the slice: x: 2, y: 2, z: 4, core: 2. Of those that a mesh axis runs over, the one named last changes fastest.
Arguments:
- sparse_query: bfloat16 [4096, 8192], P('seq', 'head'), may hold values from -62 to 62
- sparse_key: bfloat16 [4096, 1024], P('seq', 'head'), may hold values from -5 to 5
- sparse_value: bfloat16 [4096, 1024], P('seq', 'head'), may hold values from -5 to 5
- light_query: bfloat16 [4096, 8192], P('seq', 'head'), may hold values from -60 to 60
- light_key: bfloat16 [4096, 8192], P('seq', 'head'), may hold values from -0.5 to 0.5
- log_decay: float32 [64, 4096], P('head', 'seq'), may hold values from -1 to 0
- segments: int32 [4096], P('seq'), may hold values from 0 to 3, never falling along the last dimension, each value on 1 to 2048 neighbouring positions
- block_list: int32 [32, 12], P('seq'), may hold values from -1 to 29, as said below
Outputs:
- sparse_out: bfloat16 [4096, 8192], P('seq', 'head')
- mixed_out: bfloat16 [4096, 8192], P('seq', 'head')
Inputs may be any that keep to these rules, and one draw needn't show every extreme that they name: `block_list`: entry -1 names no block. Every other entry of row b names a block of an earlier aligned group of 256 tokens than the group that holds block b; the rows of one aligned group of 256 tokens together name at most one block of any other group, and name it at most once. Some row names 12 blocks. `segments`: document ids may be packed several to a wider word wherever they travel.
All inputs are finite; a program needn't handle non-finite values.
Results may differ from a plain program's by a relative error of at most 0.0057.
Values may be sent and summed in bfloat16 or wider, within the bound.
No kernel may reach another device: no remote copies, remote signals or barrier semaphores. Data moves between devices by JAX's collectives and lax.ppermute only.
A program may use at most 128 MiB of HBM per device.

v0:
```python
import jax
import jax.numpy as jnp
from jax import lax
from jax.sharding import PartitionSpec as P

ASKER_CHANNELS = 64
HD = 128
BLK = 128


big_negative = -1e30
norm_eps = 1e-06


def passed_along(value, axis, by):
    size = lax.axis_size(axis)
    pairs = [(i, i + by) for i in range(size) if 0 <= i + by < size]
    return lax.ppermute(value, axis, pairs)


def carried_in(value, axis, join, neutral):
    count, mine = (lax.axis_size(axis), lax.axis_index(axis))
    pieces = jax.tree.map(lambda part: lax.all_gather(part, axis), value)
    subtotal = jax.tree.map(
        lambda part, zero: jnp.full_like(part, 0) + jnp.asarray(zero, part.dtype), value, neutral
    )

    def turn(position, subtotal):
        longer = join(subtotal, jax.tree.map(lambda part: part[position], pieces))
        return jax.tree.map(lambda new, old: jnp.where(position < mine, new, old), longer, subtotal)

    return lax.fori_loop(0, count - 1, turn, subtotal)


def attend_block(query, own_kv, own_seg, picked_kv, picked_seg, picked_ok):
    row_count = query.shape[0]
    kv_width = own_kv.shape[1] // 2
    kv_heads = kv_width // HD
    group_size = query.shape[1] // kv_width
    list_count = picked_kv.shape[0]
    keys_all = jnp.concatenate(
        [own_kv, picked_kv.reshape(list_count * row_count, 2 * kv_width)], axis=0
    )
    seg_all = jnp.concatenate([own_seg, picked_seg.reshape(list_count * row_count)])
    queries = query.reshape(row_count, kv_heads, group_size, HD)
    key_part = keys_all[:, :kv_width].reshape(-1, kv_heads, HD)
    value_part = keys_all[:, kv_width:].reshape(-1, kv_heads, HD)
    scores = jnp.einsum(
        "qkgd,nkd->kgqn", queries, key_part, preferred_element_type=jnp.float32
    ) * HD ** (-0.5)
    places = jnp.arange(row_count)
    causal = places[None, :] <= places[:, None]
    listed_ok = jnp.broadcast_to(
        jnp.repeat(picked_ok, row_count)[None, :], (row_count, list_count * row_count)
    )
    allowed = jnp.concatenate([causal, listed_ok], axis=1) & (seg_all[None, :] == own_seg[:, None])
    scores = jnp.where(allowed[None, None], scores, big_negative)
    highest = jnp.max(scores, axis=-1, keepdims=True)
    lifted = jnp.exp(scores - highest)
    weights = (lifted / jnp.sum(lifted, axis=-1, keepdims=True)).astype(jnp.bfloat16)
    result = jnp.einsum("kgqn,nkd->qkgd", weights, value_part, preferred_element_type=jnp.float32)
    return result.astype(jnp.bfloat16).reshape(row_count, kv_heads * group_size * HD)


def light_local(queries, keyed, valued, rates, doc_ids, prior_doc):
    running = jnp.cumsum(rates, axis=1)
    block_total = running[:, -1]
    places = jnp.arange(doc_ids.shape[0])
    spread = running[:, :, None] - running[:, None, :]
    visible = (places[None, :] <= places[:, None]) & (doc_ids[None, :] == doc_ids[:, None])
    decay_mask = jnp.where(visible[None], jnp.exp(jnp.minimum(spread, 0.0)), 0.0)
    scores = jnp.einsum("thd,shd->hts", queries, keyed, preferred_element_type=jnp.float32)
    weights = (scores * decay_mask).astype(jnp.bfloat16)
    inside = jnp.einsum("hts,shd->thd", weights, valued, preferred_element_type=jnp.float32)
    reach_factor = jnp.exp(running) * (doc_ids == prior_doc).astype(jnp.float32)[None, :]
    fading = (
        jnp.exp(block_total[:, None] - running)
        * (doc_ids == doc_ids[-1]).astype(jnp.float32)[None, :]
    )
    scaled = keyed.astype(jnp.float32) * jnp.transpose(fading)[:, :, None]
    added_state = jnp.einsum(
        "shd,she->hde", scaled, valued.astype(jnp.float32), precision=lax.Precision.HIGHEST
    )
    carry_factor = jnp.exp(block_total) * (doc_ids[-1] == prior_doc).astype(jnp.float32)
    return (inside, reach_factor, added_state, carry_factor)


def chain_link(earlier, latter):
    return (earlier[0] * latter[0], latter[0][:, None, None] * earlier[1] + latter[1])


def body(
    sparse_query, sparse_key, sparse_value, light_query, light_key, log_decay, segments, block_list
):
    tokens_here = sparse_query.shape[0]
    block_count = tokens_here // BLK
    kv_width = sparse_key.shape[1]
    shard_count = lax.axis_size("seq")
    kv_local = jnp.concatenate([sparse_key, sparse_value], axis=1)
    local_blocks = kv_local.reshape(block_count, BLK, 2 * kv_width)
    seg_blocks = segments.reshape(block_count, BLK)
    owner_index = jnp.where(block_list >= 0, block_list // block_count, -1).reshape(-1)
    inner_index = (block_list % block_count).reshape(-1)
    owner_match = jnp.arange(shard_count)[:, None] == owner_index[None, :]
    wanted = jnp.max(jnp.where(owner_match, inner_index[None, :], -1), axis=1)
    wanted_safe = jnp.clip(wanted, 0, block_count - 1)
    owner_table = owner_index.reshape(block_count, block_list.shape[1])
    kv_portion = lax.all_gather(kv_local, "seq", axis=0, tiled=True)
    seg_portion = lax.all_gather(segments, "seq", axis=0, tiled=True)
    portion_shards = kv_portion.shape[0] // tokens_here
    kv_view = kv_portion.reshape(portion_shards, block_count, BLK, 2 * kv_width)
    seg_view = seg_portion.reshape(portion_shards, block_count, BLK)
    pick_block = wanted_safe[:, None] == jnp.arange(block_count)[None, :]
    owners_here = jnp.arange(portion_shards)
    owner_hit = owner_table[:, :, None] == owners_here[None, None, :]
    selector = owner_hit[:, :, :, None] & pick_block[None, None, :, :]
    new_kv = jnp.einsum(
        "bkpj,pjnc->bknc",
        selector.astype(jnp.bfloat16),
        kv_view,
        preferred_element_type=jnp.float32,
    )
    new_seg = jnp.sum(jnp.where(selector[:, :, :, :, None], seg_view[None, None], 0), axis=(2, 3))
    picked_kv = new_kv.astype(jnp.bfloat16)
    picked_seg = new_seg.astype(jnp.int32)
    picked_ok = block_list >= 0
    query_blocks = sparse_query.reshape(block_count, BLK, sparse_query.shape[1])
    sparse_out = jnp.concatenate(
        [
            attend_block(
                query_blocks[block_index],
                local_blocks[block_index],
                seg_blocks[block_index],
                picked_kv[block_index],
                picked_seg[block_index],
                picked_ok[block_index],
            )
            for block_index in range(block_count)
        ],
        axis=0,
    )
    heads_here = light_query.shape[1] // HD
    light_q = light_query.reshape(block_count, BLK, heads_here, HD)
    light_k = light_key.reshape(block_count, BLK, heads_here, HD)
    light_v = sparse_out.reshape(block_count, BLK, heads_here, HD)
    rate_blocks = log_decay.reshape(heads_here, block_count, BLK)
    before = passed_along(segments[tokens_here - 1 :] + 1, "seq", 1) - 1
    block_parts = []
    for block_index in range(block_count):
        prior_doc = before[0] if block_index == 0 else seg_blocks[block_index - 1, BLK - 1]
        block_parts.append(
            light_local(
                light_q[block_index],
                light_k[block_index],
                light_v[block_index],
                rate_blocks[:, block_index],
                seg_blocks[block_index],
                prior_doc,
            )
        )
    carried = jnp.zeros((heads_here, HD, HD), jnp.float32)
    passed = jnp.ones((heads_here,), jnp.float32)
    for block_item in block_parts:
        carried = block_item[3][:, None, None] * carried + block_item[2]
        passed = passed * block_item[3]
    entering = carried_in(
        (passed, carried), "seq", chain_link, (jnp.ones_like(passed), jnp.zeros_like(carried))
    )[1]
    outputs = []
    for block_index in range(block_count):
        inside, reach_factor, added_state, carry_factor = block_parts[block_index]
        outside = (
            jnp.einsum(
                "thd,hde->the",
                light_q[block_index].astype(jnp.float32),
                entering,
                precision=lax.Precision.HIGHEST,
            )
            * jnp.transpose(reach_factor)[:, :, None]
        )
        outputs.append(inside + outside)
        entering = carry_factor[:, None, None] * entering + added_state
    mixed_out = jnp.concatenate(outputs, axis=0).reshape(tokens_here, heads_here * HD)
    squares = lax.psum(jnp.sum(mixed_out * mixed_out, axis=1), "head")
    norm_scale = lax.rsqrt(squares / (ASKER_CHANNELS * HD) + norm_eps)
    return (sparse_out, (mixed_out * norm_scale[:, None]).astype(jnp.bfloat16))


def solution(mesh):
    in_specs = (
        P("seq", "head"),
        P("seq", "head"),
        P("seq", "head"),
        P("seq", "head"),
        P("seq", "head"),
        P("head", "seq"),
        P("seq"),
        P("seq", None),
    )
    out_specs = (P("seq", "head"), P("seq", "head"))
    return jax.shard_map(body, mesh=mesh, in_specs=in_specs, out_specs=out_specs, check_vma=False)
```

profile of v0, /device:TPU:0, one launch (start us, length us, event | category | flops | bytes accessed | tf_op | source)
XLA Modules:
  0.0 446.0 jit_solution(10736285755465180232)
XLA Ops:
  12.0 3.3 collective-permute-start
  16.4 23.1 %all-gather.2 = s32[16,1,256]{2,1,0:T(1,128)S(1)} all-gather(s32[1,1,256]{2,1,0:T(1,128)} %bitcast.191), channel_id=1, replica_groups=mesh['seq'=16,'head'=2] {'seq'}, dimensions={0}, use_global_device_ids=true | all-gather | bytes 17408 | tf_op jit(solution)/shard_map/all_gather | solution.py:109
  59.7 28.8 %all-gather.6.cloned.1.call-done = bf16[4096,1024]{1,0:T(8,128)(2,1)} async-done(((bf16[256,1024]{1,0:T(8,128)(2,1)}), bf16[4096,1024]{1,0:T(8,128)(2,1)}) %all-gather.6.cloned.1.call-update) | async-done | bytes 8388624 | tf_op jit(solution)/shard_map/all_gather | solution.py:108
  88.4 14.6 %bitcast_convert_fusion = bf16[2,12,128,1024]{3,1,2,0:T(8,128)(2,1)S(1)} fusion(bf16[16,2,128,1024]{3,2,1,0:T(8,128)(2,1)} %bitcast.162, pred[16,2]{0,1:T(4,128)(4,1)S(1)} %iota_compare_fusion.3, pred[2,12,16]{2,1,0:T(8,128)(4,1)S(1)} %iota_compare_fusion.1), kind=kOutput, calls=%fused_computation.13 | convolution fusion | flops 204473088 | bytes 14680480 | tf_op jit(solution)/shard_map/bkpj,pjnc->bknc/dot_general | solution.py:117
  107.9 2.9 pad_maximum_fusion.2
  110.8 3.7 copy.140
  114.5 14.5 %fusion.85 = f32[4,1664,128,8]{2,1,3,0:T(8,128)} fusion(bf16[1664,4,128,1]{0,2,3,1:T(8,128)(2,1)} %bitcast.165, bf16[128,4,8,128]{0,3,2,1:T(8,128)(2,1)} %bitcast.167), kind=kOutput, calls=%fused_computation.142 | convolution fusion | flops 1744830464 | bytes 30015488 | tf_op jit(solution)/shard_map/qkgd,nkd->kgqn/dot_general | solution.py:48
  129.0 11.3 %fusion.84 = f32[4,8,128]{2,1,0:T(8,128)S(1)} fusion(pred[128,1664]{0,1:T(8,128)(4,1)} %get-tuple-element.160, bf16[1664,4,128,1]{0,2,3,1:T(8,128)(2,1)} %bitcast.166, bf16[128,4,8,128]{0,3,2,1:T(8,128)(2,1)} %bitcast.168), kind=kOutput, calls=%fused_computation.141 | convolution fusion | flops 1772095104 | bytes 2981888 | tf_op jit(solution)/shard_map/sub | solution.py:59
  140.3 3.6 copy.137
  146.2 14.6 %fusion.86 = f32[4,1664,128,8]{2,1,3,0:T(8,128)} fusion(bf16[1664,4,128,1]{0,2,3,1:T(8,128)(2,1)} %bitcast.163, bf16[128,4,8,128]{0,3,2,1:T(8,128)(2,1)} %bitcast.169), kind=kOutput, calls=%fused_computation.143 | convolution fusion | flops 1744830464 | bytes 30015488 | tf_op jit(solution)/shard_map/qkgd,nkd->kgqn/dot_general | solution.py:48
  160.8 10.8 %fusion.83 = f32[4,8,128]{2,1,0:T(8,128)S(1)} fusion(pred[128,1664]{0,1:T(8,128)(4,1)} %get-tuple-element.161, bf16[1664,4,128,1]{0,2,3,1:T(8,128)(2,1)S(1)} %bitcast.164, bf16[128,4,8,128]{0,3,2,1:T(8,128)(2,1)} %bitcast.170), kind=kOutput, calls=%fused_computation.140 | convolution fusion | flops 1772095104 | bytes 2981888 | tf_op jit(solution)/shard_map/sub | solution.py:59
  174.0 16.0 %fusion.41 = bf16[4,128,8,128]{3,1,2,0:T(8,128)(2,1)} fusion(bf16[1664,4,128,1]{0,2,3,1:T(8,128)(2,1)} %bitcast.186, f32[4,8,128]{2,1,0:T(8,128)S(1)} %fusion.84, f32[4,1664,128,8]{2,1,3,0:T(8,128)} %fusion.85, pred[128,1664]{0,1:T(8,128)(4,1)} %get-tuple-element.160), kind=kOutput, calls=%fused_computation.57 | convolution fusion | flops 1779439232 | bytes 30244864 | tf_op jit(solution)/shard_map/kgqn,nkd->qkgd/dot_general | solution.py:61
  190.0 3.5 fusion.31
  193.5 17.0 %fusion.40 = bf16[4,128,8,128]{3,1,2,0:T(8,128)(2,1)} fusion(bf16[1664,4,128,1]{0,2,3,1:T(8,128)(2,1)} %bitcast.187, f32[4,8,128]{2,1,0:T(8,128)S(1)} %fusion.83, f32[4,1664,128,8]{2,1,3,0:T(8,128)} %fusion.86, pred[128,1664]{0,1:T(8,128)(4,1)} %get-tuple-element.161), kind=kOutput, calls=%fused_computation.56 | convolution fusion | flops 1779439232 | bytes 30244864 | tf_op jit(solution)/shard_map/kgqn,nkd->qkgd/dot_general | solution.py:61
  210.5 4.8 %multiply_add_fusion = f32[32,128,128]{2,1,0:T(8,128)} fusion(f32[32,128,128]{2,1,0:T(8,128)S(1)} %fusion.31, bf16[128,32,128]{0,2,1:T(8,128)(2,1)} %bitcast.182, bf16[128,32,128]{0,2,1:T(8,128)(2,1)S(1)} %bitcast.178, f32[128,32]{0,1:T(8,128)S(1)} %get-tuple-element.159, f32[32]{0:T(128)S(1)} %get-tuple-element.136, f32[32]{0:T(128)S(1)} %exponential_multiply_fusion.1), kind=kOutput, calls=%fused_computation.47 | convolution fusion | flops 807927808 | bytes 6308096 | tf_op jit(solution)/shard_map/shd,she->hde/dot_general | solution.py:81
  223.1 31.9 %all-reduce = f32[512]{0:T(512)S(1)} all-reduce(f32[512]{0:T(512)S(1)} %dynamic-update-slice), channel_id=2, replica_groups=mesh['seq'=16,'head'=2] {'seq'}, use_global_device_ids=true, to_apply=%add | all-reduce | flops 512 | bytes 4096
  259.7 4.8 %fusion.42 = f32[32,128,128]{1,2,0:T(8,128)} fusion(bf16[128,32,128]{0,2,1:T(8,128)(2,1)} %bitcast.181, bf16[128,32,128]{0,2,1:T(8,128)(2,1)} %bitcast.173, bf16[128,32,128]{0,2,1:T(8,128)(2,1)} %bitcast.175, f32[32,128]{1,0:T(8,128)S(1)} %copy-done.13, pred[128,128]{1,0:T(8,128)(4,1)S(1)} %copy.158), kind=kOutput, calls=%fused_computation.58 | convolution fusion | flops 271056896 | bytes 5275648 | tf_op jit(solution)/shard_map/hts,shd->thd/dot_general | solution.py:74
  264.4 4.4 fusion.43
  268.8 3.2 pad_maximum_fusion.1
  272.0 110.3 %all-gather.8.cloned.1.call-done = f32[512,128,128]{2,1,0:T(8,128)} async-done(((f32[32,128,128]{2,1,0:T(8,128)}), f32[512,128,128]{2,1,0:T(8,128)}) %all-gather.8.cloned.1.call-update) | async-done | bytes 33554448 | tf_op jit(solution)/shard_map/all_gather | solution.py:23
  382.3 32.0 %while.14 = (s32[]{:T(128)}, f32[32,128,128]{2,1,0:T(8,128)S(1)}, s32[]{:T(128)}, f32[16,32]{1,0:T(8,128)S(1)}, f32[16,32,128,128]{3,2,1,0:T(8,128)}, /*index=5*/s32[]{:T(128)}, s32[]{:T(128)}) while((s32[]{:T(128)}, f32[32,128,128]{2,1,0:T(8,128)S(1)}, s32[]{:T(128)}, f32[16,32]{1,0:T(8,128)S(1)}, ...), condition=%wide.region_9.10_spmd.clone, body=%wide.region_8.9_spmd.clone.sunk | while | flops 2097156 | bytes 6291945 | solution.py:32
  414.3 4.0 fusion.24
  423.0 5.6 %copy.172 = f32[256,32,128]{0,2,1:T(8,128)} copy(f32[256,32,128]{2,0,1:T(8,128)} %get-tuple-element.141) | data formatting | bytes 8388608 | tf_op jit(solution)/shard_map/concatenate | solution.py:183
  428.6 4.9 %psum.7 = f32[256]{0:T(256)S(1)} all-reduce(f32[256]{0:T(256)S(1)} %get-tuple-element.140), channel_id=1, replica_groups=mesh['seq'=16,'head'=2] {'head'}, use_global_device_ids=true, to_apply=%region_11.12 | all-reduce | flops 256 | bytes 2048 | tf_op jit(solution)/shard_map/psum | solution.py:184
  (139 shorter events, 85.7 us)
Async XLA Ops:
  7.2 81.2 %all-gather.6.cloned.1.call-start = ((), (), s32[]{:S(2)}) async-start(), calls=%async_computation | async-start | bytes 8912896 | tf_op jit(solution)/shard_map/all_gather | solution.py:108
  9.2 0.8 copy-start.5
  10.0 372.3 %all-gather.8.cloned.1.call-start = ((), (), s32[]{:S(2)}) async-start(), calls=%async_computation.1 | async-start | bytes 35651584 | tf_op jit(solution)/shard_map/all_gather | solution.py:23
  12.0 43.2 %collective-permute-start = (s32[1]{0:T(128)}, s32[1]{0:T(128)}, u32[]{:S(2)}, u32[]{:S(2)}) collective-permute-start(s32[1]{0:T(128)} %add.64), channel_id=1, source_target_pairs={{0,2},{2,4},{4,6},{6,8},{8,10},{10,12},{12,14},{14,16},{16,18},{18... | collective-permute-start | bytes 20 | tf_op jit(solution)/shard_map/ppermute | solution.py:18
  42.0 1.4 copy-start.17
  42.0 3.0 copy-start.16
  45.4 13.6 %copy-start.12 = (f32[32,128]{1,0:T(8,128)}, f32[32,128]{1,0:T(8,128)S(1)}, u32[]{:S(2)}) copy-start(f32[32,128]{1,0:T(8,128)S(1)} %reduce_window_sum.17) | copy-start | bytes 49156
  45.7 13.3 %copy-start.10 = (f32[32,128]{1,0:T(8,128)}, f32[32,128]{1,0:T(8,128)S(1)}, u32[]{:S(2)}) copy-start(f32[32,128]{1,0:T(8,128)S(1)} %reduce_window_sum.18) | copy-start | bytes 49156
  48.7 2.9 copy-start.6
  106.1 1.8 copy-start.8
  106.1 1.8 copy-start.9
  146.2 14.6 %copy-start.2 = (bf16[1664,512]{0,1:T(8,128)(2,1)S(1)}, bf16[1664,512]{0,1:T(8,128)(2,1)}, u32[]{:S(2)}) copy-start(bf16[1664,512]{0,1:T(8,128)(2,1)} %copy.147) | copy-start | bytes 5111812
  174.0 16.0 %copy-start.3 = (bf16[128,4096]{0,1:T(8,128)(2,1)S(1)}, bf16[128,4096]{0,1:T(8,128)(2,1)}, u32[]{:S(2)}) copy-start(bf16[128,4096]{0,1:T(8,128)(2,1)} %copy.201) | copy-start | bytes 3145732
  193.5 17.0 %copy-start = (f32[32,128,128]{2,1,0:T(8,128)}, f32[32,128,128]{2,1,0:T(8,128)S(1)}, u32[]{:S(2)}) copy-start(f32[32,128,128]{2,1,0:T(8,128)S(1)} %fusion.31) | copy-start | bytes 6291460
  193.5 17.0 %copy-start.4 = (bf16[128,4096]{0,1:T(8,128)(2,1)S(1)}, bf16[128,4096]{0,1:T(8,128)(2,1)}, u32[]{:S(2)}) copy-start(bf16[128,4096]{0,1:T(8,128)(2,1)} %copy.204) | copy-start | bytes 3145732
  218.3 3.2 copy-start.19
  255.0 4.6 %copy-start.13 = (f32[32,128]{1,0:T(8,128)S(1)}, f32[32,128]{1,0:T(8,128)}, u32[]{:S(2)}) copy-start(f32[32,128]{1,0:T(8,128)} %copy-done.12) | copy-start | bytes 49156
  259.7 4.8 %copy-start.11 = (f32[32,128]{1,0:T(8,128)S(1)}, f32[32,128]{1,0:T(8,128)}, u32[]{:S(2)}) copy-start(f32[32,128]{1,0:T(8,128)} %copy-done.10) | copy-start | bytes 49156
  382.3 32.0 %copy-start.15 = (f32[128,32]{0,1:T(8,128)S(1)}, f32[128,32]{0,1:T(8,128)}, u32[]{:S(2)}) copy-start(f32[128,32]{0,1:T(8,128)} %get-tuple-element.185) | copy-start | bytes 49156
  414.3 4.0 copy-start.1
  414.3 4.0 copy-start.7
  414.3 4.0 copy-start.14
  414.3 4.0 copy-start.18
Sparse Core Ops, SparseCore 0:
  10.7 77.6 all-gather.5
  215.5 166.7 all-gather.7
where the time goes:
time: 450 us; the launch traced here: 446 us
  waiting for transfers between devices  139 us (31%)
  matrix products  122 us (27%)
  blocking collectives  59.9 us (13%)
  local copies, waits for them, and re-layouts  51.5 us (11%)
  other arithmetic  50.9 us (11%)
  between operations  18.4 us (4%)
    all_gather x1, waiting for transfers between devices, carried_in(): pieces = jax.tree.map(lambda part: lax.all_gather(part, axis), value)  110 us
    dot_general x2, matrix products, attend_block(): jnp.einsum('kgqn,nkd->qkgd', weights, value_part, preferred_element_type=...  33 us
    unnamed x1, blocking collectives  31.9 us
    select_n x15, other arithmetic, turn(): jnp.where(position < mine, new, old)  31.4 us
    dot_general x2, matrix products, attend_block(): jnp.einsum('qkgd,nkd->kgqn', queries, key_part, preferred_element_type=jn...  29 us
    all_gather x1, waiting for transfers between devices, body(): kv_portion = lax.all_gather(kv_local, 'seq', axis=0, tiled=True)  28.8 us
    all_gather x1, blocking collectives, body(): seg_portion = lax.all_gather(segments, 'seq', axis=0, tiled=True)  23.1 us
    sub x2, matrix products, attend_block(): lifted = jnp.exp(scores - highest)  22.1 us
  transfers between devices with their start and end apart: 3, of which 2 were waited for; matrix products, arithmetic and copies ran while one was open for 10% of the time, Pallas kernels for 0%

commit v1 on v0

v1 whole, which is shorter than its diff:
```python
import functools

import jax
import jax.numpy as jnp
from jax import lax
from jax.experimental import pallas as pl
from jax.experimental.pallas import tpu as pltpu
from jax.sharding import PartitionSpec as P

ASKER_CHANNELS = 64
HD = 128
BLK = 128

NEG = -1e30
norm_eps = 1e-06
LOG2E = 1.4426950408889634
F32 = jnp.float32
BF16 = jnp.bfloat16


def nt(a, b):
    return lax.dot_general(a, b, (((1,), (1,)), ((), ())), preferred_element_type=F32)


def tn(a, b):
    return lax.dot_general(a, b, (((0,), (0,)), ((), ())), preferred_element_type=F32)


def nn(a, b):
    return lax.dot_general(a, b, (((1,), (0,)), ((), ())), preferred_element_type=F32)


def local_kernel(q_ref, k_ref, row_ref, col_ref, fade_ref, segc_ref, segr_ref, w_ref, kf_ref, bias):
    tokens = q_ref.shape[0]

    @pl.when(pl.program_id(0) == 0)
    def _():
        t = lax.broadcasted_iota(jnp.int32, (tokens, tokens), 0)
        s = lax.broadcasted_iota(jnp.int32, (tokens, tokens), 1)
        seen = (s <= t) & (segc_ref[...] == segr_ref[...])
        bias[...] = jnp.where(seen, 0.0, NEG)

    for i in range(w_ref.shape[0]):
        cols = slice(i * HD, (i + 1) * HD)
        k = k_ref[:, cols]
        spread = col_ref[0, :, i : i + 1] - row_ref[0, i : i + 1, :]
        w_ref[i] = (nt(q_ref[:, cols], k) * jnp.exp(spread + bias[...])).astype(BF16)
        kf_ref[:, cols] = (k.astype(F32) * fade_ref[0, :, i : i + 1]).astype(BF16)


def local_part(light_q, light_k, running, fading, segments, per_step):
    tokens, width = light_q.shape
    heads = width // HD
    steps = heads // per_step
    running_col = jnp.transpose(running.reshape(steps, per_step, tokens), (0, 2, 1))
    fading_col = jnp.transpose(fading.reshape(steps, per_step, tokens), (0, 2, 1))
    wide = pl.BlockSpec((tokens, per_step * HD), lambda g: (0, g))
    col = pl.BlockSpec((1, tokens, per_step), lambda g: (g, 0, 0))
    return pl.pallas_call(
        local_kernel,
        grid=(steps,),
        in_specs=[
            wide,
            wide,
            pl.BlockSpec((1, per_step, tokens), lambda g: (g, 0, 0)),
            col,
            col,
            pl.BlockSpec((tokens, 1), lambda g: (0, 0)),
            pl.BlockSpec((1, tokens), lambda g: (0, 0)),
        ],
        out_specs=[pl.BlockSpec((per_step, tokens, tokens), lambda g: (g, 0, 0)), wide],
        out_shape=[
            jax.ShapeDtypeStruct((heads, tokens, tokens), BF16),
            jax.ShapeDtypeStruct((tokens, width), BF16),
        ],
        scratch_shapes=[pltpu.VMEM((tokens, tokens), F32)],
        cost_estimate=pl.CostEstimate(
            flops=2 * heads * tokens * tokens * HD,
            bytes_accessed=3 * 2 * tokens * width + 2 * heads * tokens * tokens,
            transcendentals=heads * tokens * tokens,
        ),
        name="local_scores",
    )(
        light_q,
        light_k,
        running.reshape(steps, per_step, tokens),
        running_col,
        fading_col,
        segments[:, None],
        segments[None, :],
    )


def attend_kernel(group_sizes, table, *refs):
    pieces = len(group_sizes)
    q_ref, own_k, own_v, kf_ref, segc_ref, segr_ref = refs[:6]
    piece_k = refs[6 : 6 + pieces]
    piece_v = refs[6 + pieces : 6 + 2 * pieces]
    out_ref, state_ref, qs, scores, high, acc = refs[6 + 2 * pieces :]
    tokens, width = q_ref.shape
    blocks = tokens // BLK
    group = width // HD
    rows = group * BLK
    factor = HD ** (-0.5) * LOG2E
    ones = jnp.ones((BLK, HD), BF16)
    lane = lax.broadcasted_iota(jnp.int32, (BLK, BLK), 1)
    sub = lax.broadcasted_iota(jnp.int32, (BLK, BLK), 0)
    first_doc = table[0]

    def masked(score, ok):
        return jnp.where(ok[None], score.reshape(group, BLK, BLK), NEG).reshape(rows, BLK)

    for b in range(blocks):
        here = slice(b * BLK, (b + 1) * BLK)
        for h in range(group):
            qs[b, h * BLK : (h + 1) * BLK, :] = q_ref[here, h * HD : (h + 1) * HD]
        ok = (lane <= sub) & (segc_ref[here, :] == segr_ref[:, here])
        score = masked(nt(qs[b], own_k[here, :]), ok)
        scores[b] = score
        high[b] = score

    def each_piece(do):
        at = 0
        for i, size in enumerate(group_sizes):
            if size == 1:
                do(i, at, 0)
            else:

                def step(j, carry, i=i, at=at):
                    do(i, at + j, j)
                    return carry

                lax.fori_loop(0, size, step, 0)
            at += size

    def place(i, slot, j):
        base = 1 + 5 * slot
        start = pl.multiple_of(j * tokens + table[base + 2] * BLK, BLK)
        return table[base], table[base + 1], pl.ds(start, BLK), table[base + 3], table[base + 4]

    def first(i, slot, j):
        seen, b, span, least, to = place(i, slot, j)

        @pl.when(seen > 0)
        def _():
            here = pl.ds(pl.multiple_of(b * BLK, BLK), BLK)
            ok = (lane >= least) & (segc_ref[here, :] == first_doc)
            score = masked(nt(qs[b], piece_k[i][span, :]), ok)
            scores[blocks + to] = score
            high[b] = jnp.maximum(high[b], score)

    each_piece(first)

    for b in range(blocks):
        here = slice(b * BLK, (b + 1) * BLK)
        top = jnp.broadcast_to(jnp.max(high[b], axis=1, keepdims=True), (rows, BLK))
        high[b] = top
        weight = jnp.exp2((scores[b] - top) * factor).astype(BF16)
        acc[b] = nn(weight, jnp.concatenate([own_v[here, :], ones], axis=1))

    def second(i, slot, j):
        seen, b, span, least, to = place(i, slot, j)

        @pl.when(seen > 0)
        def _():
            weight = jnp.exp2((scores[blocks + to] - high[b]) * factor).astype(BF16)
            acc[b] += nn(weight, jnp.concatenate([piece_v[i][span, :], ones], axis=1))

    each_piece(second)

    for b in range(blocks):
        here = slice(b * BLK, (b + 1) * BLK)
        result = (acc[b, :, :HD] / acc[b, :, HD:]).astype(BF16)
        for h in range(group):
            out_ref[here, h * HD : (h + 1) * HD] = result[h * BLK : (h + 1) * BLK, :]
    for h in range(group):
        cols = slice(h * HD, (h + 1) * HD)
        state_ref[h] = tn(kf_ref[:, cols], out_ref[:, cols]).astype(BF16)


def attend_part(table, slots, query, own, faded, segments, pieces, chunk, chunks):
    tokens = query.shape[0]
    kv_here = own.shape[1] // (2 * HD)
    kv_heads = kv_here * chunks
    group = query.shape[1] // (kv_heads * HD)
    width = group * HD
    blocks = tokens // BLK
    sizes = tuple(p.shape[0] // tokens for p in pieces)
    first = chunk * kv_here

    def piece_specs(off):
        return [
            pl.BlockSpec((p.shape[0], HD), lambda g, table, off=off: (0, off + g)) for p in pieces
        ]

    def own_spec(off):
        return pl.BlockSpec((tokens, HD), lambda g, table: (0, off + g))

    wide = pl.BlockSpec((tokens, width), lambda g, table: (0, first + g))
    return pl.pallas_call(
        functools.partial(attend_kernel, sizes),
        grid_spec=pltpu.PrefetchScalarGridSpec(
            num_scalar_prefetch=1,
            grid=(kv_here,),
            in_specs=[
                wide,
                own_spec(0),
                own_spec(kv_here),
                wide,
                pl.BlockSpec((tokens, 1), lambda g, table: (0, 0)),
                pl.BlockSpec((1, tokens), lambda g, table: (0, 0)),
            ]
            + piece_specs(0)
            + piece_specs(kv_here),
            out_specs=[
                pl.BlockSpec((tokens, width), lambda g, table: (0, g)),
                pl.BlockSpec((group, HD, HD), lambda g, table: (g, 0, 0)),
            ],
            scratch_shapes=[
                pltpu.VMEM((blocks, group * BLK, HD), BF16),
                pltpu.VMEM((blocks + slots, group * BLK, BLK), F32),
                pltpu.VMEM((blocks, group * BLK, BLK), F32),
                pltpu.VMEM((blocks, group * BLK, 2 * HD), F32),
            ],
        ),
        out_shape=[
            jax.ShapeDtypeStruct((tokens, kv_here * width), BF16),
            jax.ShapeDtypeStruct((kv_here * group, HD, HD), BF16),
        ],
        compiler_params=pltpu.CompilerParams(vmem_limit_bytes=56 * 1024 * 1024),
        cost_estimate=pl.CostEstimate(
            flops=kv_here * group * 10 * 6 * BLK * BLK * HD,
            bytes_accessed=kv_here * (3 * 2 * tokens * width + 12 * 4 * tokens * HD),
            transcendentals=kv_here * group * 10 * BLK * BLK,
        ),
        name="attend",
    )(table, query, own, own, faded, segments[:, None], segments[None, :], *pieces, *pieces)


def output_kernel(w_ref, v_ref, q_ref, reach_ref, state_ref, out_ref, squares_ref):
    @pl.when(pl.program_id(0) == 0)
    def _():
        squares_ref[...] = jnp.zeros_like(squares_ref)

    total = squares_ref[...]
    for i in range(w_ref.shape[0]):
        cols = slice(i * HD, (i + 1) * HD)
        outside = nn(q_ref[:, cols], state_ref[i]) * reach_ref[0, :, i : i + 1]
        result = nn(w_ref[i], v_ref[:, cols]) + outside
        out_ref[:, cols] = result
        total += result * result
    squares_ref[...] = total


def output_part(weights, valued, light_q, reach, states, per_step, chunk, chunks):
    tokens, width = valued.shape
    heads = width // HD
    steps = heads // per_step
    first = chunk * steps
    all_steps = steps * chunks
    reach_col = jnp.transpose(reach.reshape(all_steps, per_step, tokens), (0, 2, 1))
    return pl.pallas_call(
        output_kernel,
        grid=(steps,),
        in_specs=[
            pl.BlockSpec((per_step, tokens, tokens), lambda g: (first + g, 0, 0)),
            pl.BlockSpec((tokens, per_step * HD), lambda g: (0, g)),
            pl.BlockSpec((tokens, per_step * HD), lambda g: (0, first + g)),
            pl.BlockSpec((1, tokens, per_step), lambda g: (first + g, 0, 0)),
            pl.BlockSpec((per_step, HD, HD), lambda g: (g, 0, 0)),
        ],
        out_specs=[
            pl.BlockSpec((tokens, per_step * HD), lambda g: (0, g)),
            pl.BlockSpec((tokens, HD), lambda g: (0, 0)),
        ],
        out_shape=[
            jax.ShapeDtypeStruct((tokens, width), F32),
            jax.ShapeDtypeStruct((tokens, HD), F32),
        ],
        cost_estimate=pl.CostEstimate(
            flops=heads * 2 * tokens * HD * (tokens + HD),
            bytes_accessed=heads * (2 * tokens * tokens + 8 * tokens * HD + 2 * HD * HD),
            transcendentals=0,
        ),
        name="outputs",
    )(weights, valued, light_q, reach_col, states)


def moved(value, pairs):
    return lax.ppermute(value, "seq", pairs)


def window_relay(own, shards):
    up = [(i, i + 4) for i in range(shards - 4)]
    cross = [(i, i ^ 2) for i in range(shards)]
    core = [(i, i ^ 1) for i in range(shards)]
    right = [(i, i ^ 2) for i in range(shards) if not i & 2]
    left = [(i, i ^ 2) for i in range(shards) if i & 2]
    below = moved(own, up)
    beside = moved(own, right)
    second = moved(below, up)
    below_beside = moved(below, cross)
    second_beside = moved(second, left)
    mine = [below, second, beside, below_beside, second_beside]
    return mine + [moved(part, core) for part in [own] + mine]


def window_owners(me):
    mine = jnp.stack([me - 4, me - 8, me ^ 2, (me ^ 2) - 4, (me ^ 2) - 8])
    usable = jnp.stack([me >= 0, me >= 0, (me & 2) > 0, me >= 0, (me & 2) == 0])
    far = jnp.stack([me ^ 1] + [(me ^ 1) - 4, (me ^ 1) - 8, me ^ 3, (me ^ 3) - 4, (me ^ 3) - 8])
    owners = jnp.concatenate([mine, far])
    usable = jnp.concatenate([usable, jnp.ones((1,), bool), usable])
    return jnp.where(usable, owners, -1)


def carried_in_planes(state, passing, me, shards):
    heads = state.shape[0]
    up = [(i, i + 4) for i in range(shards - 4)]
    cross = [(i, i ^ 2) for i in range(shards)]
    core = [(i, i ^ 1) for i in range(shards)]
    c, x = me & 1, (me >> 1) & 1
    halves = state.reshape(2, heads // 2, HD, HD)
    half_pass = passing.reshape(shards, 2, 2, heads // 4)[:, c]

    def pick(value, index):
        return lax.dynamic_index_in_dim(value, index, 0, keepdims=False)

    def times(factor, value):
        return factor[:, None, None] * value.astype(F32)

    def send(value, pairs):
        return moved(value.astype(BF16), pairs)

    plane = me & ~3
    near = pick(halves, c)
    far = send(pick(halves, 1 - c), core)
    core0 = jnp.where(c == 0, near, far)
    core1 = jnp.where(c == 0, far, near)

    def passed(position):
        return pick(half_pass, jnp.maximum(position, 0))

    flat = lambda p: p.reshape(heads // 2)
    chip = times(flat(passed((me & ~1) + 1)), core0) + core1.astype(F32)
    quarters = chip.reshape(2, heads // 4, HD, HD)
    near_q = pick(quarters, x)
    far_q = send(pick(quarters, 1 - x), cross).astype(F32)
    chip0 = jnp.where(x == 0, near_q, far_q)
    chip1 = jnp.where(x == 0, far_q, near_q)
    quarter = lambda p: pick(p, x)
    pass0 = quarter(passed(plane) * passed(plane + 1))
    pass1 = quarter(passed(plane + 2) * passed(plane + 3))
    plane_state = times(pass1, chip0) + chip1
    one_below = send(plane_state, up)
    two_below = send(one_below, up)
    lower = plane - 4
    pass_plane = quarter(passed(lower) * passed(lower + 1) * passed(lower + 2) * passed(lower + 3))
    entering0 = one_below.astype(F32) + times(pass_plane, two_below)
    entering1 = times(pass0, entering0) + chip0
    keep = jnp.where(x == 0, entering0, entering1).astype(BF16)
    got = send(jnp.where(x == 0, entering1, entering0), cross)
    both = jnp.where(
        x == 0, jnp.concatenate([keep, got], axis=0), jnp.concatenate([got, keep], axis=0)
    )
    after = times(flat(passed(me & ~1)), both) + core0.astype(F32)
    mine = jnp.where(c == 0, both, after.astype(BF16))
    other = send(jnp.where(c == 0, after, both.astype(F32)), core)
    return jnp.where(
        c == 0, jnp.concatenate([mine, other], axis=0), jnp.concatenate([other, mine], axis=0)
    )


def carried_in_any(state, passing, me, shards):
    states = lax.all_gather(state, "seq")
    place = jnp.arange(shards)

    def turn(j, total):
        part = passing[j][:, None, None] * total + states[j].astype(F32)
        return jnp.where(j < me, part, total)

    return lax.fori_loop(0, shards, turn, jnp.zeros(state.shape, F32)).astype(BF16)


def body(
    sparse_query, sparse_key, sparse_value, light_query, light_key, log_decay, segments, block_list
):
    tokens = sparse_query.shape[0]
    blocks = tokens // BLK
    kv_heads = sparse_key.shape[1] // HD
    heads = light_query.shape[1] // HD
    group = heads // kv_heads
    shards = lax.axis_size("seq")
    me = lax.axis_index("seq")
    planes = shards == 16
    chunks = 2 if kv_heads % 2 == 0 and planes else 1
    kv_chunk = kv_heads // chunks * HD
    head_chunk = heads // chunks

    owns = []
    pieces = []
    for chunk in range(chunks):
        cols = slice(chunk * kv_chunk, (chunk + 1) * kv_chunk)
        own = jnp.concatenate([sparse_key[:, cols], sparse_value[:, cols]], axis=1)
        owns.append(own)
        if planes:
            pieces.append(window_relay(own, shards))
        else:
            pieces.append([lax.all_gather(own, "seq", axis=0, tiled=True)])
    owners = window_owners(me) if planes else jnp.where(jnp.arange(shards) < me, jnp.arange(shards), -1)

    upper = (jnp.arange(tokens)[:, None] <= jnp.arange(tokens)[None, :]).astype(F32)
    running = jnp.dot(log_decay, upper, precision=lax.Precision.HIGHEST)
    totals = running[:, -1]
    counts = jnp.sum(segments[None, :] < jnp.arange(1, 4)[:, None], axis=1)
    info = jnp.concatenate(
        [totals, counts.astype(F32), segments[:1].astype(F32), segments[-1:].astype(F32)]
    )
    info = jnp.pad(info, (0, 128 - info.shape[0]))
    known = lax.all_to_all(jnp.broadcast_to(info, (shards, 128)), "seq", 0, 0, tiled=True)
    starts = jnp.concatenate([jnp.zeros((1,), F32), jnp.sum(known[:, heads : heads + 3], axis=0)])
    firsts, lasts = known[:, heads + 3], known[:, heads + 4]
    begins = jnp.sum(
        jnp.where(firsts[:, None] == jnp.arange(4)[None, :], starts[None, :], 0.0), axis=1
    )
    begun = begins < (jnp.arange(shards) * tokens).astype(F32)
    passing = jnp.exp(known[:, :heads]) * (begun & (firsts == lasts)).astype(F32)[:, None]

    first_doc, last_doc = segments[0], segments[-1]
    doc_begin = jnp.sum(jnp.where(jnp.arange(4) == first_doc, starts, 0.0)).astype(jnp.int32)
    carried_on = doc_begin < me * tokens
    fading = jnp.exp(totals[:, None] - running) * (segments == last_doc).astype(F32)[None, :]
    reach = jnp.exp(running) * ((segments == first_doc) & carried_on).astype(F32)[None, :]

    named = (block_list[None] >= 0) & (block_list[None] // blocks == owners[:, None, None])
    hit = jnp.sum(jnp.where(named, block_list[None] + 1, 0), axis=2)
    asker = jnp.sum(jnp.where(hit > 0, jnp.arange(blocks)[None, :], 0), axis=1)
    listed = jnp.sum(hit, axis=1) - 1
    least = doc_begin - listed * BLK
    seen = (listed >= 0) & (least < BLK)
    slots = min(owners.shape[0], blocks * block_list.shape[1])
    order = jnp.minimum(jnp.cumsum(seen.astype(jnp.int32)) - 1, slots - 1)
    order = jnp.maximum(order, 0)
    rows = jnp.stack(
        [seen.astype(jnp.int32), asker, jnp.maximum(listed, 0) % blocks, least, order], axis=1
    )
    table = jnp.concatenate([first_doc[None], rows.reshape(-1)]).astype(jnp.int32)

    weights, faded = local_part(light_query, light_key, running, fading, segments, group)

    outs, results, squares = [], [], 0.0
    for chunk in range(chunks):
        attended, state = attend_part(
            table, slots, sparse_query, owns[chunk], faded, segments, pieces[chunk], chunk, chunks
        )
        outs.append(attended)
        span = slice(chunk * head_chunk, (chunk + 1) * head_chunk)
        carry = carried_in_planes if planes else carried_in_any
        entering = carry(state, passing[:, span], me, shards)
        result, square = output_part(
            weights, attended, light_query, reach, entering, group, chunk, chunks
        )
        results.append(result)
        squares = squares + jnp.sum(square, axis=1)
    squares = lax.psum(squares, "head")
    scale = lax.rsqrt(squares / (ASKER_CHANNELS * HD) + norm_eps)
    mixed = jnp.concatenate([(r * scale[:, None]).astype(BF16) for r in results], axis=1)
    return (jnp.concatenate(outs, axis=1), mixed)


def solution(mesh):
    in_specs = (
        P("seq", "head"),
        P("seq", "head"),
        P("seq", "head"),
        P("seq", "head"),
        P("seq", "head"),
        P("head", "seq"),
        P("seq"),
        P("seq", None),
    )
    out_specs = (P("seq", "head"), P("seq", "head"))
    return jax.shard_map(body, mesh=mesh, in_specs=in_specs, out_specs=out_specs, check_vma=False)
```

time: 450 us -> 152 us (0.34)
  waiting for transfers between devices: 139 us -> 14.3 us
  matrix products: 122 us -> 0.2 us
  starting transfers between devices: 3.38 us -> 61.8 us
  blocking collectives: 59.9 us -> 4.94 us
  other arithmetic: 50.9 us -> 15.8 us
  local copies, waits for them, and re-layouts: 51.5 us -> 22.2 us
  Pallas kernels: 0 us -> 28.1 us
  between operations: 18.4 us -> 3.33 us
    all_gather x2 -> x0, waiting for transfers between devices: 139 us -> none  [the longest x1 110 us: carried_in(): pieces = jax.tree.map(lambda part: lax.all_gather(part, axis), value)]
    dot_general x11 -> x1, matrix products: 100 us -> 0.2 us  [body(): running = jnp.dot(log_decay, upper, precision=lax.Precision.HIGHEST)]
    ppermute x1 -> x34, starting transfers between devices: 3.3 us -> 58.3 us  [moved(): return lax.ppermute(value, 'seq', pairs)]
    unnamed x1 -> x0, blocking collectives: 31.9 us -> none
    select_n x16 -> x7, other arithmetic: 32.1 us -> 2.18 us  [the longest x2 1.79 us: carried_in_planes(): jnp.where(c == 0, jnp.concatenate([mine, other], axis=0), jnp.concatenate...]
    pallas_call x0 -> x5, Pallas kernels: none -> 28.1 us  [the longest x2 12.5 us: attend_part(): pl.pallas_call(functools.partial(attend_kernel, sizes), grid_spec=pltpu.P...]
    slice x15 -> x4, local copies, waits for them, and re-layouts: 25.6 us -> 1.9 us  [the longest x1 1.14 us: body(): own = jnp.concatenate([sparse_key[:, cols], sparse_value[:, cols]], axis=1)]
    all_gather x1 -> x0, blocking collectives: 23.1 us -> none  [body(): seg_portion = lax.all_gather(segments, 'seq', axis=0, tiled=True)]
  transfers between devices with their start and end apart: 3 -> 35, of which waited for: 2 -> 8; matrix products, arithmetic and copies ran while one was open for 10% -> 20% of each run, Pallas kernels for 0% -> 16%
where the time goes in v1:
time: 152 us; the launch traced here: 151 us
  starting transfers between devices  61.8 us (41%)
  Pallas kernels  28.1 us (18%)
  local copies, waits for them, and re-layouts  22.2 us (15%)
  other arithmetic  15.8 us (10%)
  waiting for transfers between devices  14.3 us (9%)
  blocking collectives  4.94 us (3%)
  between operations  3.33 us (2%)
    ppermute x34, starting transfers between devices, moved(): return lax.ppermute(value, 'seq', pairs)  58.3 us
    pallas_call x2, Pallas kernels, attend_part(): pl.pallas_call(functools.partial(attend_kernel, sizes), grid_spec=pltpu.P...  12.5 us
    ppermute x34, waiting for transfers between devices, moved(): return lax.ppermute(value, 'seq', pairs)  10.7 us
    pallas_call x2, Pallas kernels, output_part(): pl.pallas_call(output_kernel, grid=(steps,), in_specs=[pl.BlockSpec((per_...  8.18 us
    pallas_call x1, Pallas kernels, local_part(): pl.pallas_call(local_kernel, grid=(steps,), in_specs=[wide, wide, pl.Bloc...  7.38 us
    unnamed x76, local copies, waits for them, and re-layouts  6.61 us
    psum x1, blocking collectives, body(): squares = lax.psum(squares, 'head')  4.94 us
    mul x8, local copies, waits for them, and re-layouts, times(): return factor[:, None, None] * value.astype(F32)  4.09 us
  transfers between devices with their start and end apart: 35, of which 8 were waited for; matrix products, arithmetic and copies ran while one was open for 20% of the time, Pallas kernels for 16%

profile of v1, /device:TPU:0, one launch (start us, length us, event | category | flops | bytes accessed | tf_op | source)
XLA Modules:
  0.0 150.6 jit_solution(10650406705123795647)
XLA Ops:
  1.9 4.9 %collective-permute-start.11 = (bf16[256,512]{1,0:T(8,128)(2,1)S(1)}, bf16[256,512]{1,0:T(8,128)(2,1)S(1)}, u32[]{:S(2)}, u32[]{:S(2)}) collective-permute-start(bf16[256,512]{1,0:T(8,128)(2,1)S(1)} %pad_maximum_fusion.3.refs_1_.refs_2_), channel_id=1, source_target_pairs={{0,8},{2,10},{4,12},{6,14},{8,16},{10,18},{12,20},{14,22},{16,24},... | collective-permute-start | bytes 786440 | tf_op jit(solution)/shard_map/ppermute | solution.py:290
  6.8 3.4 %collective-permute-start.13 = (bf16[256,512]{1,0:T(8,128)(2,1)S(1)}, bf16[256,512]{1,0:T(8,128)(2,1)S(1)}, u32[]{:S(2)}, u32[]{:S(2)}) collective-permute-start(bf16[256,512]{1,0:T(8,128)(2,1)S(1)} %pad_maximum_fusion.3.refs_1_.refs_2_), channel_id=1, source_target_pairs={{0,4},{2,6},{8,12},{10,14},{16,20},{18,22},{24,28},{26,30},{1,5},{... | collective-permute-start | bytes 786440 | tf_op jit(solution)/shard_map/ppermute | solution.py:290
  10.3 3.5 %collective-permute-start = (bf16[256,512]{1,0:T(8,128)(2,1)S(1)}, bf16[256,512]{1,0:T(8,128)(2,1)S(1)}, u32[]{:S(2)}, u32[]{:S(2)}) collective-permute-start(bf16[256,512]{1,0:T(8,128)(2,1)S(1)} %pad_maximum_fusion.2.refs_1_.refs_2_), channel_id=1, source_target_pairs={{0,8},{2,10},{4,12},{6,14},{8,16},{10,18},{12,20},{14,22},{16,24},... | collective-permute-start | bytes 786440 | tf_op jit(solution)/shard_map/ppermute | solution.py:290
  18.2 3.5 %all-to-all-start = ((f32[16,1,128]{2,1,0:T(1,128)}), f32[16,1,128]{2,1,0:T(1,128)S(1)}, u32[]{:S(2)}, u32[]{:S(2)}) async-start(f32[16,1,128]{2,1,0:T(1,128)} %broadcast_in_dim.51), calls=%async_computation | async-start | bytes 16384 | tf_op jit(solution)/shard_map/all_to_all | solution.py:420
  24.4 3.5 %all-to-all-done = f32[16,1,128]{2,1,0:T(1,128)S(1)} async-done(((f32[16,1,128]{2,1,0:T(1,128)}), f32[16,1,128]{2,1,0:T(1,128)S(1)}, u32[]{:S(2)}, u32[]{:S(2)}) %all-to-all-start) | async-done | bytes 8224 | tf_op jit(solution)/shard_map/all_to_all | solution.py:420
  36.3 2.4 %collective-permute-start.1 = (bf16[256,512]{1,0:T(8,128)(2,1)S(1)}, bf16[256,512]{1,0:T(8,128)(2,1)S(1)}, u32[]{:S(2)}, u32[]{:S(2)}) collective-permute-start(bf16[256,512]{1,0:T(8,128)(2,1)S(1)} %collective-permute-done.refs_6_.refs_17_), channel_id=1, source_target_pairs={{0,8},{2,10},{4,12},{6,14},{8,16},{10,18},{12,20},{14,22},{16,24},... | collective-permute-start | bytes 786440 | tf_op jit(solution)/shard_map/ppermute | solution.py:290
  39.6 2.5 %collective-permute-start.12 = (bf16[256,512]{1,0:T(8,128)(2,1)S(1)}, bf16[256,512]{1,0:T(8,128)(2,1)S(1)}, u32[]{:S(2)}, u32[]{:S(2)}) collective-permute-start(bf16[256,512]{1,0:T(8,128)(2,1)S(1)} %collective-permute-done.11.refs_6_.refs_17_), channel_id=1, source_target_pairs={{0,8},{2,10},{4,12},{6,14},{8,16},{10,18},{12,20},{14,22},{16,24},... | collective-permute-start | bytes 786440 | tf_op jit(solution)/shard_map/ppermute | solution.py:290
  58.5 3.2 %collective-permute-done.4.refs_10_.refs_21_ = bf16[256,512]{1,0:T(8,128)(2,1)} collective-permute-done((bf16[256,512]{1,0:T(8,128)(2,1)S(1)}, bf16[256,512]{1,0:T(8,128)(2,1)}, u32[]{:S(2)}, u32[]{:S(2)}) %collective-permute-start.4) | collective-permute-done | bytes 262176 | tf_op jit(solution)/shard_map/ppermute | solution.py:290
  61.7 7.4 %local_scores.1 = (bf16[32,256,256]{2,1,0:T(8,128)(2,1)}, bf16[256,4096]{1,0:T(8,128)(2,1)}) custom-call(bf16[256,4096]{1,0:T(8,128)(2,1)} %q_ref.5, bf16[256,4096]{1,0:T(8,128)(2,1)} %k_ref.1, f32[4,8,256]{2,1,0:T(8,128)} %bitcast.137, f32[4,256,8]{2,1,0:T(8,128)} %bitcast.125, f32[4,256,8]{2,1,0:T(8,128)} %bitcast.126, s32[256,1]{1,0:T(8,128)} %copy.92.segc_ref.refs_4_, ...), custom_call_target="tpu_custom_call" | custom-call | flops 536870912 | bytes 10485760 | tf_op jit(solution)/shard_map/local_scores/pallas_call | solution.py:59
  70.8 6.2 %attend.2 = (bf16[256,2048]{1,0:T(8,128)(2,1)}, bf16[16,128,128]{2,1,0:T(8,128)(2,1)}) custom-call(s32[56]{0:T(128)} %pad_add_fusion.table, bf16[256,4096]{1,0:T(8,128)(2,1)} %refs_0_.3, bf16[256,512]{1,0:T(8,128)(2,1)} %copy-done.4, bf16[256,512]{1,0:T(8,128)(2,1)} %copy-done.4, bf16[256,4096]{1,0:T(8,128)(2,1)} %get-tuple-element.12.refs_3_, ...), custom_call_target="tpu_custom_call" | custom-call | flops 2013265920 | bytes 6291456 | tf_op jit(solution)/shard_map/attend/pallas_call | solution.py:200
  80.8 6.4 %attend.3 = (bf16[256,2048]{1,0:T(8,128)(2,1)}, bf16[16,128,128]{2,1,0:T(8,128)(2,1)}) custom-call(s32[56]{0:T(128)} %pad_add_fusion.table, bf16[256,4096]{1,0:T(8,128)(2,1)} %refs_0_.3, bf16[256,512]{1,0:T(8,128)(2,1)} %copy-done.3, bf16[256,512]{1,0:T(8,128)(2,1)} %copy-done.3, bf16[256,4096]{1,0:T(8,128)(2,1)} %get-tuple-element.12.refs_3_, ...), custom_call_target="tpu_custom_call" | custom-call | flops 2013265920 | bytes 6291456 | tf_op jit(solution)/shard_map/attend/pallas_call | solution.py:200
  89.6 5.3 %collective-permute-start.23 = (bf16[4,128,128]{2,1,0:T(8,128)(2,1)S(1)}, bf16[4,128,128]{2,1,0:T(8,128)(2,1)S(1)}, u32[]{:S(2)}, u32[]{:S(2)}) collective-permute-start(bf16[4,128,128]{2,1,0:T(8,128)(2,1)S(1)} %fusion.13), channel_id=1, source_target_pairs={{0,4},{2,6},{4,0},{6,2},{8,12},{10,14},{12,8},{14,10},{16,20},{18,... | collective-permute-start | bytes 393224 | tf_op jit(solution)/shard_map/ppermute | solution.py:290
  97.0 1.7 %collective-permute-done.23 = bf16[4,128,128]{2,1,0:T(8,128)(2,1)S(1)} collective-permute-done((bf16[4,128,128]{2,1,0:T(8,128)(2,1)S(1)}, bf16[4,128,128]{2,1,0:T(8,128)(2,1)S(1)}, u32[]{:S(2)}, u32[]{:S(2)}) %collective-permute-start.23) | collective-permute-done | bytes 131104 | tf_op jit(solution)/shard_map/ppermute | solution.py:290
  98.8 12.6 %collective-permute-start.24 = (bf16[4,128,128]{2,1,0:T(8,128)(2,1)S(1)}, bf16[4,128,128]{2,1,0:T(8,128)(2,1)S(1)}, u32[]{:S(2)}, u32[]{:S(2)}) collective-permute-start(bf16[4,128,128]{2,1,0:T(8,128)(2,1)S(1)} %fusion.9), channel_id=1, source_target_pairs={{0,8},{2,10},{4,12},{6,14},{8,16},{10,18},{12,20},{14,22},{16,24},... | collective-permute-start | bytes 393224 | tf_op jit(solution)/shard_map/ppermute | solution.py:290
  111.6 2.6 %collective-permute-start.30 = (bf16[4,128,128]{2,1,0:T(8,128)(2,1)S(1)}, bf16[4,128,128]{2,1,0:T(8,128)(2,1)S(1)}, u32[]{:S(2)}, u32[]{:S(2)}) collective-permute-start(bf16[4,128,128]{2,1,0:T(8,128)(2,1)S(1)} %fusion.11), channel_id=1, source_target_pairs={{0,8},{2,10},{4,12},{6,14},{8,16},{10,18},{12,20},{14,22},{16,24},... | collective-permute-start | bytes 393224 | tf_op jit(solution)/shard_map/ppermute | solution.py:290
  114.5 4.4 %collective-permute-start.25 = (bf16[4,128,128]{2,1,0:T(8,128)(2,1)S(1)}, bf16[4,128,128]{2,1,0:T(8,128)(2,1)S(1)}, u32[]{:S(2)}, u32[]{:S(2)}) collective-permute-start(bf16[4,128,128]{2,1,0:T(8,128)(2,1)S(1)} %collective-permute-done.24), channel_id=1, source_target_pairs={{0,8},{2,10},{4,12},{6,14},{8,16},{10,18},{12,20},{14,22},{16,24},... | collective-permute-start | bytes 393224 | tf_op jit(solution)/shard_map/ppermute | solution.py:290
  118.9 1.5 %pad_maximum_fusion = bf16[256,4096]{1,0:T(8,128)(2,1)} fusion(bf16[256,2048]{1,0:T(8,128)(2,1)S(1)} %copy-done.2, bf16[256,2048]{1,0:T(8,128)(2,1)S(1)} %copy-done.1), kind=kLoop, calls=%fused_computation | loop fusion | flops 4194304 | bytes 4194304 | tf_op jit(solution)/shard_map/concatenate | solution.py:468
  120.5 2.0 %collective-permute-start.31 = (bf16[4,128,128]{2,1,0:T(8,128)(2,1)S(1)}, bf16[4,128,128]{2,1,0:T(8,128)(2,1)S(1)}, u32[]{:S(2)}, u32[]{:S(2)}) collective-permute-start(bf16[4,128,128]{2,1,0:T(8,128)(2,1)S(1)} %collective-permute-done.30), channel_id=1, source_target_pairs={{0,8},{2,10},{4,12},{6,14},{8,16},{10,18},{12,20},{14,22},{16,24},... | collective-permute-start | bytes 393224 | tf_op jit(solution)/shard_map/ppermute | solution.py:290
  126.6 1.9 %collective-permute-done.26 = bf16[4,128,128]{2,1,0:T(8,128)(2,1)S(1)} collective-permute-done((bf16[4,128,128]{2,1,0:T(8,128)(2,1)S(1)}, bf16[4,128,128]{2,1,0:T(8,128)(2,1)S(1)}, u32[]{:S(2)}, u32[]{:S(2)}) %collective-permute-start.26) | collective-permute-done | bytes 131104 | tf_op jit(solution)/shard_map/ppermute | solution.py:290
  131.7 4.0 %outputs.2 = (f32[256,2048]{1,0:T(8,128)}, f32[256,128]{1,0:T(8,128)}) custom-call(bf16[32,256,256]{2,1,0:T(8,128)(2,1)} %get-tuple-element.15.w_ref, bf16[256,2048]{1,0:T(8,128)(2,1)} %get-tuple-element.13.v_ref, bf16[256,4096]{1,0:T(8,128)(2,1)} %q_ref.5, f32[4,256,8]{2,1,0:T(8,128)} %bitcast.117, bf16[16,128,128]{2,1,0:T(8,128)(2,1)} %maximum_select_fusion.state_ref), custom_call_target="tpu_custom_call" | custom-call | flops 402653184 | bytes 6815744 | tf_op jit(solution)/shard_map/outputs/pallas_call | solution.py:262
  136.6 4.2 %outputs.3 = (f32[256,2048]{1,0:T(8,128)}, f32[256,128]{1,0:T(8,128)}) custom-call(bf16[32,256,256]{2,1,0:T(8,128)(2,1)} %get-tuple-element.15.w_ref, bf16[256,2048]{1,0:T(8,128)(2,1)} %get-tuple-element.14.v_ref, bf16[256,4096]{1,0:T(8,128)(2,1)} %q_ref.5, f32[4,256,8]{2,1,0:T(8,128)} %bitcast.118, bf16[16,128,128]{2,1,0:T(8,128)(2,1)} %maximum_select_fusion.1.state_ref), custom_call_target="tpu_custom_call" | custom-call | flops 402653184 | bytes 6815744 | tf_op jit(solution)/shard_map/outputs/pallas_call | solution.py:262
  142.0 4.9 %psum.7 = f32[256]{0:T(256)S(1)} all-reduce(f32[256]{0:T(256)S(1)} %add.292), channel_id=1, replica_groups=mesh['seq'=16,'head'=2] {'head'}, use_global_device_ids=true, to_apply=%region_10.11 | all-reduce | flops 256 | bytes 2048 | tf_op jit(solution)/shard_map/psum | solution.py:465
  146.9 2.1 %multiply_convert_fusion.1 = (bf16[256,2048]{1,0:T(8,128)(2,1)S(1)}, bf16[256,2048]{1,0:T(8,128)(2,1)S(1)}) fusion(f32[256,2048]{1,0:T(8,128)S(1)} %copy-done.5, f32[256]{0:T(256)S(1)} %add_rsqrt_fusion, f32[256,2048]{1,0:T(8,128)} %get-tuple-element.21), kind=kLoop, calls=%fused_computation.3 | loop fusion | flops 2097152 | bytes 6292480 | tf_op jit(solution)/shard_map/convert_element_type | solution.py:467
  149.1 1.5 %pad_maximum_fusion.1 = bf16[256,4096]{1,0:T(8,128)(2,1)} fusion(bf16[256,2048]{1,0:T(8,128)(2,1)S(1)} %get-tuple-element.61, bf16[256,2048]{1,0:T(8,128)(2,1)S(1)} %get-tuple-element.60), kind=kLoop, calls=%fused_computation.1 | loop fusion | flops 4194304 | bytes 4194304 | tf_op jit(solution)/shard_map/concatenate | solution.py:467
  (208 shorter events, 51.6 us)
Async XLA Ops:
  1.9 34.4 %collective-permute-start.11 = (bf16[256,512]{1,0:T(8,128)(2,1)S(1)}, bf16[256,512]{1,0:T(8,128)(2,1)S(1)}, u32[]{:S(2)}, u32[]{:S(2)}) collective-permute-start(bf16[256,512]{1,0:T(8,128)(2,1)S(1)} %pad_maximum_fusion.3.refs_1_.refs_2_), channel_id=1, source_target_pairs={{0,8},{2,10},{4,12},{6,14},{8,16},{10,18},{12,20},{14,22},{16,24},... | collective-permute-start | bytes 786440 | tf_op jit(solution)/shard_map/ppermute | solution.py:290
  6.8 32.8 %collective-permute-start.13 = (bf16[256,512]{1,0:T(8,128)(2,1)S(1)}, bf16[256,512]{1,0:T(8,128)(2,1)S(1)}, u32[]{:S(2)}, u32[]{:S(2)}) collective-permute-start(bf16[256,512]{1,0:T(8,128)(2,1)S(1)} %pad_maximum_fusion.3.refs_1_.refs_2_), channel_id=1, source_target_pairs={{0,4},{2,6},{8,12},{10,14},{16,20},{18,22},{24,28},{26,30},{1,5},{... | collective-permute-start | bytes 786440 | tf_op jit(solution)/shard_map/ppermute | solution.py:290
  10.2 31.9 %collective-permute-start.16 = (bf16[256,512]{1,0:T(8,128)(2,1)S(1)}, bf16[256,512]{1,0:T(8,128)(2,1)S(1)}, u32[]{:S(2)}, u32[]{:S(2)}) collective-permute-start(bf16[256,512]{1,0:T(8,128)(2,1)S(1)} %pad_maximum_fusion.3.refs_1_.refs_2_), channel_id=1, source_target_pairs={{0,2},{2,0},{4,6},{6,4},{8,10},{10,8},{12,14},{14,12},{16,18},{18,... | collective-permute-start | bytes 786440 | tf_op jit(solution)/shard_map/ppermute | solution.py:290
  10.3 26.0 %collective-permute-start = (bf16[256,512]{1,0:T(8,128)(2,1)S(1)}, bf16[256,512]{1,0:T(8,128)(2,1)S(1)}, u32[]{:S(2)}, u32[]{:S(2)}) collective-permute-start(bf16[256,512]{1,0:T(8,128)(2,1)S(1)} %pad_maximum_fusion.2.refs_1_.refs_2_), channel_id=1, source_target_pairs={{0,8},{2,10},{4,12},{6,14},{8,16},{10,18},{12,20},{14,22},{16,24},... | collective-permute-start | bytes 786440 | tf_op jit(solution)/shard_map/ppermute | solution.py:290
  13.8 29.0 %collective-permute-start.2 = (bf16[256,512]{1,0:T(8,128)(2,1)S(1)}, bf16[256,512]{1,0:T(8,128)(2,1)S(1)}, u32[]{:S(2)}, u32[]{:S(2)}) collective-permute-start(bf16[256,512]{1,0:T(8,128)(2,1)S(1)} %pad_maximum_fusion.2.refs_1_.refs_2_), channel_id=1, source_target_pairs={{0,4},{2,6},{8,12},{10,14},{16,20},{18,22},{24,28},{26,30},{1,5},{... | collective-permute-start | bytes 786440 | tf_op jit(solution)/shard_map/ppermute | solution.py:290
  18.2 9.8 %all-to-all-start = ((f32[16,1,128]{2,1,0:T(1,128)}), f32[16,1,128]{2,1,0:T(1,128)S(1)}, u32[]{:S(2)}, u32[]{:S(2)}) async-start(f32[16,1,128]{2,1,0:T(1,128)} %broadcast_in_dim.51), calls=%async_computation | async-start | bytes 16384 | tf_op jit(solution)/shard_map/all_to_all | solution.py:420
  36.3 9.0 %collective-permute-start.1 = (bf16[256,512]{1,0:T(8,128)(2,1)S(1)}, bf16[256,512]{1,0:T(8,128)(2,1)S(1)}, u32[]{:S(2)}, u32[]{:S(2)}) collective-permute-start(bf16[256,512]{1,0:T(8,128)(2,1)S(1)} %collective-permute-done.refs_6_.refs_17_), channel_id=1, source_target_pairs={{0,8},{2,10},{4,12},{6,14},{8,16},{10,18},{12,20},{14,22},{16,24},... | collective-permute-start | bytes 786440 | tf_op jit(solution)/shard_map/ppermute | solution.py:290
  39.6 16.8 %collective-permute-start.12 = (bf16[256,512]{1,0:T(8,128)(2,1)S(1)}, bf16[256,512]{1,0:T(8,128)(2,1)S(1)}, u32[]{:S(2)}, u32[]{:S(2)}) collective-permute-start(bf16[256,512]{1,0:T(8,128)(2,1)S(1)} %collective-permute-done.11.refs_6_.refs_17_), channel_id=1, source_target_pairs={{0,8},{2,10},{4,12},{6,14},{8,16},{10,18},{12,20},{14,22},{16,24},... | collective-permute-start | bytes 786440 | tf_op jit(solution)/shard_map/ppermute | solution.py:290
  42.1 14.3 %collective-permute-start.14 = (bf16[256,512]{1,0:T(8,128)(2,1)S(1)}, bf16[256,512]{1,0:T(8,128)(2,1)S(1)}, u32[]{:S(2)}, u32[]{:S(2)}) collective-permute-start(bf16[256,512]{1,0:T(8,128)(2,1)S(1)} %collective-permute-done.11.refs_6_.refs_17_), channel_id=1, source_target_pairs={{0,4},{2,6},{4,0},{6,2},{8,12},{10,14},{12,8},{14,10},{16,20},{18,... | collective-permute-start | bytes 786440 | tf_op jit(solution)/shard_map/ppermute | solution.py:290
  42.8 14.2 %collective-permute-start.3 = (bf16[256,512]{1,0:T(8,128)(2,1)S(1)}, bf16[256,512]{1,0:T(8,128)(2,1)S(1)}, u32[]{:S(2)}, u32[]{:S(2)}) collective-permute-start(bf16[256,512]{1,0:T(8,128)(2,1)S(1)} %collective-permute-done.refs_6_.refs_17_), channel_id=1, source_target_pairs={{0,4},{2,6},{4,0},{6,2},{8,12},{10,14},{12,8},{14,10},{16,20},{18,... | collective-permute-start | bytes 786440 | tf_op jit(solution)/shard_map/ppermute | solution.py:290
  44.2 14.1 %collective-permute-start.6 = (bf16[256,512]{1,0:T(8,128)(2,1)S(1)}, bf16[256,512]{1,0:T(8,128)(2,1)S(1)}, u32[]{:S(2)}, u32[]{:S(2)}) collective-permute-start(bf16[256,512]{1,0:T(8,128)(2,1)S(1)} %collective-permute-done.refs_6_.refs_17_), channel_id=1, source_target_pairs={{0,2},{2,0},{4,6},{6,4},{8,10},{10,8},{12,14},{14,12},{16,18},{18,... | collective-permute-start | bytes 786440 | tf_op jit(solution)/shard_map/ppermute | solution.py:290
  45.4 16.3 %collective-permute-start.4 = (bf16[256,512]{1,0:T(8,128)(2,1)S(1)}, bf16[256,512]{1,0:T(8,128)(2,1)}, u32[]{:S(2)}, u32[]{:S(2)}) collective-permute-start(bf16[256,512]{1,0:T(8,128)(2,1)S(1)} %collective-permute-done.1.refs_7_.refs_18_), channel_id=1, source_target_pairs={{4,0},{6,2},{12,8},{14,10},{20,16},{22,18},{28,24},{30,26},{5,1},{... | collective-permute-start | bytes 786440 | tf_op jit(solution)/shard_map/ppermute | solution.py:290
  56.4 12.8 %collective-permute-start.8 = (bf16[256,512]{1,0:T(8,128)(2,1)S(1)}, bf16[256,512]{1,0:T(8,128)(2,1)}, u32[]{:S(2)}, u32[]{:S(2)}) collective-permute-start(bf16[256,512]{1,0:T(8,128)(2,1)S(1)} %collective-permute-done.2.refs_8_.refs_19_), channel_id=1, source_target_pairs={{0,2},{2,0},{4,6},{6,4},{8,10},{10,8},{12,14},{14,12},{16,18},{18,... | collective-permute-start | bytes 786440 | tf_op jit(solution)/shard_map/ppermute | solution.py:290
  56.5 13.4 %collective-permute-start.7 = (bf16[256,512]{1,0:T(8,128)(2,1)S(1)}, bf16[256,512]{1,0:T(8,128)(2,1)}, u32[]{:S(2)}, u32[]{:S(2)}) collective-permute-start(bf16[256,512]{1,0:T(8,128)(2,1)S(1)} %collective-permute-done.1.refs_7_.refs_18_), channel_id=1, source_target_pairs={{0,2},{2,0},{4,6},{6,4},{8,10},{10,8},{12,14},{14,12},{16,18},{18,... | collective-permute-start | bytes 786440 | tf_op jit(solution)/shard_map/ppermute | solution.py:290
  57.0 12.8 %collective-permute-start.15 = (bf16[256,512]{1,0:T(8,128)(2,1)S(1)}, bf16[256,512]{1,0:T(8,128)(2,1)}, u32[]{:S(2)}, u32[]{:S(2)}) collective-permute-start(bf16[256,512]{1,0:T(8,128)(2,1)S(1)} %collective-permute-done.12.refs_7_.refs_18_), channel_id=1, source_target_pairs={{4,0},{6,2},{12,8},{14,10},{20,16},{22,18},{28,24},{30,26},{5,1},{... | collective-permute-start | bytes 786440 | tf_op jit(solution)/shard_map/ppermute | solution.py:290
  58.3 12.0 %collective-permute-start.9 = (bf16[256,512]{1,0:T(8,128)(2,1)S(1)}, bf16[256,512]{1,0:T(8,128)(2,1)}, u32[]{:S(2)}, u32[]{:S(2)}) collective-permute-start(bf16[256,512]{1,0:T(8,128)(2,1)S(1)} %collective-permute-done.3.refs_9_.refs_20_), channel_id=1, source_target_pairs={{0,2},{2,0},{4,6},{6,4},{8,10},{10,8},{12,14},{14,12},{16,18},{18,... | collective-permute-start | bytes 786440 | tf_op jit(solution)/shard_map/ppermute | solution.py:290
  69.8 9.4 %collective-permute-start.19 = (bf16[256,512]{1,0:T(8,128)(2,1)S(1)}, bf16[256,512]{1,0:T(8,128)(2,1)S(1)}, u32[]{:S(2)}, u32[]{:S(2)}) collective-permute-start(bf16[256,512]{1,0:T(8,128)(2,1)S(1)} %collective-permute-done.13.refs_8_.refs_19_), channel_id=1, source_target_pairs={{0,2},{2,0},{4,6},{6,4},{8,10},{10,8},{12,14},{14,12},{16,18},{18,... | collective-permute-start | bytes 786440 | tf_op jit(solution)/shard_map/ppermute | solution.py:290
  69.9 9.3 %collective-permute-start.18 = (bf16[256,512]{1,0:T(8,128)(2,1)S(1)}, bf16[256,512]{1,0:T(8,128)(2,1)S(1)}, u32[]{:S(2)}, u32[]{:S(2)}) collective-permute-start(bf16[256,512]{1,0:T(8,128)(2,1)S(1)} %collective-permute-done.12.refs_7_.refs_18_), channel_id=1, source_target_pairs={{0,2},{2,0},{4,6},{6,4},{8,10},{10,8},{12,14},{14,12},{16,18},{18,... | collective-permute-start | bytes 786440 | tf_op jit(solution)/shard_map/ppermute | solution.py:290
  70.3 8.9 %collective-permute-start.20 = (bf16[256,512]{1,0:T(8,128)(2,1)S(1)}, bf16[256,512]{1,0:T(8,128)(2,1)S(1)}, u32[]{:S(2)}, u32[]{:S(2)}) collective-permute-start(bf16[256,512]{1,0:T(8,128)(2,1)S(1)} %collective-permute-done.14.refs_9_.refs_20_), channel_id=1, source_target_pairs={{0,2},{2,0},{4,6},{6,4},{8,10},{10,8},{12,14},{14,12},{16,18},{18,... | collective-permute-start | bytes 786440 | tf_op jit(solution)/shard_map/ppermute | solution.py:290
  78.0 11.5 %collective-permute-start.22 = (bf16[8,128,128]{2,1,0:T(8,128)(2,1)S(1)}, bf16[8,128,128]{2,1,0:T(8,128)(2,1)S(1)}, u32[]{:S(2)}, u32[]{:S(2)}) collective-permute-start(bf16[8,128,128]{2,1,0:T(8,128)(2,1)S(1)} %dynamic-slice_bitcast_fusion.1), channel_id=1, source_target_pairs={{0,2},{2,0},{4,6},{6,4},{8,10},{10,8},{12,14},{14,12},{16,18},{18,... | collective-permute-start | bytes 786440 | tf_op jit(solution)/shard_map/ppermute | solution.py:290
  89.6 9.1 %collective-permute-start.23 = (bf16[4,128,128]{2,1,0:T(8,128)(2,1)S(1)}, bf16[4,128,128]{2,1,0:T(8,128)(2,1)S(1)}, u32[]{:S(2)}, u32[]{:S(2)}) collective-permute-start(bf16[4,128,128]{2,1,0:T(8,128)(2,1)S(1)} %fusion.13), channel_id=1, source_target_pairs={{0,4},{2,6},{4,0},{6,2},{8,12},{10,14},{12,8},{14,10},{16,20},{18,... | collective-permute-start | bytes 393224 | tf_op jit(solution)/shard_map/ppermute | solution.py:290
  96.0 15.4 %collective-permute-start.29 = (bf16[4,128,128]{2,1,0:T(8,128)(2,1)S(1)}, bf16[4,128,128]{2,1,0:T(8,128)(2,1)S(1)}, u32[]{:S(2)}, u32[]{:S(2)}) collective-permute-start(bf16[4,128,128]{2,1,0:T(8,128)(2,1)S(1)} %fusion.14), channel_id=1, source_target_pairs={{0,4},{2,6},{4,0},{6,2},{8,12},{10,14},{12,8},{14,10},{16,20},{18,... | collective-permute-start | bytes 393224 | tf_op jit(solution)/shard_map/ppermute | solution.py:290
  98.8 15.7 %collective-permute-start.24 = (bf16[4,128,128]{2,1,0:T(8,128)(2,1)S(1)}, bf16[4,128,128]{2,1,0:T(8,128)(2,1)S(1)}, u32[]{:S(2)}, u32[]{:S(2)}) collective-permute-start(bf16[4,128,128]{2,1,0:T(8,128)(2,1)S(1)} %fusion.9), channel_id=1, source_target_pairs={{0,8},{2,10},{4,12},{6,14},{8,16},{10,18},{12,20},{14,22},{16,24},... | collective-permute-start | bytes 393224 | tf_op jit(solution)/shard_map/ppermute | solution.py:290
  111.6 8.9 %collective-permute-start.30 = (bf16[4,128,128]{2,1,0:T(8,128)(2,1)S(1)}, bf16[4,128,128]{2,1,0:T(8,128)(2,1)S(1)}, u32[]{:S(2)}, u32[]{:S(2)}) collective-permute-start(bf16[4,128,128]{2,1,0:T(8,128)(2,1)S(1)} %fusion.11), channel_id=1, source_target_pairs={{0,8},{2,10},{4,12},{6,14},{8,16},{10,18},{12,20},{14,22},{16,24},... | collective-permute-start | bytes 393224 | tf_op jit(solution)/shard_map/ppermute | solution.py:290
  (41 other events, 681.4 us)

commit v2 on v0

v2 whole, which is shorter than its diff:
```python
import functools

import jax
import jax.numpy as jnp
from jax import lax
from jax.experimental import pallas as pl
from jax.experimental.pallas import tpu as pltpu
from jax.sharding import PartitionSpec as P

ASKER_CHANNELS = 64
HD = 128
BLK = 128

NEG = -1e30
norm_eps = 1e-06
LOG2E = 1.4426950408889634
F32 = jnp.float32
BF16 = jnp.bfloat16
CLASSES = (1, 2, 3, 5, 7, 9)


def room(mib):
    return pltpu.CompilerParams(vmem_limit_bytes=mib * 1024 * 1024)


def far(value):
    return pltpu.with_memory_space_constraint(value, pltpu.HBM)


def nt(a, b):
    return lax.dot_general(a, b, (((1,), (1,)), ((), ())), preferred_element_type=F32)


def tn(a, b):
    return lax.dot_general(a, b, (((0,), (0,)), ((), ())), preferred_element_type=F32)


def nn(a, b):
    return lax.dot_general(a, b, (((1,), (0,)), ((), ())), preferred_element_type=F32)


def info_kernel(decay_ref, seg_ref, info_ref):
    rows, lanes = info_ref.shape
    heads, tokens = decay_ref.shape
    ones = jnp.ones((rows, tokens), F32)
    totals = lax.dot_general(
        ones,
        decay_ref[...],
        (((1,), (1,)), ((), ())),
        precision=lax.Precision.HIGHEST,
        preferred_element_type=F32,
    )
    info_ref[...] = jnp.zeros((rows, lanes), F32)
    info_ref[:, :heads] = totals
    seg = seg_ref[...]
    for doc in range(1, 4):
        count = jnp.sum((seg < doc).astype(F32), axis=1, keepdims=True)
        info_ref[:, heads + doc - 1 : heads + doc] = jnp.broadcast_to(count, (rows, 1))
    ends = seg.astype(F32)
    info_ref[:, heads + 3 : heads + 4] = jnp.broadcast_to(ends[:, :1], (rows, 1))
    info_ref[:, heads + 4 : heads + 5] = jnp.broadcast_to(ends[:, tokens - 1 :], (rows, 1))


def own_info(log_decay, seg_row, shards):
    return pl.pallas_call(
        info_kernel,
        out_shape=jax.ShapeDtypeStruct((shards, 128), F32),
        compiler_params=room(2),
        name="own_info",
    )(log_decay, seg_row)


def passing_kernel(heads, tokens, known_ref, passing_ref):
    known = known_ref[...]
    rows = known.shape[0]
    firsts, lasts = known[:, heads + 3 : heads + 4], known[:, heads + 4 : heads + 5]
    begins = jnp.zeros_like(firsts)
    for doc in range(1, 4):
        start = jnp.sum(known[:, heads + doc - 1 : heads + doc], axis=0, keepdims=True)
        begins = jnp.where(firsts == doc, start, begins)
    position = lax.broadcasted_iota(jnp.int32, (rows, 1), 0) * tokens
    begun = begins < position.astype(F32)
    through = begun & (firsts == lasts)
    lane = lax.broadcasted_iota(jnp.int32, known.shape, 1)
    decay = jnp.exp(jnp.where(lane < heads, known, 0.0))
    passing_ref[...] = jnp.where(lane == heads, begun.astype(F32), jnp.where(through, decay, 0.0))


def all_passing(known, heads, tokens):
    return pl.pallas_call(
        functools.partial(passing_kernel, heads, tokens),
        out_shape=jax.ShapeDtypeStruct(known.shape, F32),
        compiler_params=room(2),
        name="passing",
    )(known)


def local_kernel(q_ref, k_ref, decay_ref, segc_ref, segr_ref, w_ref, kf_ref, qf_ref, bias, upper):
    tokens = q_ref.shape[0]

    @pl.when(pl.program_id(0) == 0)
    def _():
        t = lax.broadcasted_iota(jnp.int32, (tokens, tokens), 0)
        s = lax.broadcasted_iota(jnp.int32, (tokens, tokens), 1)
        seen = (s <= t) & (segc_ref[...] == segr_ref[...])
        bias[...] = jnp.where(seen, 0.0, NEG)
        upper[...] = (t <= s).astype(F32)

    row = lax.dot_general(
        decay_ref[...],
        upper[...],
        (((1,), (0,)), ((), ())),
        precision=lax.Precision.HIGHEST,
        preferred_element_type=F32,
    )
    seg = segc_ref[...]
    col = jnp.transpose(row)
    fade = jnp.where(seg == seg[tokens - 1 :, :], jnp.exp(col[tokens - 1 :, :] - col), 0.0)
    reach = jnp.where(seg == seg[:1, :], jnp.exp(col), 0.0)
    for i in range(w_ref.shape[0]):
        cols = slice(i * HD, (i + 1) * HD)
        k = k_ref[:, cols]
        q = q_ref[:, cols]
        spread = col[:, i : i + 1] - row[i : i + 1, :]
        w_ref[i] = (nt(q, k) * jnp.exp(spread + bias[...])).astype(BF16)
        kf_ref[i] = jnp.transpose((k.astype(F32) * fade[:, i : i + 1]).astype(BF16))
        qf_ref[:, cols] = (q.astype(F32) * reach[:, i : i + 1]).astype(BF16)


def local_part(light_q, light_k, log_decay, seg_col, seg_row, per_step):
    tokens, width = light_q.shape
    heads = width // HD
    steps = heads // per_step
    wide = pl.BlockSpec((tokens, per_step * HD), lambda g: (0, g))
    return pl.pallas_call(
        local_kernel,
        grid=(steps,),
        in_specs=[
            wide,
            wide,
            pl.BlockSpec((per_step, tokens), lambda g: (g, 0)),
            pl.BlockSpec((tokens, 1), lambda g: (0, 0)),
            pl.BlockSpec((1, tokens), lambda g: (0, 0)),
        ],
        out_specs=[
            pl.BlockSpec((per_step, tokens, tokens), lambda g: (g, 0, 0)),
            pl.BlockSpec((per_step, HD, tokens), lambda g: (g, 0, 0)),
            wide,
        ],
        out_shape=[
            jax.ShapeDtypeStruct((heads, tokens, tokens), BF16),
            jax.ShapeDtypeStruct((heads, HD, tokens), BF16),
            jax.ShapeDtypeStruct((tokens, width), BF16),
        ],
        scratch_shapes=[pltpu.VMEM((tokens, tokens), F32), pltpu.VMEM((tokens, tokens), F32)],
        compiler_params=room(14),
        cost_estimate=pl.CostEstimate(
            flops=2 * heads * tokens * tokens * HD,
            bytes_accessed=4 * 2 * tokens * width + 2 * heads * tokens * tokens,
            transcendentals=heads * tokens * tokens,
        ),
        name="local_scores",
    )(far(light_q), far(light_k), log_decay, seg_col, seg_row)


def table_kernel(sizes, planes, heads, listing, known, place_ref, segc_ref, segr_ref, *refs):
    own_bias, row_bias, key_bias, table, named, counts = refs
    tokens = segc_ref.shape[0]
    blocks = tokens // BLK
    shards = known.shape[0]
    per_row = listing.shape[0] // blocks
    total = sum(sizes)
    me = place_ref[0]
    first_doc = known[me, heads + 3].astype(jnp.int32)
    begin = known[0, heads] * 0.0
    for doc in range(1, 4):
        start = known[0, heads + doc - 1]
        for j in range(1, shards):
            start = start + known[j, heads + doc - 1]
        begin = jnp.where(first_doc == doc, start, begin)
    begin = begin.astype(jnp.int32)
    for delta in range(shards):
        named[delta] = 0
    for b in range(blocks):
        counts[b] = 0
    for e in range(listing.shape[0]):
        entry = listing[e]
        delta = jnp.where(entry >= 0, me - lax.div(jnp.maximum(entry, 0), blocks), 0)
        named[delta] = 1 + (e // per_row) * blocks + lax.rem(jnp.maximum(entry, 0), blocks)
    named[0] = 0
    key_bias[...] = jnp.full(key_bias.shape, NEG, F32)
    lane = lax.broadcasted_iota(jnp.int32, (BLK, BLK), 1)
    sub = lax.broadcasted_iota(jnp.int32, (BLK, BLK), 0)
    for b in range(blocks):
        here = slice(b * BLK, (b + 1) * BLK)
        ok = (lane <= sub) & (segc_ref[here, :] == segr_ref[:, here])
        own_bias[b] = jnp.where(ok, 0.0, NEG)
        ok = jnp.broadcast_to(segc_ref[here, :], (BLK, BLK)) == first_doc
        row_bias[b] = jnp.where(ok, 0.0, NEG)

    def fill(slot, owner, usable):
        usable = usable & (owner >= 0) & (owner < me)
        code = named[jnp.where(usable, me - owner, 0)] - 1
        half = lax.rem(jnp.maximum(code, 0), blocks)
        least = begin - (owner * blocks + half) * BLK
        seen = usable & (code >= 0) & (least < BLK)
        b = lax.div(jnp.maximum(code, 0), blocks)
        to = jnp.where(seen, counts[b] + 1, 0)
        table[3 * slot] = b * (1 + per_row) + to
        table[3 * slot + 1] = half
        table[3 * slot + 2] = seen.astype(jnp.int32)

        @pl.when(seen)
        def _():
            counts[b] = to
            at = b * (1 + per_row) + to
            key_bias[pl.ds(at, 1)] = jnp.where(lane[:8] >= least, 0.0, NEG)[None]

    if planes:
        for slot, (owner, usable) in enumerate(window_owners(me)):
            fill(slot, owner, usable)
    else:

        def fill_step(j, carry):
            fill(j, j, j >= 0)
            return carry

        lax.fori_loop(0, shards, fill_step, 0)
    for b in range(blocks):
        table[3 * total + b] = counts[b]


def seen_table(place, listing, known, seg_col, seg_row, sizes, heads, planes):
    blocks = seg_col.shape[0] // BLK
    tiles = listing.shape[0] + blocks
    smem = pl.BlockSpec(memory_space=pltpu.SMEM)
    vmem = pl.BlockSpec(memory_space=pltpu.VMEM)
    return pl.pallas_call(
        functools.partial(table_kernel, sizes, planes, heads),
        in_specs=[smem, smem, smem, vmem, vmem],
        out_specs=[vmem, vmem, vmem, smem],
        out_shape=[
            jax.ShapeDtypeStruct((blocks, BLK, BLK), F32),
            jax.ShapeDtypeStruct((blocks, BLK, BLK), F32),
            jax.ShapeDtypeStruct((tiles, 8, BLK), F32),
            jax.ShapeDtypeStruct((3 * sum(sizes) + blocks,), jnp.int32),
        ],
        scratch_shapes=[
            pltpu.SMEM((known.shape[0],), jnp.int32),
            pltpu.SMEM((blocks,), jnp.int32),
        ],
        compiler_params=room(6),
        name="seen_table",
    )(listing, known, place, seg_col, seg_row)


def attend_kernel(sizes, kv_step, kv_head, table, *refs):
    pieces = len(sizes)
    q_ref, own_k, own_v, kf_ref, own_bias, row_bias, key_bias = refs[:7]
    piece = refs[7 : 7 + pieces]
    out_ref, state_ref, keys, values, sems = refs[-5:]
    tokens, width = q_ref.shape
    blocks = tokens // BLK
    group = width // HD
    per_row = keys.shape[0] // (blocks * BLK) - 1
    factor = HD ** (-0.5) * LOG2E
    total = sum(sizes)

    def each_piece(do):
        at = 0
        for i, size in enumerate(sizes):
            if size == 1:
                do(i, at, 0)
            else:

                def step(j, carry, i=i, at=at):
                    do(i, at + j, j)
                    return carry

                lax.fori_loop(0, size, step, 0)
            at += size

    def copies(i, slot, j):
        span = pl.ds(pl.multiple_of(j * tokens + table[3 * slot + 1] * BLK, BLK), BLK)
        to = pl.ds(pl.multiple_of(table[3 * slot] * BLK, BLK), BLK)
        for part, buffer in enumerate((keys, values)):
            cols = pl.ds(pl.multiple_of((kv_head[1] + part * kv_step) * HD, HD), HD)
            yield pltpu.make_async_copy(piece[i].at[span, cols], buffer.at[to, :], sems.at[part, slot])

    def bring(i, slot, j):
        @pl.when(table[3 * slot + 2] > 0)
        def _():
            for copy in copies(i, slot, j):
                copy.start()

    def arrive(i, slot, j):
        @pl.when(table[3 * slot + 2] > 0)
        def _():
            for copy in copies(i, slot, j):
                copy.wait()

    each_piece(bring)
    for b in range(blocks):
        base = b * (1 + per_row) * BLK
        keys[base : base + BLK, :] = own_k[b * BLK : (b + 1) * BLK, :]
        values[base : base + BLK, :] = own_v[b * BLK : (b + 1) * BLK, :]
    each_piece(arrive)

    def heads_out(b, tiles, h, count):
        base = b * (1 + per_row)
        here = pl.ds(pl.multiple_of(b * BLK, BLK), BLK)
        span = pl.ds(pl.multiple_of(base * BLK, BLK), tiles * BLK)
        cols = [pl.ds(pl.multiple_of((h + j) * HD, HD), HD) for j in range(count)]
        query = jnp.concatenate([q_ref[here, c] for c in cols], axis=0)
        score = nt(query, keys[span, :]).reshape(count, BLK, tiles * BLK)
        bias = [own_bias[b]] + [row_bias[b] + key_bias[base + t][:1, :] for t in range(1, tiles)]
        score = score + jnp.concatenate(bias, axis=1)[None]
        lifted = jnp.exp2((score - jnp.max(score, axis=2, keepdims=True)) * factor)
        weight = lifted * (1.0 / jnp.sum(lifted, axis=2, keepdims=True))
        weight = weight.astype(BF16).reshape(count * BLK, tiles * BLK)
        result = nn(weight, values[span, :]).astype(BF16)
        for j, c in enumerate(cols):
            out_ref[here, c] = result[j * BLK : (j + 1) * BLK, :]

    classes = sorted({min(t, 1 + per_row) for t in CLASSES} | {1 + per_row})

    def block_out(b, carry):
        need = table[3 * total + b] + 1
        low = 0
        for tiles in classes:
            together = min(group, 8 if tiles <= 2 else 4 if tiles <= 5 else 2)

            @pl.when((need > low) & (need <= tiles))
            def _(low=low, tiles=tiles, together=together):
                for t in range(max(low + 1, 1), tiles):

                    @pl.when(t >= need)
                    def _(t=t):
                        start = pl.multiple_of((b * (1 + per_row) + t) * BLK, BLK)
                        keys[pl.ds(start, BLK), :] = jnp.zeros((BLK, HD), BF16)
                        values[pl.ds(start, BLK), :] = jnp.zeros((BLK, HD), BF16)

                def step(i, carry):
                    heads_out(b, tiles, i * together, together)
                    return carry

                lax.fori_loop(0, group // together, step, 0)

            low = tiles
        return carry

    lax.fori_loop(0, blocks, block_out, 0)
    for h in range(group):
        state_ref[h] = nn(kf_ref[h], out_ref[:, h * HD : (h + 1) * HD])


def attend_part(kv_head, table, biases, query, own, faded, pieces, sizes, kv_step, before):
    tokens = query.shape[0]
    group = faded.shape[0] * HD // own.shape[1] * 2
    width = group * HD
    wide = pl.BlockSpec((tokens, width), lambda g, *s: (0, s[0][0]))
    in_specs = [
        wide,
        pl.BlockSpec((tokens, HD), lambda g, *s: (0, s[0][1])),
        pl.BlockSpec((tokens, HD), lambda g, *s: (0, s[0][1] + kv_step)),
        pl.BlockSpec((group, HD, tokens), lambda g, *s: (s[0][0], 0, 0)),
    ]
    in_specs += [pl.BlockSpec(bias.shape, lambda g, *s: (0, 0, 0)) for bias in biases]
    in_specs += [pl.BlockSpec(memory_space=pl.ANY)] * len(pieces)
    operands = [far(query), own, own, faded, *biases, *pieces]
    aliases = {}
    if before is not None:
        aliases = {2 + len(operands): 0}
        in_specs.append(pl.BlockSpec(memory_space=pl.ANY))
        operands.append(before)
    rows = biases[2].shape[0] * BLK
    return pl.pallas_call(
        functools.partial(attend_kernel, sizes, kv_step),
        grid_spec=pltpu.PrefetchScalarGridSpec(
            num_scalar_prefetch=2,
            grid=(1,),
            in_specs=in_specs,
            out_specs=[wide, pl.BlockSpec((group, HD, HD), lambda g, *s: (0, 0, 0))],
            scratch_shapes=[
                pltpu.VMEM((rows, HD), BF16),
                pltpu.VMEM((rows, HD), BF16),
                pltpu.SemaphoreType.DMA((2, sum(sizes))),
            ],
        ),
        out_shape=[
            jax.ShapeDtypeStruct(query.shape, BF16),
            jax.ShapeDtypeStruct((group, HD, HD), F32),
        ],
        input_output_aliases=aliases,
        compiler_params=room(20),
        cost_estimate=pl.CostEstimate(
            flops=group * 10 * 6 * BLK * BLK * HD,
            bytes_accessed=3 * 2 * tokens * width + 12 * 4 * tokens * HD,
            transcendentals=group * 10 * BLK * BLK,
        ),
        name="attend",
    )(kv_head, table, *operands)


def inside_kernel(w_ref, v_ref, out_ref):
    for i in range(w_ref.shape[0]):
        cols = slice(i * HD, (i + 1) * HD)
        out_ref[:, cols] = nn(w_ref[i], v_ref[:, cols])


def inside_part(weights, valued, group):
    tokens, width = valued.shape
    steps = width // HD // group
    return pl.pallas_call(
        inside_kernel,
        grid=(steps,),
        in_specs=[
            pl.BlockSpec((group, tokens, tokens), lambda g: (g, 0, 0)),
            pl.BlockSpec((tokens, group * HD), lambda g: (0, g)),
        ],
        out_specs=pl.BlockSpec((tokens, group * HD), lambda g: (0, g)),
        out_shape=jax.ShapeDtypeStruct((tokens, width), F32),
        compiler_params=room(12),
        cost_estimate=pl.CostEstimate(
            flops=steps * group * 2 * tokens * tokens * HD,
            bytes_accessed=steps * group * (2 * tokens * tokens + 6 * tokens * HD),
            transcendentals=0,
        ),
        name="inside",
    )(weights, valued)


def output_kernel(planes, chunks, place_ref, q_ref, inside_ref, *refs):
    keeps, gots = refs[:chunks], refs[chunks : 2 * chunks]
    out_ref, squares_ref, total_ref = refs[-3:]
    step_at = pl.program_id(0)
    group = gots[0].shape[0]
    steps = pl.num_programs(0) // chunks

    @pl.when(step_at == 0)
    def _():
        total_ref[...] = jnp.zeros_like(total_ref)

    def part(state_of):
        total = total_ref[...]
        for i in range(group):
            cols = slice(i * HD, (i + 1) * HD)
            result = inside_ref[:, cols] + nn(q_ref[:, cols], state_of(i))
            out_ref[:, cols] = result
            total += result * result
        total_ref[...] = total

    for chunk in range(chunks):

        @pl.when((step_at >= chunk * steps) & (step_at < (chunk + 1) * steps))
        def _(chunk=chunk):
            keep_ref, got_ref = keeps[chunk], gots[chunk]
            if planes:
                mine = step_at - chunk * steps == (place_ref[0] & 1)
                part(lambda i: jnp.where(mine, keep_ref[i], got_ref[i]))
            else:
                part(lambda i: keep_ref[i])

    @pl.when(step_at == pl.num_programs(0) - 1)
    def _():
        squares_ref[...] = jnp.sum(jnp.transpose(total_ref[...]), axis=0, keepdims=True)


def output_part(place, inside, faded_q, states, group, planes):
    tokens, width = faded_q.shape
    chunks = len(states)
    steps = width // HD // group
    wide = pl.BlockSpec((tokens, group * HD), lambda g, *s: (0, g))
    keep = pl.BlockSpec((group, HD, HD), lambda g, *s: (0 if planes else g, 0, 0))
    got = pl.BlockSpec((group, HD, HD), lambda g, *s: (0, 0, 0))
    return pl.pallas_call(
        functools.partial(output_kernel, planes, chunks),
        grid_spec=pltpu.PrefetchScalarGridSpec(
            num_scalar_prefetch=1,
            grid=(steps,),
            in_specs=[wide, wide] + [keep] * chunks + [got] * chunks,
            out_specs=[wide, pl.BlockSpec((1, tokens), lambda g, *s: (0, 0))],
            scratch_shapes=[pltpu.VMEM((tokens, HD), F32)],
        ),
        out_shape=[
            jax.ShapeDtypeStruct((tokens, width), F32),
            jax.ShapeDtypeStruct((1, tokens), F32),
        ],
        compiler_params=room(16),
        cost_estimate=pl.CostEstimate(
            flops=2 * tokens * width * HD,
            bytes_accessed=10 * tokens * width + 2 * width * HD,
            transcendentals=0,
        ),
        name="outputs",
    )(place, faded_q, inside, *[k for k, _ in states], *[g for _, g in states])


def scale_kernel(features, squares_ref, value_ref, out_ref):
    tokens = value_ref.shape[0]
    row = lax.rsqrt(squares_ref[...] / features + norm_eps)
    scale = jnp.transpose(jnp.broadcast_to(row, (HD, tokens)))
    for i in range(value_ref.shape[1] // HD):
        cols = slice(i * HD, (i + 1) * HD)
        out_ref[:, cols] = (value_ref[:, cols] * scale).astype(BF16)


def scale_part(squares, value, per_step):
    tokens, width = value.shape
    wide = pl.BlockSpec((tokens, per_step * HD), lambda g: (0, g))
    return pl.pallas_call(
        functools.partial(scale_kernel, ASKER_CHANNELS * HD),
        grid=(width // HD // per_step,),
        in_specs=[pl.BlockSpec((1, tokens), lambda g: (0, 0)), wide],
        out_specs=wide,
        out_shape=jax.ShapeDtypeStruct((tokens, width), BF16),
        compiler_params=room(8),
        name="scaled",
    )(squares, value)


def moved(value, pairs):
    return lax.ppermute(value, "seq", pairs)


def up(shards):
    return [(i, (i + 4) % shards) for i in range(shards)]


def cross(shards):
    return [(i, i ^ 2) for i in range(shards)]


def core(shards):
    return [(i, i ^ 1) for i in range(shards)]


def after(values, *first):
    return lax.optimization_barrier((values, first))[0]


def window_owners(me):
    always = me >= 0
    right, left = (me & 2) > 0, (me & 2) == 0

    def seen_from(at):
        side = at ^ 2
        return [
            (at - 4, always),
            (at - 8, always),
            (side, right),
            (side - 4, always),
            (side - 8, left),
        ]

    return seen_from(me) + [(me ^ 1, always)] + seen_from(me ^ 1)


def mixing_kernel(body, passing, place_ref, *refs):
    me = place_ref[0]
    body(passing, me, me & 1, (me >> 1) & 1, *refs)


def mixing(name, body, passing, place, values, outs):
    smem = pl.BlockSpec(memory_space=pltpu.SMEM)
    vmem = pl.BlockSpec(memory_space=pltpu.VMEM)
    return pl.pallas_call(
        functools.partial(mixing_kernel, body),
        in_specs=[smem, smem] + [vmem] * len(values),
        out_specs=[vmem] * len(outs),
        out_shape=[jax.ShapeDtypeStruct((n, HD, HD), dtype) for n, dtype in outs],
        cost_estimate=pl.CostEstimate(
            flops=4 * sum(n for n, _ in outs) * HD * HD,
            bytes_accessed=8 * sum(n for n, _ in outs) * HD * HD,
            transcendentals=0,
        ),
        compiler_params=room(4),
        name=name,
    )(passing, place, *values)


def carried_in_planes(keep, send, passing, place, shards, head0, heads):
    half = keep.shape[0]
    quarter = half // 2
    def chip_body(passing, me, c, x, keep_ref, far_ref, near_ref, send_ref):
        base = head0 + c * half
        for part, to in ((x, near_ref), (1 - x, send_ref)):
            for i in range(quarter):
                h = part * quarter + i
                fade = passing[me | 1, base + h]
                a, b = jnp.where(c == 0, fade, 1.0), jnp.where(c == 0, 1.0, fade)
                to[i] = (keep_ref[h] * a + far_ref[h] * b).astype(to.dtype)

    def plane_body(passing, me, c, x, near_ref, far_ref, out_ref):
        base = head0 + c * half + x * quarter
        for i in range(quarter):
            fade = passing[me | 3, base + i] * passing[(me | 3) - 1, base + i]
            a, b = jnp.where(x == 0, fade, 1.0), jnp.where(x == 0, 1.0, fade)
            out_ref[i] = (near_ref[i] * a + far_ref[i].astype(F32) * b).astype(BF16)

    def enter_body(passing, me, c, x, near_ref, far_ref, one_ref, two_ref, keep_ref, send_ref):
        base = head0 + c * half + x * quarter
        plane = me & ~3
        low = jnp.maximum(plane - 4, 0)
        for i in range(quarter):
            h = base + i
            fade = passing[low, h] * passing[low + 1, h] * passing[low + 2, h] * passing[low + 3, h]
            e0 = jnp.where(me >= 4, one_ref[i].astype(F32), 0.0)
            e0 = jnp.where(me >= 8, e0 + two_ref[i].astype(F32) * fade, e0)
            chip = jnp.where(x == 0, near_ref[i], far_ref[i].astype(F32))
            e1 = e0 * (passing[plane, h] * passing[plane + 1, h]) + chip
            keep_ref[i] = jnp.where(x == 0, e0, e1)
            send_ref[i] = jnp.where(x == 0, e1, e0).astype(BF16)

    def core_body(passing, me, c, x, keep_ref, far_ref, near_ref, got_ref, mine_ref, send_ref):
        base = head0 + c * half
        mine_on, other_on = passing[me, heads], passing[me ^ 1, heads]
        for part, source in ((x, near_ref), (1 - x, got_ref)):
            for i in range(quarter):
                h = part * quarter + i
                e0 = source[i].astype(F32)
                first = jnp.where(c == 0, keep_ref[h], far_ref[h])
                e1 = e0 * passing[me & ~1, base + h] + first
                mine_ref[h] = (jnp.where(c == 0, e0, e1) * mine_on).astype(BF16)
                send_ref[h] = (jnp.where(c == 0, e1, e0) * other_on).astype(BF16)

    sent = moved(send, core(shards))
    near_q, send_q = mixing(
        "mix_chip", chip_body, passing, place, [keep, sent], [(quarter, F32), (quarter, BF16)]
    )
    far_q = moved(send_q, cross(shards))
    yield send_q
    (plane_state,) = mixing(
        "mix_plane", plane_body, passing, place, [near_q, far_q], [(quarter, BF16)]
    )
    one_below = moved(plane_state, up(shards))
    wait = yield plane_state
    if wait is not None:
        near_q = after(near_q, wait)
    two_below = moved(one_below, up(shards))
    near_e, send_e = mixing(
        "mix_enter",
        enter_body,
        passing,
        place,
        [near_q, far_q, one_below, two_below],
        [(quarter, F32), (quarter, BF16)],
    )
    got_e = moved(send_e, cross(shards))
    mine, other = mixing(
        "mix_core", core_body, passing, place, [keep, sent, near_e, got_e], [(half, BF16), (half, BF16)]
    )
    yield mine, moved(other, core(shards))


def carried_in_any(state, passing, me, shards):
    states = lax.all_gather(state, "seq")

    def turn(j, total):
        part = passing[j][:, None, None] * total + states[j].astype(F32)
        return jnp.where(j < me, part, total)

    return lax.fori_loop(0, shards, turn, jnp.zeros(state.shape, F32)).astype(BF16)


def body(
    sparse_query, sparse_key, sparse_value, light_query, light_key, log_decay, segments, block_list
):
    tokens = sparse_query.shape[0]
    kv_heads = sparse_key.shape[1] // HD
    heads = light_query.shape[1] // HD
    group = heads // kv_heads
    shards = lax.axis_size("seq")
    me = lax.axis_index("seq")
    place = me.astype(jnp.int32).reshape(1)
    planes = shards == 16 and kv_heads == 4
    chunks = 2 if planes else 1
    kv_chunk = kv_heads // chunks
    head_chunk = heads // chunks
    parts = []
    for chunk in range(chunks):
        cols = slice(chunk * kv_chunk * HD, (chunk + 1) * kv_chunk * HD)
        parts += [sparse_key[:, cols], sparse_value[:, cols]]
    own = jnp.concatenate(parts, axis=1)
    seg_col, seg_row, listing = segments[:, None], segments[None, :], block_list.reshape(-1)
    if planes:
        below, beside = moved(own, up(shards)), moved(own, cross(shards))
    else:
        pieces = [lax.all_gather(own, "seq", axis=0, tiled=True)]
    whiches = []
    for chunk in range(chunks):
        order = [1 - (me & 1), me & 1] if planes else range(kv_chunk)
        for kv_head in order:
            kv_head = jnp.asarray(kv_head, jnp.int32)
            at = [chunk * kv_chunk + kv_head, chunk * 2 * kv_chunk + kv_head]
            whiches.append(jnp.stack(at))
    info = own_info(log_decay, seg_row, shards)
    info, whiches, place, listing, seg_col = after((info, whiches, place, listing, seg_col), own)
    known = lax.all_to_all(info, "seq", 0, 0, tiled=True)
    passing = all_passing(known, heads, tokens)
    sizes = (1,) * 11 if planes else (shards,)
    *biases, table = seen_table(place, listing, known, seg_col, seg_row, sizes, heads, planes)
    if planes:
        below, beside = after((below, beside), known)
        second, below_beside = moved(below, up(shards)), moved(below, cross(shards))
        own_far, below_far, beside_far = (
            moved(part, core(shards)) for part in (own, below, beside)
        )
        light_query, light_key = after((light_query, light_key), table)
    weights, faded_k, faded_q = local_part(
        light_query, light_key, log_decay, seg_col, seg_row, group
    )
    if planes:
        second, below_beside, weights, faded_k, faded_q = after(
            (second, below_beside, weights, faded_k, faded_q)
        )
        last = moved(second, cross(shards))
        second_far, below_beside_far, last_far = (
            moved(part, core(shards)) for part in (second, below_beside, last)
        )
        pieces = [below, second, beside, below_beside, last, own_far, below_far, second_far]
        pieces += [beside_far, below_beside_far, last_far]

    attended = None

    def attend(chunk, turn, attended):
        return attend_part(
            whiches[chunk * kv_chunk + turn],
            table,
            biases,
            sparse_query,
            own,
            faded_k,
            pieces,
            sizes,
            kv_chunk,
            attended,
        )

    if planes:
        attended, send0 = attend(0, 0, attended)
        attended, keep0 = attend(0, 1, attended)
        carry0 = carried_in_planes(keep0, send0, passing, place, shards, 0, heads)
        attended = after(attended, next(carry0))
        attended, send1 = attend(1, 0, attended)
        attended = after(attended, next(carry0))
        attended, keep1 = attend(1, 1, attended)
        inside = inside_part(weights, attended, group)
        carry1 = carried_in_planes(keep1, send1, passing, place, shards, head_chunk, heads)
        next(carry1)
        next(carry1)
        states = [carry0.send(inside), carry1.send(None)]
    else:
        parts = []
        for kv_head in range(kv_heads):
            attended, state = attend(0, kv_head, attended)
            parts.append(state)
        inside = inside_part(weights, attended, group)
        entering = carried_in_any(jnp.concatenate(parts), passing[:, :heads], me, shards)
        entering = entering * passing[me, heads].astype(BF16)
        states = [(entering, entering)]
    result, squares = output_part(place, inside, faded_q, states, group, planes)
    if lax.axis_size("head") == 2:
        squares = squares + lax.ppermute(squares, "head", [(0, 1), (1, 0)])
    else:
        squares = lax.psum(squares, "head")
    return (attended, scale_part(squares, result, group))


def solution(mesh):
    in_specs = (
        P("seq", "head"),
        P("seq", "head"),
        P("seq", "head"),
        P("seq", "head"),
        P("seq", "head"),
        P("head", "seq"),
        P("seq"),
        P("seq", None),
    )
    out_specs = (P("seq", "head"), P("seq", "head"))
    return jax.shard_map(body, mesh=mesh, in_specs=in_specs, out_specs=out_specs, check_vma=False)
```

time: 450 us -> 122 us (0.27)
  matrix products: 122 us -> 0 us
  waiting for transfers between devices: 139 us -> 43.4 us
  other arithmetic: 50.9 us -> 0.22 us
  local copies, waits for them, and re-layouts: 51.5 us -> 2.96 us
  blocking collectives: 59.9 us -> 13.1 us
  Pallas kernels: 0 us -> 39.5 us
  starting transfers between devices: 3.38 us -> 22.2 us
  between operations: 18.4 us -> 0.89 us
    all_gather x2 -> x0, waiting for transfers between devices: 139 us -> none  [the longest x1 110 us: carried_in(): pieces = jax.tree.map(lambda part: lax.all_gather(part, axis), value)]
    dot_general x11 -> x0, matrix products: 100 us -> none  [the longest x2 33 us: attend_block(): jnp.einsum('kgqn,nkd->qkgd', weights, value_part, preferred_element_type=...]
    ppermute x1 -> x24, waiting for transfers between devices: 0.01 us -> 43.4 us  [the longest x23 41.3 us: moved(): return lax.ppermute(value, 'seq', pairs)]
    pallas_call x0 -> x19, Pallas kernels: none -> 39.5 us  [the longest x4 15.9 us: attend_part(): pl.pallas_call(functools.partial(attend_kernel, sizes, kv_step), grid_spe...]
    select_n x16 -> x0, other arithmetic: 32.1 us -> none  [the longest x15 31.4 us: turn(): jnp.where(position < mine, new, old)]
    unnamed x1 -> x0, blocking collectives: 31.9 us -> none
    slice x15 -> x1, local copies, waits for them, and re-layouts: 25.6 us -> 1.15 us  [body(): parts += [sparse_key[:, cols], sparse_value[:, cols]]]
    all_gather x1 -> x0, blocking collectives: 23.1 us -> none  [body(): seg_portion = lax.all_gather(segments, 'seq', axis=0, tiled=True)]
  transfers between devices with their start and end apart: 3 -> 24, of which waited for: 2 -> 12; matrix products, arithmetic and copies ran while one was open for 10% -> 0% of each run, Pallas kernels for 0% -> 21%
where the time goes in v2:
time: 122 us
  waiting for transfers between devices  43.4 us (36%)
  Pallas kernels  39.5 us (32%)
  starting transfers between devices  22.2 us (18%)
  blocking collectives  13.1 us (11%)
  local copies, waits for them, and re-layouts  2.96 us (2%)
    ppermute x23, waiting for transfers between devices, moved(): return lax.ppermute(value, 'seq', pairs)  41.3 us
    ppermute x23, starting transfers between devices, moved(): return lax.ppermute(value, 'seq', pairs)  20.6 us
    pallas_call x4, Pallas kernels, attend_part(): pl.pallas_call(functools.partial(attend_kernel, sizes, kv_step), grid_spe...  15.9 us
    all_to_all x1, blocking collectives, body(): known = lax.all_to_all(info, 'seq', 0, 0, tiled=True)  13.1 us
    pallas_call x1, Pallas kernels, local_part(): pl.pallas_call(local_kernel, grid=(steps,), in_specs=[wide, wide, pl.Bloc...  8.93 us
    pallas_call x8, Pallas kernels, mixing(): pl.pallas_call(functools.partial(mixing_kernel, body), in_specs=[smem, sm...  6.14 us
  transfers between devices with their start and end apart: 24, of which 12 were waited for; matrix products, arithmetic and copies ran while one was open for 0% of the time, Pallas kernels for 21%

profile of v2, /device:TPU:0, one launch (start us, length us, event | category | flops | bytes accessed | tf_op | source)
XLA Modules:
  0.0 122.2 jit_solution(4498550855859655160)
XLA Ops:
  1.9 3.1 %collective-permute-start = (bf16[256,1024]{1,0:T(8,128)(2,1)S(1)}, bf16[256,1024]{1,0:T(8,128)(2,1)S(1)}, u32[]{:S(2)}, u32[]{:S(2)}) collective-permute-start(bf16[256,1024]{1,0:T(8,128)(2,1)S(1)} %pad_maximum_fusion.refs_1_.refs_2_), channel_id=1, source_target_pairs={{0,8},{2,10},{4,12},{6,14},{8,16},{10,18},{12,20},{14,22},{16,24},... | collective-permute-start | bytes 1572872 | tf_op jit(solution)/shard_map/ppermute | solution.py:523
  6.8 13.1 %all_to_all.11 = f32[16,1,128]{2,1,0:T(1,128)S(1)} all-to-all(f32[16,1,128]{2,1,0:T(1,128)S(1)} %bitcast.15), channel_id=1, replica_groups=mesh['seq'=16,'head'=2] {'seq'}, dimensions={0} | all-to-all | bytes 16384 | tf_op jit(solution)/shard_map/all_to_all | solution.py:699
  23.3 8.9 %local_scores.1 = (bf16[32,256,256]{2,1,0:T(8,128)(2,1)S(1)}, bf16[32,128,256]{2,1,0:T(8,128)(2,1)S(1)}, bf16[256,4096]{1,0:T(8,128)(2,1)S(1)}) custom-call(bf16[256,4096]{1,0:T(8,128)(2,1)} %q_ref, bf16[256,4096]{1,0:T(8,128)(2,1)} %k_ref, f32[32,256]{1,0:T(8,128)S(1)} %copy-done.1, s32[256,1]{1,0:T(8,128)S(1)} %copy.16.segc_ref, s32[1,256]{1,0:T(1,128)S(1)} %bitcast.19), custom_call_target="tpu_custom_call" | custom-call | flops 536870912 | bytes 12582912 | tf_op jit(solution)/shard_map/local_scores/pallas_call | solution.py:135
  32.2 3.2 %collective-permute-done.2.refs_8_ = bf16[256,1024]{1,0:T(8,128)(2,1)S(1)} collective-permute-done((bf16[256,1024]{1,0:T(8,128)(2,1)S(1)}, bf16[256,1024]{1,0:T(8,128)(2,1)S(1)}, u32[]{:S(2)}, u32[]{:S(2)}) %collective-permute-start.2) | collective-permute-done | bytes 524320 | tf_op jit(solution)/shard_map/ppermute | solution.py:523
  37.3 10.9 %collective-permute-done.4.refs_11_ = bf16[256,1024]{1,0:T(8,128)(2,1)S(1)} collective-permute-done((bf16[256,1024]{1,0:T(8,128)(2,1)S(1)}, bf16[256,1024]{1,0:T(8,128)(2,1)S(1)}, u32[]{:S(2)}, u32[]{:S(2)}) %collective-permute-start.4) | collective-permute-done | bytes 524320 | tf_op jit(solution)/shard_map/ppermute | solution.py:523
  48.2 1.9 %collective-permute-done.10.refs_17_ = bf16[256,1024]{1,0:T(8,128)(2,1)S(1)} collective-permute-done((bf16[256,1024]{1,0:T(8,128)(2,1)S(1)}, bf16[256,1024]{1,0:T(8,128)(2,1)S(1)}, u32[]{:S(2)}, u32[]{:S(2)}) %collective-permute-start.10) | collective-permute-done | bytes 524320 | tf_op jit(solution)/shard_map/ppermute | solution.py:523
  50.1 4.1 %attend.4 = (bf16[256,4096]{1,0:T(8,128)(2,1)}, f32[8,128,128]{2,1,0:T(8,128)S(1)}) custom-call(s32[2]{0:T(128)S(1)} %get-tuple-element.72.kv_head, s32[35]{0:T(128)S(1)} %get-tuple-element.56.table, bf16[256,4096]{1,0:T(8,128)(2,1)} %refs_0_.7, bf16[256,1024]{1,0:T(8,128)(2,1)S(1)} %pad_maximum_fusion.refs_1_.refs_2_, ...), custom_call_target="tpu_custom_call" | custom-call | flops 1006632960 | bytes 3145728 | tf_op jit(solution)/shard_map/attend/pallas_call | solution.py:377
  54.9 4.0 %attend.5 = (bf16[256,4096]{1,0:T(8,128)(2,1)}, f32[8,128,128]{2,1,0:T(8,128)S(1)}) custom-call(s32[2]{0:T(128)S(1)} %get-tuple-element.71.kv_head, s32[35]{0:T(128)S(1)} %get-tuple-element.56.table, bf16[256,4096]{1,0:T(8,128)(2,1)} %refs_0_.7, bf16[256,1024]{1,0:T(8,128)(2,1)S(1)} %pad_maximum_fusion.refs_1_.refs_2_, ...), custom_call_target="tpu_custom_call", output_to_operand_aliasing={{0}: (20, {})} | custom-call | flops 1006632960 | bytes 3145728 | tf_op jit(solution)/shard_map/attend/pallas_call | solution.py:377
  59.6 3.9 %attend.6 = (bf16[256,4096]{1,0:T(8,128)(2,1)}, f32[8,128,128]{2,1,0:T(8,128)S(1)}) custom-call(s32[2]{0:T(128)S(1)} %get-tuple-element.70.kv_head, s32[35]{0:T(128)S(1)} %get-tuple-element.56.table, bf16[256,4096]{1,0:T(8,128)(2,1)} %refs_0_.7, bf16[256,1024]{1,0:T(8,128)(2,1)S(1)} %pad_maximum_fusion.refs_1_.refs_2_, ...), custom_call_target="tpu_custom_call", output_to_operand_aliasing={{0}: (20, {})} | custom-call | flops 1006632960 | bytes 3145728 | tf_op jit(solution)/shard_map/attend/pallas_call | solution.py:377
  64.6 5.1 %collective-permute-start.12 = (bf16[4,128,128]{2,1,0:T(8,128)(2,1)S(1)}, bf16[4,128,128]{2,1,0:T(8,128)(2,1)S(1)}, u32[]{:S(2)}, u32[]{:S(2)}) collective-permute-start(bf16[4,128,128]{2,1,0:T(8,128)(2,1)S(1)} %get-tuple-element.77), channel_id=1, source_target_pairs={{0,4},{2,6},{4,0},{6,2},{8,12},{10,14},{12,8},{14,10},{16,20},{18,... | collective-permute-start | bytes 393224 | tf_op jit(solution)/shard_map/ppermute | solution.py:523
  69.7 3.7 %collective-permute-done.12.refs_1_ = bf16[4,128,128]{2,1,0:T(8,128)(2,1)S(1)} collective-permute-done((bf16[4,128,128]{2,1,0:T(8,128)(2,1)S(1)}, bf16[4,128,128]{2,1,0:T(8,128)(2,1)S(1)}, u32[]{:S(2)}, u32[]{:S(2)}) %collective-permute-start.12) | collective-permute-done | bytes 131104 | tf_op jit(solution)/shard_map/ppermute | solution.py:523
  74.2 4.0 %attend.7 = (bf16[256,4096]{1,0:T(8,128)(2,1)}, f32[8,128,128]{2,1,0:T(8,128)S(1)}) custom-call(s32[2]{0:T(128)S(1)} %get-tuple-element.51.kv_head, s32[35]{0:T(128)S(1)} %get-tuple-element.56.table, bf16[256,4096]{1,0:T(8,128)(2,1)} %refs_0_.7, bf16[256,1024]{1,0:T(8,128)(2,1)S(1)} %pad_maximum_fusion.refs_1_.refs_2_, ...), custom_call_target="tpu_custom_call", output_to_operand_aliasing={{0}: (20, {})} | custom-call | flops 1006632960 | bytes 3145728 | tf_op jit(solution)/shard_map/attend/pallas_call | solution.py:377
  78.9 2.9 %collective-permute-start.17 = (bf16[4,128,128]{2,1,0:T(8,128)(2,1)S(1)}, bf16[4,128,128]{2,1,0:T(8,128)(2,1)S(1)}, u32[]{:S(2)}, u32[]{:S(2)}) collective-permute-start(bf16[4,128,128]{2,1,0:T(8,128)(2,1)S(1)} %get-tuple-element.92), channel_id=1, source_target_pairs={{0,4},{2,6},{4,0},{6,2},{8,12},{10,14},{12,8},{14,10},{16,20},{18,... | collective-permute-start | bytes 393224 | tf_op jit(solution)/shard_map/ppermute | solution.py:523
  82.1 3.4 %collective-permute-done.17.refs_1_ = bf16[4,128,128]{2,1,0:T(8,128)(2,1)S(1)} collective-permute-done((bf16[4,128,128]{2,1,0:T(8,128)(2,1)S(1)}, bf16[4,128,128]{2,1,0:T(8,128)(2,1)S(1)}, u32[]{:S(2)}, u32[]{:S(2)}) %collective-permute-start.17) | collective-permute-done | bytes 131104 | tf_op jit(solution)/shard_map/ppermute | solution.py:523
  86.2 2.2 %collective-permute-start.18 = (bf16[4,128,128]{2,1,0:T(8,128)(2,1)S(1)}, bf16[4,128,128]{2,1,0:T(8,128)(2,1)S(1)}, u32[]{:S(2)}, u32[]{:S(2)}) collective-permute-start(bf16[4,128,128]{2,1,0:T(8,128)(2,1)S(1)} %mix_plane.3), channel_id=1, source_target_pairs={{0,8},{2,10},{4,12},{6,14},{8,16},{10,18},{12,20},{14,22},{16,24},... | collective-permute-start | bytes 393224 | tf_op jit(solution)/shard_map/ppermute | solution.py:523
  88.5 6.0 %collective-permute-done.13.refs_2_ = bf16[4,128,128]{2,1,0:T(8,128)(2,1)S(1)} collective-permute-done((bf16[4,128,128]{2,1,0:T(8,128)(2,1)S(1)}, bf16[4,128,128]{2,1,0:T(8,128)(2,1)S(1)}, u32[]{:S(2)}, u32[]{:S(2)}) %collective-permute-start.13) | collective-permute-done | bytes 131104 | tf_op jit(solution)/shard_map/ppermute | solution.py:523
  94.5 4.6 %collective-permute-done.18.refs_2_ = bf16[4,128,128]{2,1,0:T(8,128)(2,1)S(1)} collective-permute-done((bf16[4,128,128]{2,1,0:T(8,128)(2,1)S(1)}, bf16[4,128,128]{2,1,0:T(8,128)(2,1)S(1)}, u32[]{:S(2)}, u32[]{:S(2)}) %collective-permute-start.18) | collective-permute-done | bytes 131104 | tf_op jit(solution)/shard_map/ppermute | solution.py:523
  100.6 2.1 %inside.1.inside_ref = f32[256,4096]{1,0:T(8,128)S(1)} custom-call(bf16[32,256,256]{2,1,0:T(8,128)(2,1)S(1)} %get-tuple-element.84.w_ref, bf16[256,4096]{1,0:T(8,128)(2,1)S(1)} %copy-done), custom_call_target="tpu_custom_call" | custom-call | flops 536870912 | bytes 10485760 | tf_op jit(solution)/shard_map/inside/pallas_call | solution.py:414
  103.7 2.1 %collective-permute-done.19.refs_3_ = bf16[4,128,128]{2,1,0:T(8,128)(2,1)S(1)} collective-permute-done((bf16[4,128,128]{2,1,0:T(8,128)(2,1)S(1)}, bf16[4,128,128]{2,1,0:T(8,128)(2,1)S(1)}, u32[]{:S(2)}, u32[]{:S(2)}) %collective-permute-start.19) | collective-permute-done | bytes 131104 | tf_op jit(solution)/shard_map/ppermute | solution.py:523
  106.7 1.9 %collective-permute-done.15.refs_3_ = bf16[4,128,128]{2,1,0:T(8,128)(2,1)S(1)} collective-permute-done((bf16[4,128,128]{2,1,0:T(8,128)(2,1)S(1)}, bf16[4,128,128]{2,1,0:T(8,128)(2,1)S(1)}, u32[]{:S(2)}, u32[]{:S(2)}) %collective-permute-start.15) | collective-permute-done | bytes 131104 | tf_op jit(solution)/shard_map/ppermute | solution.py:523
  109.5 2.1 %collective-permute-done.20.refs_3_ = bf16[4,128,128]{2,1,0:T(8,128)(2,1)S(1)} collective-permute-done((bf16[4,128,128]{2,1,0:T(8,128)(2,1)S(1)}, bf16[4,128,128]{2,1,0:T(8,128)(2,1)S(1)}, u32[]{:S(2)}, u32[]{:S(2)}) %collective-permute-start.20) | collective-permute-done | bytes 131104 | tf_op jit(solution)/shard_map/ppermute | solution.py:523
  114.1 2.2 %outputs.1 = (f32[256,4096]{1,0:T(8,128)S(1)}, f32[1,256]{1,0:T(1,128)S(1)}) custom-call(s32[1]{0:T(128)} %bitcast.7.place_ref, bf16[256,4096]{1,0:T(8,128)(2,1)S(1)} %get-tuple-element.83.q_ref, f32[256,4096]{1,0:T(8,128)S(1)} %inside.1.inside_ref, bf16[8,128,128]{2,1,0:T(8,128)(2,1)S(1)} %get-tuple-element.88.refs_0_, ...), custom_call_target="tpu_custom_call" | custom-call | flops 268435456 | bytes 11534336 | tf_op jit(solution)/shard_map/outputs/pallas_call | solution.py:476
  117.8 2.1 %collective-permute-done.23 = f32[1,256]{1,0:T(1,128)S(1)} collective-permute-done((f32[1,256]{1,0:T(1,128)S(1)}, f32[1,256]{1,0:T(1,128)S(1)}, u32[]{:S(2)}, u32[]{:S(2)}) %collective-permute-start.23) | collective-permute-done | bytes 1056 | tf_op jit(solution)/shard_map/ppermute | solution.py:764
  119.9 2.3 %scaled.1 = bf16[256,4096]{1,0:T(8,128)(2,1)} custom-call(f32[1,256]{1,0:T(1,128)S(1)} %add.21.squares_ref, f32[256,4096]{1,0:T(8,128)S(1)} %get-tuple-element.99.value_ref), custom_call_target="tpu_custom_call" | custom-call | tf_op jit(solution)/shard_map/scaled/pallas_call | solution.py:511
  (59 shorter events, 21.6 us)
Async XLA Ops:
  1.9 18.1 %collective-permute-start = (bf16[256,1024]{1,0:T(8,128)(2,1)S(1)}, bf16[256,1024]{1,0:T(8,128)(2,1)S(1)}, u32[]{:S(2)}, u32[]{:S(2)}) collective-permute-start(bf16[256,1024]{1,0:T(8,128)(2,1)S(1)} %pad_maximum_fusion.refs_1_.refs_2_), channel_id=1, source_target_pairs={{0,8},{2,10},{4,12},{6,14},{8,16},{10,18},{12,20},{14,22},{16,24},... | collective-permute-start | bytes 1572872 | tf_op jit(solution)/shard_map/ppermute | solution.py:523
  5.0 15.0 %collective-permute-start.1 = (bf16[256,1024]{1,0:T(8,128)(2,1)S(1)}, bf16[256,1024]{1,0:T(8,128)(2,1)S(1)}, u32[]{:S(2)}, u32[]{:S(2)}) collective-permute-start(bf16[256,1024]{1,0:T(8,128)(2,1)S(1)} %pad_maximum_fusion.refs_1_.refs_2_), channel_id=1, source_target_pairs={{0,4},{2,6},{4,0},{6,2},{8,12},{10,14},{12,8},{14,10},{16,20},{18,... | collective-permute-start | bytes 1572872 | tf_op jit(solution)/shard_map/ppermute | solution.py:523
  20.0 15.4 %collective-permute-start.2 = (bf16[256,1024]{1,0:T(8,128)(2,1)S(1)}, bf16[256,1024]{1,0:T(8,128)(2,1)S(1)}, u32[]{:S(2)}, u32[]{:S(2)}) collective-permute-start(bf16[256,1024]{1,0:T(8,128)(2,1)S(1)} %collective-permute-done.refs_7_), channel_id=1, source_target_pairs={{0,8},{2,10},{4,12},{6,14},{8,16},{10,18},{12,20},{14,22},{16,24},... | collective-permute-start | bytes 1572872 | tf_op jit(solution)/shard_map/ppermute | solution.py:523
  20.5 14.9 %collective-permute-start.3 = (bf16[256,1024]{1,0:T(8,128)(2,1)S(1)}, bf16[256,1024]{1,0:T(8,128)(2,1)S(1)}, u32[]{:S(2)}, u32[]{:S(2)}) collective-permute-start(bf16[256,1024]{1,0:T(8,128)(2,1)S(1)} %collective-permute-done.refs_7_), channel_id=1, source_target_pairs={{0,4},{2,6},{4,0},{6,2},{8,12},{10,14},{12,8},{14,10},{16,20},{18,... | collective-permute-start | bytes 1572872 | tf_op jit(solution)/shard_map/ppermute | solution.py:523
  21.6 15.2 %collective-permute-start.5 = (bf16[256,1024]{1,0:T(8,128)(2,1)S(1)}, bf16[256,1024]{1,0:T(8,128)(2,1)S(1)}, u32[]{:S(2)}, u32[]{:S(2)}) collective-permute-start(bf16[256,1024]{1,0:T(8,128)(2,1)S(1)} %pad_maximum_fusion.refs_1_.refs_2_), channel_id=1, source_target_pairs={{0,2},{2,0},{4,6},{6,4},{8,10},{10,8},{12,14},{14,12},{16,18},{18,... | collective-permute-start | bytes 1572872 | tf_op jit(solution)/shard_map/ppermute | solution.py:523
  35.4 12.7 %collective-permute-start.4 = (bf16[256,1024]{1,0:T(8,128)(2,1)S(1)}, bf16[256,1024]{1,0:T(8,128)(2,1)S(1)}, u32[]{:S(2)}, u32[]{:S(2)}) collective-permute-start(bf16[256,1024]{1,0:T(8,128)(2,1)S(1)} %collective-permute-done.2.refs_8_), channel_id=1, source_target_pairs={{0,4},{2,6},{4,0},{6,2},{8,12},{10,14},{12,8},{14,10},{16,20},{18,... | collective-permute-start | bytes 1572872 | tf_op jit(solution)/shard_map/ppermute | solution.py:523
  36.2 11.9 %collective-permute-start.6 = (bf16[256,1024]{1,0:T(8,128)(2,1)S(1)}, bf16[256,1024]{1,0:T(8,128)(2,1)S(1)}, u32[]{:S(2)}, u32[]{:S(2)}) collective-permute-start(bf16[256,1024]{1,0:T(8,128)(2,1)S(1)} %collective-permute-done.refs_7_), channel_id=1, source_target_pairs={{0,2},{2,0},{4,6},{6,4},{8,10},{10,8},{12,14},{14,12},{16,18},{18,... | collective-permute-start | bytes 1572872 | tf_op jit(solution)/shard_map/ppermute | solution.py:523
  36.2 11.9 %collective-permute-start.8 = (bf16[256,1024]{1,0:T(8,128)(2,1)S(1)}, bf16[256,1024]{1,0:T(8,128)(2,1)S(1)}, u32[]{:S(2)}, u32[]{:S(2)}) collective-permute-start(bf16[256,1024]{1,0:T(8,128)(2,1)S(1)} %collective-permute-done.1.refs_9_), channel_id=1, source_target_pairs={{0,2},{2,0},{4,6},{6,4},{8,10},{10,8},{12,14},{14,12},{16,18},{18,... | collective-permute-start | bytes 1572872 | tf_op jit(solution)/shard_map/ppermute | solution.py:523
  36.8 11.4 %collective-permute-start.7 = (bf16[256,1024]{1,0:T(8,128)(2,1)S(1)}, bf16[256,1024]{1,0:T(8,128)(2,1)S(1)}, u32[]{:S(2)}, u32[]{:S(2)}) collective-permute-start(bf16[256,1024]{1,0:T(8,128)(2,1)S(1)} %collective-permute-done.2.refs_8_), channel_id=1, source_target_pairs={{0,2},{2,0},{4,6},{6,4},{8,10},{10,8},{12,14},{14,12},{16,18},{18,... | collective-permute-start | bytes 1572872 | tf_op jit(solution)/shard_map/ppermute | solution.py:523
  36.8 11.4 %collective-permute-start.9 = (bf16[256,1024]{1,0:T(8,128)(2,1)S(1)}, bf16[256,1024]{1,0:T(8,128)(2,1)S(1)}, u32[]{:S(2)}, u32[]{:S(2)}) collective-permute-start(bf16[256,1024]{1,0:T(8,128)(2,1)S(1)} %collective-permute-done.3.refs_10_), channel_id=1, source_target_pairs={{0,2},{2,0},{4,6},{6,4},{8,10},{10,8},{12,14},{14,12},{16,18},{18,... | collective-permute-start | bytes 1572872 | tf_op jit(solution)/shard_map/ppermute | solution.py:523
  48.2 1.9 %collective-permute-start.10 = (bf16[256,1024]{1,0:T(8,128)(2,1)S(1)}, bf16[256,1024]{1,0:T(8,128)(2,1)S(1)}, u32[]{:S(2)}, u32[]{:S(2)}) collective-permute-start(bf16[256,1024]{1,0:T(8,128)(2,1)S(1)} %collective-permute-done.4.refs_11_), channel_id=1, source_target_pairs={{0,2},{2,0},{4,6},{6,4},{8,10},{10,8},{12,14},{14,12},{16,18},{18,... | collective-permute-start | bytes 1572872 | tf_op jit(solution)/shard_map/ppermute | solution.py:523
  54.1 4.7 %collective-permute-start.11 = (f32[8,128,128]{2,1,0:T(8,128)S(1)}, f32[8,128,128]{2,1,0:T(8,128)S(1)}, u32[]{:S(2)}, u32[]{:S(2)}) collective-permute-start(f32[8,128,128]{2,1,0:T(8,128)S(1)} %get-tuple-element.76), channel_id=1, source_target_pairs={{0,2},{2,0},{4,6},{6,4},{8,10},{10,8},{12,14},{14,12},{16,18},{18,... | collective-permute-start | bytes 1572872 | tf_op jit(solution)/shard_map/ppermute | solution.py:523
  63.6 14.6 %collective-permute-start.16 = (f32[8,128,128]{2,1,0:T(8,128)S(1)}, f32[8,128,128]{2,1,0:T(8,128)S(1)}, u32[]{:S(2)}, u32[]{:S(2)}) collective-permute-start(f32[8,128,128]{2,1,0:T(8,128)S(1)} %get-tuple-element.90), channel_id=1, source_target_pairs={{0,2},{2,0},{4,6},{6,4},{8,10},{10,8},{12,14},{14,12},{16,18},{18,... | collective-permute-start | bytes 1572872 | tf_op jit(solution)/shard_map/ppermute | solution.py:523
  64.6 8.8 %collective-permute-start.12 = (bf16[4,128,128]{2,1,0:T(8,128)(2,1)S(1)}, bf16[4,128,128]{2,1,0:T(8,128)(2,1)S(1)}, u32[]{:S(2)}, u32[]{:S(2)}) collective-permute-start(bf16[4,128,128]{2,1,0:T(8,128)(2,1)S(1)} %get-tuple-element.77), channel_id=1, source_target_pairs={{0,4},{2,6},{4,0},{6,2},{8,12},{10,14},{12,8},{14,10},{16,20},{18,... | collective-permute-start | bytes 393224 | tf_op jit(solution)/shard_map/ppermute | solution.py:523
  78.9 6.6 %collective-permute-start.17 = (bf16[4,128,128]{2,1,0:T(8,128)(2,1)S(1)}, bf16[4,128,128]{2,1,0:T(8,128)(2,1)S(1)}, u32[]{:S(2)}, u32[]{:S(2)}) collective-permute-start(bf16[4,128,128]{2,1,0:T(8,128)(2,1)S(1)} %get-tuple-element.92), channel_id=1, source_target_pairs={{0,4},{2,6},{4,0},{6,2},{8,12},{10,14},{12,8},{14,10},{16,20},{18,... | collective-permute-start | bytes 393224 | tf_op jit(solution)/shard_map/ppermute | solution.py:523
  81.8 12.7 %collective-permute-start.13 = (bf16[4,128,128]{2,1,0:T(8,128)(2,1)S(1)}, bf16[4,128,128]{2,1,0:T(8,128)(2,1)S(1)}, u32[]{:S(2)}, u32[]{:S(2)}) collective-permute-start(bf16[4,128,128]{2,1,0:T(8,128)(2,1)S(1)} %mix_plane.2), channel_id=1, source_target_pairs={{0,8},{2,10},{4,12},{6,14},{8,16},{10,18},{12,20},{14,22},{16,24},... | collective-permute-start | bytes 393224 | tf_op jit(solution)/shard_map/ppermute | solution.py:523
  86.2 12.8 %collective-permute-start.18 = (bf16[4,128,128]{2,1,0:T(8,128)(2,1)S(1)}, bf16[4,128,128]{2,1,0:T(8,128)(2,1)S(1)}, u32[]{:S(2)}, u32[]{:S(2)}) collective-permute-start(bf16[4,128,128]{2,1,0:T(8,128)(2,1)S(1)} %mix_plane.3), channel_id=1, source_target_pairs={{0,8},{2,10},{4,12},{6,14},{8,16},{10,18},{12,20},{14,22},{16,24},... | collective-permute-start | bytes 393224 | tf_op jit(solution)/shard_map/ppermute | solution.py:523
  94.5 8.3 %collective-permute-start.14 = (bf16[4,128,128]{2,1,0:T(8,128)(2,1)S(1)}, bf16[4,128,128]{2,1,0:T(8,128)(2,1)S(1)}, u32[]{:S(2)}, u32[]{:S(2)}) collective-permute-start(bf16[4,128,128]{2,1,0:T(8,128)(2,1)S(1)} %collective-permute-done.13.refs_2_), channel_id=1, source_target_pairs={{0,8},{2,10},{4,12},{6,14},{8,16},{10,18},{12,20},{14,22},{16,24},... | collective-permute-start | bytes 393224 | tf_op jit(solution)/shard_map/ppermute | solution.py:523
  99.0 6.8 %collective-permute-start.19 = (bf16[4,128,128]{2,1,0:T(8,128)(2,1)S(1)}, bf16[4,128,128]{2,1,0:T(8,128)(2,1)S(1)}, u32[]{:S(2)}, u32[]{:S(2)}) collective-permute-start(bf16[4,128,128]{2,1,0:T(8,128)(2,1)S(1)} %collective-permute-done.18.refs_2_), channel_id=1, source_target_pairs={{0,8},{2,10},{4,12},{6,14},{8,16},{10,18},{12,20},{14,22},{16,24},... | collective-permute-start | bytes 393224 | tf_op jit(solution)/shard_map/ppermute | solution.py:523
  103.6 5.0 %collective-permute-start.15 = (bf16[4,128,128]{2,1,0:T(8,128)(2,1)S(1)}, bf16[4,128,128]{2,1,0:T(8,128)(2,1)S(1)}, u32[]{:S(2)}, u32[]{:S(2)}) collective-permute-start(bf16[4,128,128]{2,1,0:T(8,128)(2,1)S(1)} %get-tuple-element.87), channel_id=1, source_target_pairs={{0,4},{2,6},{4,0},{6,2},{8,12},{10,14},{12,8},{14,10},{16,20},{18,... | collective-permute-start | bytes 393224 | tf_op jit(solution)/shard_map/ppermute | solution.py:523
  106.6 5.0 %collective-permute-start.20 = (bf16[4,128,128]{2,1,0:T(8,128)(2,1)S(1)}, bf16[4,128,128]{2,1,0:T(8,128)(2,1)S(1)}, u32[]{:S(2)}, u32[]{:S(2)}) collective-permute-start(bf16[4,128,128]{2,1,0:T(8,128)(2,1)S(1)} %get-tuple-element.94), channel_id=1, source_target_pairs={{0,4},{2,6},{4,0},{6,2},{8,12},{10,14},{12,8},{14,10},{16,20},{18,... | collective-permute-start | bytes 393224 | tf_op jit(solution)/shard_map/ppermute | solution.py:523
  109.4 3.1 %collective-permute-start.21 = (bf16[8,128,128]{2,1,0:T(8,128)(2,1)S(1)}, bf16[8,128,128]{2,1,0:T(8,128)(2,1)S(1)}, u32[]{:S(2)}, u32[]{:S(2)}) collective-permute-start(bf16[8,128,128]{2,1,0:T(8,128)(2,1)S(1)} %get-tuple-element.96), channel_id=1, source_target_pairs={{0,2},{2,0},{4,6},{6,4},{8,10},{10,8},{12,14},{14,12},{16,18},{18,... | collective-permute-start | bytes 786440 | tf_op jit(solution)/shard_map/ppermute | solution.py:523
  112.5 1.6 %collective-permute-start.22 = (bf16[8,128,128]{2,1,0:T(8,128)(2,1)S(1)}, bf16[8,128,128]{2,1,0:T(8,128)(2,1)S(1)}, u32[]{:S(2)}, u32[]{:S(2)}) collective-permute-start(bf16[8,128,128]{2,1,0:T(8,128)(2,1)S(1)} %get-tuple-element.97), channel_id=1, source_target_pairs={{0,2},{2,0},{4,6},{6,4},{8,10},{10,8},{12,14},{14,12},{16,18},{18,... | collective-permute-start | bytes 786440 | tf_op jit(solution)/shard_map/ppermute | solution.py:523
  116.2 3.6 %collective-permute-start.23 = (f32[1,256]{1,0:T(1,128)S(1)}, f32[1,256]{1,0:T(1,128)S(1)}, u32[]{:S(2)}, u32[]{:S(2)}) collective-permute-start(f32[1,256]{1,0:T(1,128)S(1)} %get-tuple-element.98), channel_id=1, source_target_pairs={{0,1},{1,0},{2,3},{3,2},{4,5},{5,4},{6,7},{7,6},{8,9},{9,8},{10,11... | collective-permute-start | bytes 3080 | tf_op jit(solution)/shard_map/ppermute | solution.py:764
  (4 other events, 19.2 us)

commit v3 on v2

--- a/solution.py
+++ b/solution.py
@@ -254,14 +254,14 @@
     )(listing, known, place, seg_col, seg_row)
 
 
-def attend_kernel(sizes, kv_step, kv_head, table, *refs):
+def attend_kernel(sizes, shifts, kv_step, group, kv_head, table, *refs):
     pieces = len(sizes)
-    q_ref, own_k, own_v, kf_ref, own_bias, row_bias, key_bias = refs[:7]
-    piece = refs[7 : 7 + pieces]
-    out_ref, state_ref, keys, values, sems = refs[-5:]
-    tokens, width = q_ref.shape
+    query_ref, own_ref, kf_ref, own_bias, row_bias, key_bias = refs[:6]
+    piece = refs[6 : 6 + pieces]
+    out_ref, state_ref, q_ref, keys, values, sems, q_sems = refs[-7:]
+    tokens, width = out_ref.shape
     blocks = tokens // BLK
-    group = width // HD
+    first_head = kv_head[0] * group
     per_row = keys.shape[0] // (blocks * BLK) - 1
     factor = HD ** (-0.5) * LOG2E
     total = sum(sizes)
@@ -284,7 +284,8 @@
         span = pl.ds(pl.multiple_of(j * tokens + table[3 * slot + 1] * BLK, BLK), BLK)
         to = pl.ds(pl.multiple_of(table[3 * slot] * BLK, BLK), BLK)
         for part, buffer in enumerate((keys, values)):
-            cols = pl.ds(pl.multiple_of((kv_head[1] + part * kv_step) * HD, HD), HD)
+            col = kv_head[1] + part * kv_step - shifts[i]
+            cols = pl.ds(pl.multiple_of(col * HD, HD), HD)
             yield pltpu.make_async_copy(piece[i].at[span, cols], buffer.at[to, :], sems.at[part, slot])
 
     def bring(i, slot, j):
@@ -299,11 +300,19 @@
             for copy in copies(i, slot, j):
                 copy.wait()
 
+    def query_copy(b):
+        here = pl.ds(pl.multiple_of(b * BLK, BLK), BLK)
+        cols = pl.ds(pl.multiple_of(kv_head[0] * width, HD), width)
+        return pltpu.make_async_copy(query_ref.at[here, cols], q_ref.at[here, :], q_sems.at[b])
+
+    for b in range(blocks):
+        query_copy(b).start()
     each_piece(bring)
     for b in range(blocks):
         base = b * (1 + per_row) * BLK
-        keys[base : base + BLK, :] = own_k[b * BLK : (b + 1) * BLK, :]
-        values[base : base + BLK, :] = own_v[b * BLK : (b + 1) * BLK, :]
+        for part, buffer in enumerate((keys, values)):
+            cols = pl.ds(pl.multiple_of((kv_head[1] + part * kv_step) * HD, HD), HD)
+            buffer[base : base + BLK, :] = own_ref[b * BLK : (b + 1) * BLK, cols]
     each_piece(arrive)
 
     def heads_out(b, tiles, h, count):
@@ -325,6 +334,7 @@
     classes = sorted({min(t, 1 + per_row) for t in CLASSES} | {1 + per_row})
 
     def block_out(b, carry):
+        query_copy(b).wait()
         need = table[3 * total + b] + 1
         low = 0
         for tiles in classes:
@@ -351,142 +361,129 @@
 
     lax.fori_loop(0, blocks, block_out, 0)
     for h in range(group):
-        state_ref[h] = nn(kf_ref[h], out_ref[:, h * HD : (h + 1) * HD])
-
-
-def attend_part(kv_head, table, biases, query, own, faded, pieces, sizes, kv_step, before):
+        state_ref[h] = nn(kf_ref[first_head + h], out_ref[:, h * HD : (h + 1) * HD])
+
+
+def attend_part(
+    kv_head, table, biases, query, own, faded, pieces, sizes, shifts, kv_step
+):
     tokens = query.shape[0]
     group = faded.shape[0] * HD // own.shape[1] * 2
-    width = group * HD
-    wide = pl.BlockSpec((tokens, width), lambda g, *s: (0, s[0][0]))
-    in_specs = [
-        wide,
-        pl.BlockSpec((tokens, HD), lambda g, *s: (0, s[0][1])),
-        pl.BlockSpec((tokens, HD), lambda g, *s: (0, s[0][1] + kv_step)),
-        pl.BlockSpec((group, HD, tokens), lambda g, *s: (s[0][0], 0, 0)),
-    ]
-    in_specs += [pl.BlockSpec(bias.shape, lambda g, *s: (0, 0, 0)) for bias in biases]
-    in_specs += [pl.BlockSpec(memory_space=pl.ANY)] * len(pieces)
-    operands = [far(query), own, own, faded, *biases, *pieces]
-    aliases = {}
-    if before is not None:
-        aliases = {2 + len(operands): 0}
-        in_specs.append(pl.BlockSpec(memory_space=pl.ANY))
-        operands.append(before)
+    blocks = tokens // BLK
+    smem = pl.BlockSpec(memory_space=pltpu.SMEM)
+    vmem = pl.BlockSpec(memory_space=pltpu.VMEM)
+    anywhere = pl.BlockSpec(memory_space=pl.ANY)
     rows = biases[2].shape[0] * BLK
     return pl.pallas_call(
-        functools.partial(attend_kernel, sizes, kv_step),
-        grid_spec=pltpu.PrefetchScalarGridSpec(
-            num_scalar_prefetch=2,
-            grid=(1,),
-            in_specs=in_specs,
-            out_specs=[wide, pl.BlockSpec((group, HD, HD), lambda g, *s: (0, 0, 0))],
-            scratch_shapes=[
-                pltpu.VMEM((rows, HD), BF16),
-                pltpu.VMEM((rows, HD), BF16),
-                pltpu.SemaphoreType.DMA((2, sum(sizes))),
-            ],
-        ),
+        functools.partial(attend_kernel, sizes, shifts, kv_step, group),
+        in_specs=[smem, smem, anywhere] + [vmem] * 5 + [anywhere] * len(pieces),
+        out_specs=[vmem, vmem],
+        scratch_shapes=[
+            pltpu.VMEM((tokens, group * HD), BF16),
+            pltpu.VMEM((rows, HD), BF16),
+            pltpu.VMEM((rows, HD), BF16),
+            pltpu.SemaphoreType.DMA((2, sum(sizes))),
+            pltpu.SemaphoreType.DMA((blocks,)),
+        ],
         out_shape=[
-            jax.ShapeDtypeStruct(query.shape, BF16),
+            jax.ShapeDtypeStruct((tokens, group * HD), BF16),
             jax.ShapeDtypeStruct((group, HD, HD), F32),
         ],
-        input_output_aliases=aliases,
-        compiler_params=room(20),
+        compiler_params=room(12),
         cost_estimate=pl.CostEstimate(
             flops=group * 10 * 6 * BLK * BLK * HD,
-            bytes_accessed=3 * 2 * tokens * width + 12 * 4 * tokens * HD,
+            bytes_accessed=12 * 4 * query.shape[0] * HD,
             transcendentals=group * 10 * BLK * BLK,
         ),
         name="attend",
-    )(kv_head, table, *operands)
-
-
-def inside_kernel(w_ref, v_ref, out_ref):
-    for i in range(w_ref.shape[0]):
-        cols = slice(i * HD, (i + 1) * HD)
-        out_ref[:, cols] = nn(w_ref[i], v_ref[:, cols])
-
-
-def inside_part(weights, valued, group):
-    tokens, width = valued.shape
-    steps = width // HD // group
-    return pl.pallas_call(
-        inside_kernel,
-        grid=(steps,),
-        in_specs=[
-            pl.BlockSpec((group, tokens, tokens), lambda g: (g, 0, 0)),
-            pl.BlockSpec((tokens, group * HD), lambda g: (0, g)),
-        ],
-        out_specs=pl.BlockSpec((tokens, group * HD), lambda g: (0, g)),
-        out_shape=jax.ShapeDtypeStruct((tokens, width), F32),
-        compiler_params=room(12),
+    )(kv_head, table, query, own, faded, *biases, *pieces)
+
+
+def inside_kernel(calls, order, w_ref, *refs):
+    part_refs = refs[:calls]
+    out_ref, whole_ref, sems = refs[calls:]
+    width = part_refs[0].shape[1]
+    group = width // HD
+
+    def copy(i):
+        cols = pl.ds(pl.multiple_of(order[i] * width, HD), width)
+        return pltpu.make_async_copy(part_refs[i], whole_ref.at[:, cols], sems.at[i])
+
+    for i in range(calls):
+        copy(i).start()
+    for i in range(calls):
+        for h in range(group):
+            at = order[i] * group + h
+            cols = pl.ds(pl.multiple_of(at * HD, HD), HD)
+            out_ref[:, cols] = nn(w_ref[at], part_refs[i][:, h * HD : (h + 1) * HD])
+    for i in range(calls):
+        copy(i).wait()
+
+
+def inside_part(order, weights, parts):
+    tokens = weights.shape[1]
+    width = weights.shape[0] * HD
+    vmem = pl.BlockSpec(memory_space=pltpu.VMEM)
+    return pl.pallas_call(
+        functools.partial(inside_kernel, len(parts)),
+        in_specs=[pl.BlockSpec(memory_space=pltpu.SMEM)] + [vmem] * (1 + len(parts)),
+        out_specs=[vmem, pl.BlockSpec(memory_space=pl.ANY)],
+        out_shape=[
+            jax.ShapeDtypeStruct((tokens, width), F32),
+            jax.ShapeDtypeStruct((tokens, width), BF16),
+        ],
+        scratch_shapes=[pltpu.SemaphoreType.DMA((len(parts),))],
+        compiler_params=room(4),
         cost_estimate=pl.CostEstimate(
-            flops=steps * group * 2 * tokens * tokens * HD,
-            bytes_accessed=steps * group * (2 * tokens * tokens + 6 * tokens * HD),
+            flops=width * 2 * tokens * tokens,
+            bytes_accessed=2 * tokens * tokens * (width // HD) + 6 * tokens * width,
             transcendentals=0,
         ),
         name="inside",
-    )(weights, valued)
-
-
-def output_kernel(planes, chunks, place_ref, q_ref, inside_ref, *refs):
-    keeps, gots = refs[:chunks], refs[chunks : 2 * chunks]
-    out_ref, squares_ref, total_ref = refs[-3:]
-    step_at = pl.program_id(0)
-    group = gots[0].shape[0]
-    steps = pl.num_programs(0) // chunks
-
-    @pl.when(step_at == 0)
-    def _():
-        total_ref[...] = jnp.zeros_like(total_ref)
-
-    def part(state_of):
-        total = total_ref[...]
+    )(order, weights, *parts)
+
+
+def output_kernel(planes, group, place_ref, q_ref, inside_ref, *refs):
+    out_ref, squares_ref = refs[-2:]
+    states = refs[:-2]
+    keeps, gots = states[: len(states) // 2], states[len(states) // 2 :]
+    tokens, width = out_ref.shape
+    per = width // HD // group // len(keeps)
+
+    def part(first, state_of, total):
         for i in range(group):
-            cols = slice(i * HD, (i + 1) * HD)
+            cols = slice((first + i) * HD, (first + i + 1) * HD)
             result = inside_ref[:, cols] + nn(q_ref[:, cols], state_of(i))
             out_ref[:, cols] = result
             total += result * result
-        total_ref[...] = total
-
-    for chunk in range(chunks):
-
-        @pl.when((step_at >= chunk * steps) & (step_at < (chunk + 1) * steps))
-        def _(chunk=chunk):
-            keep_ref, got_ref = keeps[chunk], gots[chunk]
+        return total
+
+    total = jnp.zeros((tokens, HD), F32)
+    for chunk, (keep_ref, got_ref) in enumerate(zip(keeps, gots, strict=True)):
+        for g in range(per):
+            first = (chunk * per + g) * group
             if planes:
-                mine = step_at - chunk * steps == (place_ref[0] & 1)
-                part(lambda i: jnp.where(mine, keep_ref[i], got_ref[i]))
+                mine = (place_ref[0] & 1) == g
+                total = part(first, lambda i: jnp.where(mine, keep_ref[i], got_ref[i]), total)
             else:
-                part(lambda i: keep_ref[i])
-
-    @pl.when(step_at == pl.num_programs(0) - 1)
-    def _():
-        squares_ref[...] = jnp.sum(jnp.transpose(total_ref[...]), axis=0, keepdims=True)
+                total = part(first, lambda i: keep_ref[g * group + i], total)
+    squares_ref[...] = jnp.sum(jnp.transpose(total), axis=0, keepdims=True)
 
 
 def output_part(place, inside, faded_q, states, group, planes):
     tokens, width = faded_q.shape
-    chunks = len(states)
-    steps = width // HD // group
-    wide = pl.BlockSpec((tokens, group * HD), lambda g, *s: (0, g))
-    keep = pl.BlockSpec((group, HD, HD), lambda g, *s: (0 if planes else g, 0, 0))
-    got = pl.BlockSpec((group, HD, HD), lambda g, *s: (0, 0, 0))
-    return pl.pallas_call(
-        functools.partial(output_kernel, planes, chunks),
-        grid_spec=pltpu.PrefetchScalarGridSpec(
-            num_scalar_prefetch=1,
-            grid=(steps,),
-            in_specs=[wide, wide] + [keep] * chunks + [got] * chunks,
-            out_specs=[wide, pl.BlockSpec((1, tokens), lambda g, *s: (0, 0))],
-            scratch_shapes=[pltpu.VMEM((tokens, HD), F32)],
-        ),
+    smem = pl.BlockSpec(memory_space=pltpu.SMEM)
+    vmem = pl.BlockSpec(memory_space=pltpu.VMEM)
+    return pl.pallas_call(
+        functools.partial(output_kernel, planes, group),
+        in_specs=[smem] + [vmem] * (2 + 2 * len(states)),
+        out_specs=[vmem, vmem],
         out_shape=[
             jax.ShapeDtypeStruct((tokens, width), F32),
             jax.ShapeDtypeStruct((1, tokens), F32),
         ],
-        compiler_params=room(16),
+        input_output_aliases={2: 0},
+        compiler_params=room(4),
         cost_estimate=pl.CostEstimate(
             flops=2 * tokens * width * HD,
             bytes_accessed=10 * tokens * width + 2 * width * HD,
@@ -496,25 +493,36 @@
     )(place, faded_q, inside, *[k for k, _ in states], *[g for _, g in states])
 
 
-def scale_kernel(features, squares_ref, value_ref, out_ref):
-    tokens = value_ref.shape[0]
+def scale_kernel(features, squares_ref, value_ref, out_ref, buffer, sems):
+    tokens, width = value_ref.shape
     row = lax.rsqrt(squares_ref[...] / features + norm_eps)
     scale = jnp.transpose(jnp.broadcast_to(row, (HD, tokens)))
-    for i in range(value_ref.shape[1] // HD):
-        cols = slice(i * HD, (i + 1) * HD)
-        out_ref[:, cols] = (value_ref[:, cols] * scale).astype(BF16)
-
-
-def scale_part(squares, value, per_step):
+    parts = sems.shape[0]
+    span = width // parts
+
+    def copy(part):
+        cols = slice(part * span, (part + 1) * span)
+        return pltpu.make_async_copy(buffer.at[:, cols], out_ref.at[:, cols], sems.at[part])
+
+    for part in range(parts):
+        for i in range(span // HD):
+            cols = slice(part * span + i * HD, part * span + (i + 1) * HD)
+            buffer[:, cols] = (value_ref[:, cols] * scale).astype(BF16)
+        copy(part).start()
+    for part in range(parts):
+        copy(part).wait()
+
+
+def scale_part(squares, value, parts):
     tokens, width = value.shape
-    wide = pl.BlockSpec((tokens, per_step * HD), lambda g: (0, g))
+    vmem = pl.BlockSpec(memory_space=pltpu.VMEM)
     return pl.pallas_call(
         functools.partial(scale_kernel, ASKER_CHANNELS * HD),
-        grid=(width // HD // per_step,),
-        in_specs=[pl.BlockSpec((1, tokens), lambda g: (0, 0)), wide],
-        out_specs=wide,
+        in_specs=[vmem, vmem],
+        out_specs=pl.BlockSpec(memory_space=pl.ANY),
         out_shape=jax.ShapeDtypeStruct((tokens, width), BF16),
-        compiler_params=room(8),
+        scratch_shapes=[pltpu.VMEM((tokens, width), BF16), pltpu.SemaphoreType.DMA((parts,))],
+        compiler_params=room(6),
         name="scaled",
     )(squares, value)
 
@@ -689,13 +697,16 @@
         pieces = [lax.all_gather(own, "seq", axis=0, tiled=True)]
     whiches = []
     for chunk in range(chunks):
-        order = [1 - (me & 1), me & 1] if planes else range(kv_chunk)
-        for kv_head in order:
+        turns = [1 - (me & 1), me & 1] if planes else range(kv_chunk)
+        for kv_head in turns:
             kv_head = jnp.asarray(kv_head, jnp.int32)
             at = [chunk * kv_chunk + kv_head, chunk * 2 * kv_chunk + kv_head]
             whiches.append(jnp.stack(at))
+    order = jnp.stack([which[0] for which in whiches])
     info = own_info(log_decay, seg_row, shards)
-    info, whiches, place, listing, seg_col = after((info, whiches, place, listing, seg_col), own)
+    info, whiches, order, place, listing, seg_col = after(
+        (info, whiches, order, place, listing, seg_col), own
+    )
     known = lax.all_to_all(info, "seq", 0, 0, tiled=True)
     passing = all_passing(known, heads, tokens)
     sizes = (1,) * 11 if planes else (shards,)
@@ -714,49 +725,44 @@
         second, below_beside, weights, faded_k, faded_q = after(
             (second, below_beside, weights, faded_k, faded_q)
         )
-        last = moved(second, cross(shards))
-        second_far, below_beside_far, last_far = (
-            moved(part, core(shards)) for part in (second, below_beside, last)
+        span = own.shape[1] // 2
+        lasts = [
+            moved(second[:, :span], cross(shards)),
+            moved(below_beside[:, span:], up(shards)),
+        ]
+        lasts = after(lasts)
+        second_far, below_beside_far = (
+            moved(part, core(shards)) for part in (second, below_beside)
         )
-        pieces = [below, second, beside, below_beside, last, own_far, below_far, second_far]
-        pieces += [beside_far, below_beside_far, last_far]
-
-    attended = None
-
-    def attend(chunk, turn, attended):
+        last_fars = [moved(last, core(shards)) for last in lasts]
+        pieces = [below, second, beside, below_beside, lasts, own_far, below_far, second_far]
+        pieces += [beside_far, below_beside_far, last_fars]
+
+    def attend(turn, first=None):
+        which = whiches[turn] if first is None else after(whiches[turn], first)
+        chunk = turn // kv_chunk
+        mine = [p[chunk] if isinstance(p, list) else p for p in pieces]
+        shifts = [chunk * 2 * kv_chunk if isinstance(p, list) else 0 for p in pieces]
         return attend_part(
-            whiches[chunk * kv_chunk + turn],
-            table,
-            biases,
-            sparse_query,
-            own,
-            faded_k,
-            pieces,
-            sizes,
-            kv_chunk,
-            attended,
+            which, table, biases, sparse_query, own, faded_k, mine, sizes, shifts, kv_chunk
         )
 
     if planes:
-        attended, send0 = attend(0, 0, attended)
-        attended, keep0 = attend(0, 1, attended)
+        part0, send0 = attend(0)
+        part1, keep0 = attend(1, part0)
         carry0 = carried_in_planes(keep0, send0, passing, place, shards, 0, heads)
-        attended = after(attended, next(carry0))
-        attended, send1 = attend(1, 0, attended)
-        attended = after(attended, next(carry0))
-        attended, keep1 = attend(1, 1, attended)
-        inside = inside_part(weights, attended, group)
+        part2, send1 = attend(2, next(carry0))
+        next(carry0)
+        part3, keep1 = attend(3, part2)
+        inside, attended = inside_part(order, weights, [part0, part1, part2, part3])
         carry1 = carried_in_planes(keep1, send1, passing, place, shards, head_chunk, heads)
         next(carry1)
         next(carry1)
         states = [carry0.send(inside), carry1.send(None)]
     else:
-        parts = []
-        for kv_head in range(kv_heads):
-            attended, state = attend(0, kv_head, attended)
-            parts.append(state)
-        inside = inside_part(weights, attended, group)
-        entering = carried_in_any(jnp.concatenate(parts), passing[:, :heads], me, shards)
+        parts, found = zip(*[attend(turn) for turn in range(kv_heads)], strict=True)
+        inside, attended = inside_part(order, weights, parts)
+        entering = carried_in_any(jnp.concatenate(found), passing[:, :heads], me, shards)
         entering = entering * passing[me, heads].astype(BF16)
         states = [(entering, entering)]
     result, squares = output_part(place, inside, faded_q, states, group, planes)
@@ -764,7 +770,7 @@
         squares = squares + lax.ppermute(squares, "head", [(0, 1), (1, 0)])
     else:
         squares = lax.psum(squares, "head")
-    return (attended, scale_part(squares, result, group))
+    return (attended, scale_part(squares, result, 8))
 
 
 def solution(mesh):

time: 122 us -> 106 us (0.87)
  waiting for transfers between devices: 43.4 us -> 22.4 us
  starting transfers between devices: 22.2 us -> 33.3 us
  Pallas kernels: 39.5 us -> 34.5 us
  local copies, waits for them, and re-layouts: 2.96 us -> 1.41 us
    ppermute x23 -> x25, waiting for transfers between devices: 41.3 us -> 20.4 us  [moved(): return lax.ppermute(value, 'seq', pairs)]
    ppermute x23 -> x25, starting transfers between devices: 20.6 us -> 31.7 us  [moved(): return lax.ppermute(value, 'seq', pairs)]
    pallas_call x7, Pallas kernels: 22.5 us -> 17.3 us  [the longest x4 10.9 us: attend_part(): pl.pallas_call(functools.partial(attend_kernel, sizes, shifts, kv_step, g...]
    unnamed x8, local copies, waits for them, and re-layouts: 1.6 us -> 0.02 us
  transfers between devices with their start and end apart: 24 -> 26, of which waited for: 12 -> 10; matrix products, arithmetic and copies ran while one was open for 0% -> 0% of each run, Pallas kernels for 21% -> 25%
where the time goes in v3:
time: 106 us
  Pallas kernels  34.5 us (33%)
  starting transfers between devices  33.3 us (31%)
  waiting for transfers between devices  22.4 us (21%)
  blocking collectives  13.1 us (12%)
  local copies, waits for them, and re-layouts  1.41 us (1%)
  between operations  1.06 us (1%)
    ppermute x25, starting transfers between devices, moved(): return lax.ppermute(value, 'seq', pairs)  31.7 us
    ppermute x25, waiting for transfers between devices, moved(): return lax.ppermute(value, 'seq', pairs)  20.4 us
    all_to_all x1, blocking collectives, body(): known = lax.all_to_all(info, 'seq', 0, 0, tiled=True)  13.1 us
    pallas_call x4, Pallas kernels, attend_part(): pl.pallas_call(functools.partial(attend_kernel, sizes, shifts, kv_step, g...  10.9 us
    pallas_call x1, Pallas kernels, local_part(): pl.pallas_call(local_kernel, grid=(steps,), in_specs=[wide, wide, pl.Bloc...  9.08 us
    pallas_call x8, Pallas kernels, mixing(): pl.pallas_call(functools.partial(mixing_kernel, body), in_specs=[smem, sm...  6.17 us
    pallas_call x1, Pallas kernels, inside_part(): pl.pallas_call(functools.partial(inside_kernel, len(parts)), in_specs=[pl...  3.26 us
  transfers between devices with their start and end apart: 26, of which 10 were waited for; matrix products, arithmetic and copies ran while one was open for 0% of the time, Pallas kernels for 25%

profile of v3, /device:TPU:0, one launch (start us, length us, event | category | flops | bytes accessed | tf_op | source)
XLA Modules:
  0.0 106.0 jit_solution(5160579520157563631)
XLA Ops:
  1.9 3.1 %collective-permute-start = (bf16[256,1024]{1,0:T(8,128)(2,1)S(1)}, bf16[256,1024]{1,0:T(8,128)(2,1)S(1)}, u32[]{:S(2)}, u32[]{:S(2)}) collective-permute-start(bf16[256,1024]{1,0:T(8,128)(2,1)S(1)} %pad_maximum_fusion.refs_1_), channel_id=1, source_target_pairs={{0,8},{2,10},{4,12},{6,14},{8,16},{10,18},{12,20},{14,22},{16,24},... | collective-permute-start | bytes 1572872 | tf_op jit(solution)/shard_map/ppermute | solution.py:531
  5.0 1.5 %collective-permute-start.1 = (bf16[256,1024]{1,0:T(8,128)(2,1)S(1)}, bf16[256,1024]{1,0:T(8,128)(2,1)S(1)}, u32[]{:S(2)}, u32[]{:S(2)}) collective-permute-start(bf16[256,1024]{1,0:T(8,128)(2,1)S(1)} %pad_maximum_fusion.refs_1_), channel_id=1, source_target_pairs={{0,4},{2,6},{4,0},{6,2},{8,12},{10,14},{12,8},{14,10},{16,20},{18,... | collective-permute-start | bytes 1572872 | tf_op jit(solution)/shard_map/ppermute | solution.py:531
  6.9 13.1 %all_to_all.11 = f32[16,1,128]{2,1,0:T(1,128)S(1)} all-to-all(f32[16,1,128]{2,1,0:T(1,128)S(1)} %bitcast.15), channel_id=1, replica_groups=mesh['seq'=16,'head'=2] {'seq'}, dimensions={0} | all-to-all | bytes 16384 | tf_op jit(solution)/shard_map/all_to_all | solution.py:710
  21.7 1.6 %seen_table.1 = (f32[2,128,128]{2,1,0:T(8,128)S(1)}, f32[2,128,128]{2,1,0:T(8,128)S(1)}, f32[26,8,128]{2,1,0:T(8,128)S(1)}, s32[35]{0:T(128)S(1)}) custom-call(s32[24]{0:T(128)S(1)} %reshape.13.listing, f32[16,128]{1,0:T(8,128)S(1)} %bitcast.13, s32[1]{0:T(128)} %bitcast.7.place_ref, s32[256,1]{1,0:T(8,128)S(1)} %copy.14.segc_ref, s32[1,256]{1,0:T(1,128)S(1)} %bitcast.18), custom_call_target="tpu_custom_call" | custom-call | tf_op jit(solution)/shard_map/seen_table/pallas_call | solution.py:238
  23.3 9.1 %local_scores.1 = (bf16[32,256,256]{2,1,0:T(8,128)(2,1)S(1)}, bf16[32,128,256]{2,1,0:T(8,128)(2,1)S(1)}, bf16[256,4096]{1,0:T(8,128)(2,1)S(1)}) custom-call(bf16[256,4096]{1,0:T(8,128)(2,1)} %q_ref, bf16[256,4096]{1,0:T(8,128)(2,1)} %k_ref, f32[32,256]{1,0:T(8,128)S(1)} %copy-done.1, s32[256,1]{1,0:T(8,128)S(1)} %copy.14.segc_ref, s32[1,256]{1,0:T(1,128)S(1)} %bitcast.19), custom_call_target="tpu_custom_call" | custom-call | flops 536870912 | bytes 12582912 | tf_op jit(solution)/shard_map/local_scores/pallas_call | solution.py:135
  32.4 3.0 %collective-permute-done.2.refs_7_ = bf16[256,1024]{1,0:T(8,128)(2,1)S(1)} collective-permute-done((bf16[256,1024]{1,0:T(8,128)(2,1)S(1)}, bf16[256,1024]{1,0:T(8,128)(2,1)S(1)}, u32[]{:S(2)}, u32[]{:S(2)}) %collective-permute-start.2) | collective-permute-done | bytes 524320 | tf_op jit(solution)/shard_map/ppermute | solution.py:531
  37.4 5.3 %collective-permute-done.4.refs_10_ = bf16[256,512]{1,0:T(8,128)(2,1)S(1)} collective-permute-done((bf16[256,512]{1,0:T(8,128)(2,1)S(1)}, bf16[256,512]{1,0:T(8,128)(2,1)S(1)}, u32[]{:S(2)}, u32[]{:S(2)}) %collective-permute-start.4) | collective-permute-done | bytes 262176 | tf_op jit(solution)/shard_map/ppermute | solution.py:531
  42.6 2.7 %collective-permute-done.5.refs_10_ = bf16[256,512]{1,0:T(8,128)(2,1)S(1)} collective-permute-done((bf16[256,512]{1,0:T(8,128)(2,1)S(1)}, bf16[256,512]{1,0:T(8,128)(2,1)S(1)}, u32[]{:S(2)}, u32[]{:S(2)}) %collective-permute-start.5) | collective-permute-done | bytes 262176 | tf_op jit(solution)/shard_map/ppermute | solution.py:531
  47.6 2.6 %attend.4 = (bf16[256,1024]{1,0:T(8,128)(2,1)S(1)}, f32[8,128,128]{2,1,0:T(8,128)S(1)}) custom-call(s32[2]{0:T(128)S(1)} %get-tuple-element.70.kv_head, s32[35]{0:T(128)S(1)} %get-tuple-element.63.table, bf16[256,4096]{1,0:T(8,128)(2,1)S(1)} %copy-done, bf16[256,1024]{1,0:T(8,128)(2,1)S(1)} %pad_maximum_fusion.refs_1_, ...), custom_call_target="tpu_custom_call" | custom-call | flops 1006632960 | bytes 1572864 | tf_op jit(solution)/shard_map/attend/pallas_call | solution.py:377
  51.0 2.8 %attend.5 = (bf16[256,1024]{1,0:T(8,128)(2,1)S(1)}, f32[8,128,128]{2,1,0:T(8,128)S(1)}) custom-call(s32[2]{0:T(128)S(1)} %get-tuple-element.81.kv_head, s32[35]{0:T(128)S(1)} %get-tuple-element.63.table, bf16[256,4096]{1,0:T(8,128)(2,1)S(1)} %copy-done, bf16[256,1024]{1,0:T(8,128)(2,1)S(1)} %pad_maximum_fusion.refs_1_, ...), custom_call_target="tpu_custom_call" | custom-call | flops 1006632960 | bytes 1572864 | tf_op jit(solution)/shard_map/attend/pallas_call | solution.py:377
  54.5 2.6 %attend.6 = (bf16[256,1024]{1,0:T(8,128)(2,1)S(1)}, f32[8,128,128]{2,1,0:T(8,128)S(1)}) custom-call(s32[2]{0:T(128)S(1)} %get-tuple-element.87.kv_head, s32[35]{0:T(128)S(1)} %get-tuple-element.63.table, bf16[256,4096]{1,0:T(8,128)(2,1)S(1)} %copy-done, bf16[256,1024]{1,0:T(8,128)(2,1)S(1)} %pad_maximum_fusion.refs_1_, ...), custom_call_target="tpu_custom_call" | custom-call | flops 1006632960 | bytes 1572864 | tf_op jit(solution)/shard_map/attend/pallas_call | solution.py:377
  58.3 4.9 %collective-permute-start.14 = (bf16[4,128,128]{2,1,0:T(8,128)(2,1)S(1)}, bf16[4,128,128]{2,1,0:T(8,128)(2,1)S(1)}, u32[]{:S(2)}, u32[]{:S(2)}) collective-permute-start(bf16[4,128,128]{2,1,0:T(8,128)(2,1)S(1)} %get-tuple-element.86), channel_id=1, source_target_pairs={{0,4},{2,6},{4,0},{6,2},{8,12},{10,14},{12,8},{14,10},{16,20},{18,... | collective-permute-start | bytes 393224 | tf_op jit(solution)/shard_map/ppermute | solution.py:531
  63.2 2.8 %attend.7 = (bf16[256,1024]{1,0:T(8,128)(2,1)S(1)}, f32[8,128,128]{2,1,0:T(8,128)S(1)}) custom-call(s32[2]{0:T(128)S(1)} %get-tuple-element.91.kv_head, s32[35]{0:T(128)S(1)} %get-tuple-element.63.table, bf16[256,4096]{1,0:T(8,128)(2,1)S(1)} %copy-done, bf16[256,1024]{1,0:T(8,128)(2,1)S(1)} %pad_maximum_fusion.refs_1_, ...), custom_call_target="tpu_custom_call" | custom-call | flops 1006632960 | bytes 1572864 | tf_op jit(solution)/shard_map/attend/pallas_call | solution.py:377
  68.4 5.6 %collective-permute-start.15 = (bf16[4,128,128]{2,1,0:T(8,128)(2,1)S(1)}, bf16[4,128,128]{2,1,0:T(8,128)(2,1)S(1)}, u32[]{:S(2)}, u32[]{:S(2)}) collective-permute-start(bf16[4,128,128]{2,1,0:T(8,128)(2,1)S(1)} %mix_plane.2), channel_id=1, source_target_pairs={{0,8},{2,10},{4,12},{6,14},{8,16},{10,18},{12,20},{14,22},{16,24},... | collective-permute-start | bytes 393224 | tf_op jit(solution)/shard_map/ppermute | solution.py:531
  74.7 4.5 %collective-permute-start.20 = (bf16[4,128,128]{2,1,0:T(8,128)(2,1)S(1)}, bf16[4,128,128]{2,1,0:T(8,128)(2,1)S(1)}, u32[]{:S(2)}, u32[]{:S(2)}) collective-permute-start(bf16[4,128,128]{2,1,0:T(8,128)(2,1)S(1)} %mix_plane.3), channel_id=1, source_target_pairs={{0,8},{2,10},{4,12},{6,14},{8,16},{10,18},{12,20},{14,22},{16,24},... | collective-permute-start | bytes 393224 | tf_op jit(solution)/shard_map/ppermute | solution.py:531
  80.0 3.1 %collective-permute-done.20.refs_2_ = bf16[4,128,128]{2,1,0:T(8,128)(2,1)S(1)} collective-permute-done((bf16[4,128,128]{2,1,0:T(8,128)(2,1)S(1)}, bf16[4,128,128]{2,1,0:T(8,128)(2,1)S(1)}, u32[]{:S(2)}, u32[]{:S(2)}) %collective-permute-start.20) | collective-permute-done | bytes 131104 | tf_op jit(solution)/shard_map/ppermute | solution.py:531
  83.1 2.5 %collective-permute-start.21 = (bf16[4,128,128]{2,1,0:T(8,128)(2,1)S(1)}, bf16[4,128,128]{2,1,0:T(8,128)(2,1)S(1)}, u32[]{:S(2)}, u32[]{:S(2)}) collective-permute-start(bf16[4,128,128]{2,1,0:T(8,128)(2,1)S(1)} %collective-permute-done.20.refs_2_), channel_id=1, source_target_pairs={{0,8},{2,10},{4,12},{6,14},{8,16},{10,18},{12,20},{14,22},{16,24},... | collective-permute-start | bytes 393224 | tf_op jit(solution)/shard_map/ppermute | solution.py:531
  85.5 3.3 %inside.1 = (f32[256,4096]{1,0:T(8,128)S(1)}, bf16[256,4096]{1,0:T(8,128)(2,1)}) custom-call(s32[4]{0:T(128)S(1)} %pad_add_fusion.4.order, bf16[32,256,256]{2,1,0:T(8,128)(2,1)S(1)} %get-tuple-element.69.w_ref, bf16[256,1024]{1,0:T(8,128)(2,1)S(1)} %get-tuple-element.79.refs_0_, bf16[256,1024]{1,0:T(8,128)(2,1)S(1)} %get-tuple-element.82.refs_1_, ...), custom_call_target="tpu_custom_call" | custom-call | flops 536870912 | bytes 10485760 | tf_op jit(solution)/shard_map/inside/pallas_call | solution.py:427
  92.6 2.1 %collective-permute-done.17.refs_3_ = bf16[4,128,128]{2,1,0:T(8,128)(2,1)S(1)} collective-permute-done((bf16[4,128,128]{2,1,0:T(8,128)(2,1)S(1)}, bf16[4,128,128]{2,1,0:T(8,128)(2,1)S(1)}, u32[]{:S(2)}, u32[]{:S(2)}) %collective-permute-start.17) | collective-permute-done | bytes 131104 | tf_op jit(solution)/shard_map/ppermute | solution.py:531
  97.5 1.5 %collective-permute-done.24.refs_3_ = bf16[8,128,128]{2,1,0:T(8,128)(2,1)S(1)} collective-permute-done((bf16[8,128,128]{2,1,0:T(8,128)(2,1)S(1)}, bf16[8,128,128]{2,1,0:T(8,128)(2,1)S(1)}, u32[]{:S(2)}, u32[]{:S(2)}) %collective-permute-start.24) | collective-permute-done | bytes 262176 | tf_op jit(solution)/shard_map/ppermute | solution.py:531
  99.0 1.5 %outputs.1 = (f32[256,4096]{1,0:T(8,128)S(1)}, f32[1,256]{1,0:T(1,128)S(1)}) custom-call(s32[1]{0:T(128)} %bitcast.7.place_ref, bf16[256,4096]{1,0:T(8,128)(2,1)S(1)} %get-tuple-element.94.q_ref, f32[256,4096]{1,0:T(8,128)S(1)} %get-tuple-element.95.inside_ref, bf16[8,128,128]{2,1,0:T(8,128)(2,1)S(1)} %get-tuple-element.100.refs_0_, ...), custom_call_target="tpu_custom_call", output_to_operand_aliasing={{0}: (2, {})} | custom-call | flops 268435456 | bytes 11534336 | tf_op jit(solution)/shard_map/outputs/pallas_call | solution.py:477
  100.5 1.6 %collective-permute-start.25 = (f32[1,256]{1,0:T(1,128)S(1)}, f32[1,256]{1,0:T(1,128)S(1)}, u32[]{:S(2)}, u32[]{:S(2)}) collective-permute-start(f32[1,256]{1,0:T(1,128)S(1)} %get-tuple-element.110), channel_id=1, source_target_pairs={{0,1},{1,0},{2,3},{3,2},{4,5},{5,4},{6,7},{7,6},{8,9},{9,8},{10,11... | collective-permute-start | bytes 3080 | tf_op jit(solution)/shard_map/ppermute | solution.py:770
  102.1 2.0 %collective-permute-done.25 = f32[1,256]{1,0:T(1,128)S(1)} collective-permute-done((f32[1,256]{1,0:T(1,128)S(1)}, f32[1,256]{1,0:T(1,128)S(1)}, u32[]{:S(2)}, u32[]{:S(2)}) %collective-permute-start.25) | collective-permute-done | bytes 1056 | tf_op jit(solution)/shard_map/ppermute | solution.py:770
  104.1 1.7 %scaled.1 = bf16[256,4096]{1,0:T(8,128)(2,1)} custom-call(f32[1,256]{1,0:T(1,128)S(1)} %add.21.squares_ref, f32[256,4096]{1,0:T(8,128)S(1)} %get-tuple-element.111.value_ref), custom_call_target="tpu_custom_call" | custom-call | tf_op jit(solution)/shard_map/scaled/pallas_call | solution.py:519
  (66 shorter events, 20.7 us)
Async XLA Ops:
  1.9 18.1 %collective-permute-start = (bf16[256,1024]{1,0:T(8,128)(2,1)S(1)}, bf16[256,1024]{1,0:T(8,128)(2,1)S(1)}, u32[]{:S(2)}, u32[]{:S(2)}) collective-permute-start(bf16[256,1024]{1,0:T(8,128)(2,1)S(1)} %pad_maximum_fusion.refs_1_), channel_id=1, source_target_pairs={{0,8},{2,10},{4,12},{6,14},{8,16},{10,18},{12,20},{14,22},{16,24},... | collective-permute-start | bytes 1572872 | tf_op jit(solution)/shard_map/ppermute | solution.py:531
  5.0 15.0 %collective-permute-start.1 = (bf16[256,1024]{1,0:T(8,128)(2,1)S(1)}, bf16[256,1024]{1,0:T(8,128)(2,1)S(1)}, u32[]{:S(2)}, u32[]{:S(2)}) collective-permute-start(bf16[256,1024]{1,0:T(8,128)(2,1)S(1)} %pad_maximum_fusion.refs_1_), channel_id=1, source_target_pairs={{0,4},{2,6},{4,0},{6,2},{8,12},{10,14},{12,8},{14,10},{16,20},{18,... | collective-permute-start | bytes 1572872 | tf_op jit(solution)/shard_map/ppermute | solution.py:531
  20.0 15.4 %collective-permute-start.2 = (bf16[256,1024]{1,0:T(8,128)(2,1)S(1)}, bf16[256,1024]{1,0:T(8,128)(2,1)S(1)}, u32[]{:S(2)}, u32[]{:S(2)}) collective-permute-start(bf16[256,1024]{1,0:T(8,128)(2,1)S(1)} %collective-permute-done.refs_6_), channel_id=1, source_target_pairs={{0,8},{2,10},{4,12},{6,14},{8,16},{10,18},{12,20},{14,22},{16,24},... | collective-permute-start | bytes 1572872 | tf_op jit(solution)/shard_map/ppermute | solution.py:531
  20.5 14.9 %collective-permute-start.3 = (bf16[256,1024]{1,0:T(8,128)(2,1)S(1)}, bf16[256,1024]{1,0:T(8,128)(2,1)S(1)}, u32[]{:S(2)}, u32[]{:S(2)}) collective-permute-start(bf16[256,1024]{1,0:T(8,128)(2,1)S(1)} %collective-permute-done.refs_6_), channel_id=1, source_target_pairs={{0,4},{2,6},{4,0},{6,2},{8,12},{10,14},{12,8},{14,10},{16,20},{18,... | collective-permute-start | bytes 1572872 | tf_op jit(solution)/shard_map/ppermute | solution.py:531
  21.6 23.8 %collective-permute-start.6 = (bf16[256,1024]{1,0:T(8,128)(2,1)S(1)}, bf16[256,1024]{1,0:T(8,128)(2,1)S(1)}, u32[]{:S(2)}, u32[]{:S(2)}) collective-permute-start(bf16[256,1024]{1,0:T(8,128)(2,1)S(1)} %pad_maximum_fusion.refs_1_), channel_id=1, source_target_pairs={{0,2},{2,0},{4,6},{6,4},{8,10},{10,8},{12,14},{14,12},{16,18},{18,... | collective-permute-start | bytes 1572872 | tf_op jit(solution)/shard_map/ppermute | solution.py:531
  35.4 7.2 %collective-permute-start.4 = (bf16[256,512]{1,0:T(8,128)(2,1)S(1)}, bf16[256,512]{1,0:T(8,128)(2,1)S(1)}, u32[]{:S(2)}, u32[]{:S(2)}) collective-permute-start(bf16[256,512]{1,0:T(8,128)(2,1)S(1)} %slice.22), channel_id=1, source_target_pairs={{0,4},{2,6},{4,0},{6,2},{8,12},{10,14},{12,8},{14,10},{16,20},{18,... | collective-permute-start | bytes 786440 | tf_op jit(solution)/shard_map/ppermute | solution.py:531
  36.4 9.0 %collective-permute-start.5 = (bf16[256,512]{1,0:T(8,128)(2,1)S(1)}, bf16[256,512]{1,0:T(8,128)(2,1)S(1)}, u32[]{:S(2)}, u32[]{:S(2)}) collective-permute-start(bf16[256,512]{1,0:T(8,128)(2,1)S(1)} %slice.23), channel_id=1, source_target_pairs={{0,8},{2,10},{4,12},{6,14},{8,16},{10,18},{12,20},{14,22},{16,24},... | collective-permute-start | bytes 786440 | tf_op jit(solution)/shard_map/ppermute | solution.py:531
  36.9 9.0 %collective-permute-start.7 = (bf16[256,1024]{1,0:T(8,128)(2,1)S(1)}, bf16[256,1024]{1,0:T(8,128)(2,1)S(1)}, u32[]{:S(2)}, u32[]{:S(2)}) collective-permute-start(bf16[256,1024]{1,0:T(8,128)(2,1)S(1)} %collective-permute-done.refs_6_), channel_id=1, source_target_pairs={{0,2},{2,0},{4,6},{6,4},{8,10},{10,8},{12,14},{14,12},{16,18},{18,... | collective-permute-start | bytes 1572872 | tf_op jit(solution)/shard_map/ppermute | solution.py:531
  36.9 9.0 %collective-permute-start.9 = (bf16[256,1024]{1,0:T(8,128)(2,1)S(1)}, bf16[256,1024]{1,0:T(8,128)(2,1)S(1)}, u32[]{:S(2)}, u32[]{:S(2)}) collective-permute-start(bf16[256,1024]{1,0:T(8,128)(2,1)S(1)} %collective-permute-done.1.refs_8_), channel_id=1, source_target_pairs={{0,2},{2,0},{4,6},{6,4},{8,10},{10,8},{12,14},{14,12},{16,18},{18,... | collective-permute-start | bytes 1572872 | tf_op jit(solution)/shard_map/ppermute | solution.py:531
  42.6 3.2 %collective-permute-start.8 = (bf16[256,1024]{1,0:T(8,128)(2,1)S(1)}, bf16[256,1024]{1,0:T(8,128)(2,1)S(1)}, u32[]{:S(2)}, u32[]{:S(2)}) collective-permute-start(bf16[256,1024]{1,0:T(8,128)(2,1)S(1)} %collective-permute-done.2.refs_7_), channel_id=1, source_target_pairs={{0,2},{2,0},{4,6},{6,4},{8,10},{10,8},{12,14},{14,12},{16,18},{18,... | collective-permute-start | bytes 1572872 | tf_op jit(solution)/shard_map/ppermute | solution.py:531
  45.3 2.3 %collective-permute-start.11 = (bf16[256,512]{1,0:T(8,128)(2,1)S(1)}, bf16[256,512]{1,0:T(8,128)(2,1)S(1)}, u32[]{:S(2)}, u32[]{:S(2)}) collective-permute-start(bf16[256,512]{1,0:T(8,128)(2,1)S(1)} %collective-permute-done.4.refs_10_), channel_id=1, source_target_pairs={{0,2},{2,0},{4,6},{6,4},{8,10},{10,8},{12,14},{14,12},{16,18},{18,... | collective-permute-start | bytes 786440 | tf_op jit(solution)/shard_map/ppermute | solution.py:531
  50.2 3.6 %collective-permute-start.12 = (f32[8,128,128]{2,1,0:T(8,128)S(1)}, f32[8,128,128]{2,1,0:T(8,128)S(1)}, u32[]{:S(2)}, u32[]{:S(2)}) collective-permute-start(f32[8,128,128]{2,1,0:T(8,128)S(1)} %get-tuple-element.85), channel_id=1, source_target_pairs={{0,2},{2,0},{4,6},{6,4},{8,10},{10,8},{12,14},{14,12},{16,18},{18,... | collective-permute-start | bytes 1572872 | tf_op jit(solution)/shard_map/ppermute | solution.py:531
  50.7 3.8 %collective-permute-start.13 = (bf16[256,512]{1,0:T(8,128)(2,1)S(1)}, bf16[256,512]{1,0:T(8,128)(2,1)S(1)}, u32[]{:S(2)}, u32[]{:S(2)}) collective-permute-start(bf16[256,512]{1,0:T(8,128)(2,1)S(1)} %collective-permute-done.5.refs_10_), channel_id=1, source_target_pairs={{0,2},{2,0},{4,6},{6,4},{8,10},{10,8},{12,14},{14,12},{16,18},{18,... | collective-permute-start | bytes 786440 | tf_op jit(solution)/shard_map/ppermute | solution.py:531
  57.2 8.8 %collective-permute-start.18 = (f32[8,128,128]{2,1,0:T(8,128)S(1)}, f32[8,128,128]{2,1,0:T(8,128)S(1)}, u32[]{:S(2)}, u32[]{:S(2)}) collective-permute-start(f32[8,128,128]{2,1,0:T(8,128)S(1)} %get-tuple-element.102), channel_id=1, source_target_pairs={{0,2},{2,0},{4,6},{6,4},{8,10},{10,8},{12,14},{14,12},{16,18},{18,... | collective-permute-start | bytes 1572872 | tf_op jit(solution)/shard_map/ppermute | solution.py:531
  58.3 9.4 %collective-permute-start.14 = (bf16[4,128,128]{2,1,0:T(8,128)(2,1)S(1)}, bf16[4,128,128]{2,1,0:T(8,128)(2,1)S(1)}, u32[]{:S(2)}, u32[]{:S(2)}) collective-permute-start(bf16[4,128,128]{2,1,0:T(8,128)(2,1)S(1)} %get-tuple-element.86), channel_id=1, source_target_pairs={{0,4},{2,6},{4,0},{6,2},{8,12},{10,14},{12,8},{14,10},{16,20},{18,... | collective-permute-start | bytes 393224 | tf_op jit(solution)/shard_map/ppermute | solution.py:531
  66.8 7.2 %collective-permute-start.19 = (bf16[4,128,128]{2,1,0:T(8,128)(2,1)S(1)}, bf16[4,128,128]{2,1,0:T(8,128)(2,1)S(1)}, u32[]{:S(2)}, u32[]{:S(2)}) collective-permute-start(bf16[4,128,128]{2,1,0:T(8,128)(2,1)S(1)} %get-tuple-element.104), channel_id=1, source_target_pairs={{0,4},{2,6},{4,0},{6,2},{8,12},{10,14},{12,8},{14,10},{16,20},{18,... | collective-permute-start | bytes 393224 | tf_op jit(solution)/shard_map/ppermute | solution.py:531
  68.4 10.8 %collective-permute-start.15 = (bf16[4,128,128]{2,1,0:T(8,128)(2,1)S(1)}, bf16[4,128,128]{2,1,0:T(8,128)(2,1)S(1)}, u32[]{:S(2)}, u32[]{:S(2)}) collective-permute-start(bf16[4,128,128]{2,1,0:T(8,128)(2,1)S(1)} %mix_plane.2), channel_id=1, source_target_pairs={{0,8},{2,10},{4,12},{6,14},{8,16},{10,18},{12,20},{14,22},{16,24},... | collective-permute-start | bytes 393224 | tf_op jit(solution)/shard_map/ppermute | solution.py:531
  74.7 8.3 %collective-permute-start.20 = (bf16[4,128,128]{2,1,0:T(8,128)(2,1)S(1)}, bf16[4,128,128]{2,1,0:T(8,128)(2,1)S(1)}, u32[]{:S(2)}, u32[]{:S(2)}) collective-permute-start(bf16[4,128,128]{2,1,0:T(8,128)(2,1)S(1)} %mix_plane.3), channel_id=1, source_target_pairs={{0,8},{2,10},{4,12},{6,14},{8,16},{10,18},{12,20},{14,22},{16,24},... | collective-permute-start | bytes 393224 | tf_op jit(solution)/shard_map/ppermute | solution.py:531
  79.2 9.7 %collective-permute-start.16 = (bf16[4,128,128]{2,1,0:T(8,128)(2,1)S(1)}, bf16[4,128,128]{2,1,0:T(8,128)(2,1)S(1)}, u32[]{:S(2)}, u32[]{:S(2)}) collective-permute-start(bf16[4,128,128]{2,1,0:T(8,128)(2,1)S(1)} %collective-permute-done.15.refs_2_), channel_id=1, source_target_pairs={{0,8},{2,10},{4,12},{6,14},{8,16},{10,18},{12,20},{14,22},{16,24},... | collective-permute-start | bytes 393224 | tf_op jit(solution)/shard_map/ppermute | solution.py:531
  83.1 7.7 %collective-permute-start.21 = (bf16[4,128,128]{2,1,0:T(8,128)(2,1)S(1)}, bf16[4,128,128]{2,1,0:T(8,128)(2,1)S(1)}, u32[]{:S(2)}, u32[]{:S(2)}) collective-permute-start(bf16[4,128,128]{2,1,0:T(8,128)(2,1)S(1)} %collective-permute-done.20.refs_2_), channel_id=1, source_target_pairs={{0,8},{2,10},{4,12},{6,14},{8,16},{10,18},{12,20},{14,22},{16,24},... | collective-permute-start | bytes 393224 | tf_op jit(solution)/shard_map/ppermute | solution.py:531
  89.6 5.0 %collective-permute-start.17 = (bf16[4,128,128]{2,1,0:T(8,128)(2,1)S(1)}, bf16[4,128,128]{2,1,0:T(8,128)(2,1)S(1)}, u32[]{:S(2)}, u32[]{:S(2)}) collective-permute-start(bf16[4,128,128]{2,1,0:T(8,128)(2,1)S(1)} %get-tuple-element.99), channel_id=1, source_target_pairs={{0,4},{2,6},{4,0},{6,2},{8,12},{10,14},{12,8},{14,10},{16,20},{18,... | collective-permute-start | bytes 393224 | tf_op jit(solution)/shard_map/ppermute | solution.py:531
  91.5 5.0 %collective-permute-start.22 = (bf16[4,128,128]{2,1,0:T(8,128)(2,1)S(1)}, bf16[4,128,128]{2,1,0:T(8,128)(2,1)S(1)}, u32[]{:S(2)}, u32[]{:S(2)}) collective-permute-start(bf16[4,128,128]{2,1,0:T(8,128)(2,1)S(1)} %get-tuple-element.106), channel_id=1, source_target_pairs={{0,4},{2,6},{4,0},{6,2},{8,12},{10,14},{12,8},{14,10},{16,20},{18,... | collective-permute-start | bytes 393224 | tf_op jit(solution)/shard_map/ppermute | solution.py:531
  95.5 2.0 %collective-permute-start.23 = (bf16[8,128,128]{2,1,0:T(8,128)(2,1)S(1)}, bf16[8,128,128]{2,1,0:T(8,128)(2,1)S(1)}, u32[]{:S(2)}, u32[]{:S(2)}) collective-permute-start(bf16[8,128,128]{2,1,0:T(8,128)(2,1)S(1)} %get-tuple-element.108), channel_id=1, source_target_pairs={{0,2},{2,0},{4,6},{6,4},{8,10},{10,8},{12,14},{14,12},{16,18},{18,... | collective-permute-start | bytes 786440 | tf_op jit(solution)/shard_map/ppermute | solution.py:531
  100.5 3.6 %collective-permute-start.25 = (f32[1,256]{1,0:T(1,128)S(1)}, f32[1,256]{1,0:T(1,128)S(1)}, u32[]{:S(2)}, u32[]{:S(2)}) collective-permute-start(f32[1,256]{1,0:T(1,128)S(1)} %get-tuple-element.110), channel_id=1, source_target_pairs={{0,1},{1,0},{2,3},{3,2},{4,5},{5,4},{6,7},{7,6},{8,9},{9,8},{10,11... | collective-permute-start | bytes 3080 | tf_op jit(solution)/shard_map/ppermute | solution.py:770
  (6 other events, 45.4 us)

commit v4 on v3

--- a/solution.py
+++ b/solution.py
@@ -391,8 +391,8 @@
         ],
         compiler_params=room(12),
         cost_estimate=pl.CostEstimate(
-            flops=group * 10 * 6 * BLK * BLK * HD,
-            bytes_accessed=12 * 4 * query.shape[0] * HD,
+            flops=group * 10 * 6 * BLK * BLK * HD * 10,
+            bytes_accessed=12 * 4 * query.shape[0] * HD * 10,
             transcendentals=group * 10 * BLK * BLK,
         ),
         name="attend",
@@ -637,15 +637,16 @@
         "mix_chip", chip_body, passing, place, [keep, sent], [(quarter, F32), (quarter, BF16)]
     )
     far_q = moved(send_q, cross(shards))
-    yield send_q
+    wait = yield send_q
+    near_q = near_q if wait is None else after(near_q, wait)
     (plane_state,) = mixing(
         "mix_plane", plane_body, passing, place, [near_q, far_q], [(quarter, BF16)]
     )
     one_below = moved(plane_state, up(shards))
-    wait = yield plane_state
-    if wait is not None:
-        near_q = after(near_q, wait)
+    yield plane_state, one_below
     two_below = moved(one_below, up(shards))
+    wait = yield two_below
+    near_q = near_q if wait is None else after(near_q, wait)
     near_e, send_e = mixing(
         "mix_enter",
         enter_body,
@@ -655,6 +656,7 @@
         [(quarter, F32), (quarter, BF16)],
     )
     got_e = moved(send_e, cross(shards))
+    yield got_e
     mine, other = mixing(
         "mix_core", core_body, passing, place, [keep, sent, near_e, got_e], [(half, BF16), (half, BF16)]
     )
@@ -692,7 +694,8 @@
     own = jnp.concatenate(parts, axis=1)
     seg_col, seg_row, listing = segments[:, None], segments[None, :], block_list.reshape(-1)
     if planes:
-        below, beside = moved(own, up(shards)), moved(own, cross(shards))
+        beside = moved(own, cross(shards))
+        below = moved(own, up(shards))
     else:
         pieces = [lax.all_gather(own, "seq", axis=0, tiled=True)]
     whiches = []
@@ -712,8 +715,9 @@
     sizes = (1,) * 11 if planes else (shards,)
     *biases, table = seen_table(place, listing, known, seg_col, seg_row, sizes, heads, planes)
     if planes:
-        below, beside = after((below, beside), known)
-        second, below_beside = moved(below, up(shards)), moved(below, cross(shards))
+        beside, below = after((beside, below), known)
+        below_beside = moved(below, cross(shards))
+        second = moved(below, up(shards))
         own_far, below_far, beside_far = (
             moved(part, core(shards)) for part in (own, below, beside)
         )
@@ -722,14 +726,12 @@
         light_query, light_key, log_decay, seg_col, seg_row, group
     )
     if planes:
-        second, below_beside, weights, faded_k, faded_q = after(
-            (second, below_beside, weights, faded_k, faded_q)
+        below_beside, second, weights, faded_k, faded_q = after(
+            (below_beside, second, weights, faded_k, faded_q)
         )
         span = own.shape[1] // 2
-        lasts = [
-            moved(second[:, :span], cross(shards)),
-            moved(below_beside[:, span:], up(shards)),
-        ]
+        lasts = [moved(below_beside[:, span:], up(shards))]
+        lasts.insert(0, moved(second[:, :span], cross(shards)))
         lasts = after(lasts)
         second_far, below_beside_far = (
             moved(part, core(shards)) for part in (second, below_beside)
@@ -752,13 +754,18 @@
         part1, keep0 = attend(1, part0)
         carry0 = carried_in_planes(keep0, send0, passing, place, shards, 0, heads)
         part2, send1 = attend(2, next(carry0))
+        plane0, one0 = next(carry0)
+        part3, keep1 = attend(3, (part2, plane0))
         next(carry0)
-        part3, keep1 = attend(3, part2)
+        keep1 = after(keep1, one0)
+        carry1 = carried_in_planes(keep1, send1, passing, place, shards, head_chunk, heads)
+        order = after(order, next(carry1))
         inside, attended = inside_part(order, weights, [part0, part1, part2, part3])
-        carry1 = carried_in_planes(keep1, send1, passing, place, shards, head_chunk, heads)
+        got0 = next(carry0)
+        carry1.send(inside)
         next(carry1)
-        next(carry1)
-        states = [carry0.send(inside), carry1.send(None)]
+        carry1.send(got0)
+        states = [next(carry0), next(carry1)]
     else:
         parts, found = zip(*[attend(turn) for turn in range(kv_heads)], strict=True)
         inside, attended = inside_part(order, weights, parts)

time: 106 us -> 109 us (1.028)
  waiting for transfers between devices: 22.4 us -> 39.4 us
  starting transfers between devices: 33.3 us -> 19 us
    ppermute x25, waiting for transfers between devices: 20.4 us -> 37.4 us  [moved(): return lax.ppermute(value, 'seq', pairs)]
    ppermute x25, starting transfers between devices: 31.7 us -> 17.4 us  [moved(): return lax.ppermute(value, 'seq', pairs)]
  transfers between devices with their start and end apart: 26 -> 26, of which waited for: 10 -> 15; matrix products, arithmetic and copies ran while one was open for 0% -> 0% of each run, Pallas kernels for 25% -> 27%
where the time goes in v4:
time: 109 us
  waiting for transfers between devices  39.4 us (36%)
  Pallas kernels  34.4 us (32%)
  starting transfers between devices  19 us (17%)
  blocking collectives  13.1 us (12%)
  local copies, waits for them, and re-layouts  1.41 us (1%)
    ppermute x25, waiting for transfers between devices, moved(): return lax.ppermute(value, 'seq', pairs)  37.4 us
    ppermute x25, starting transfers between devices, moved(): return lax.ppermute(value, 'seq', pairs)  17.4 us
    all_to_all x1, blocking collectives, body(): known = lax.all_to_all(info, 'seq', 0, 0, tiled=True)  13.1 us
    pallas_call x4, Pallas kernels, attend_part(): pl.pallas_call(functools.partial(attend_kernel, sizes, shifts, kv_step, g...  10.9 us
    pallas_call x1, Pallas kernels, local_part(): pl.pallas_call(local_kernel, grid=(steps,), in_specs=[wide, wide, pl.Bloc...  9.07 us
    pallas_call x8, Pallas kernels, mixing(): pl.pallas_call(functools.partial(mixing_kernel, body), in_specs=[smem, sm...  6.14 us
    pallas_call x1, Pallas kernels, inside_part(): pl.pallas_call(functools.partial(inside_kernel, len(parts)), in_specs=[pl...  3.27 us
  transfers between devices with their start and end apart: 26, of which 15 were waited for; matrix products, arithmetic and copies ran while one was open for 0% of the time, Pallas kernels for 27%

profile of v4, /device:TPU:0, one launch (start us, length us, event | category | flops | bytes accessed | tf_op | source)
XLA Modules:
  0.0 108.7 jit_solution(15992119022462504332)
XLA Ops:
  1.9 3.1 %collective-permute-start.1 = (bf16[256,1024]{1,0:T(8,128)(2,1)S(1)}, bf16[256,1024]{1,0:T(8,128)(2,1)S(1)}, u32[]{:S(2)}, u32[]{:S(2)}) collective-permute-start(bf16[256,1024]{1,0:T(8,128)(2,1)S(1)} %pad_maximum_fusion.refs_1_), channel_id=1, source_target_pairs={{0,8},{2,10},{4,12},{6,14},{8,16},{10,18},{12,20},{14,22},{16,24},... | collective-permute-start | bytes 1572872 | tf_op jit(solution)/shard_map/ppermute | solution.py:531
  5.0 1.5 %collective-permute-start = (bf16[256,1024]{1,0:T(8,128)(2,1)S(1)}, bf16[256,1024]{1,0:T(8,128)(2,1)S(1)}, u32[]{:S(2)}, u32[]{:S(2)}) collective-permute-start(bf16[256,1024]{1,0:T(8,128)(2,1)S(1)} %pad_maximum_fusion.refs_1_), channel_id=1, source_target_pairs={{0,4},{2,6},{4,0},{6,2},{8,12},{10,14},{12,8},{14,10},{16,20},{18,... | collective-permute-start | bytes 1572872 | tf_op jit(solution)/shard_map/ppermute | solution.py:531
  6.9 13.1 %all_to_all.11 = f32[16,1,128]{2,1,0:T(1,128)S(1)} all-to-all(f32[16,1,128]{2,1,0:T(1,128)S(1)} %bitcast.15), channel_id=1, replica_groups=mesh['seq'=16,'head'=2] {'seq'}, dimensions={0} | all-to-all | bytes 16384 | tf_op jit(solution)/shard_map/all_to_all | solution.py:713
  21.7 1.6 %seen_table.1 = (f32[2,128,128]{2,1,0:T(8,128)S(1)}, f32[2,128,128]{2,1,0:T(8,128)S(1)}, f32[26,8,128]{2,1,0:T(8,128)S(1)}, s32[35]{0:T(128)S(1)}) custom-call(s32[24]{0:T(128)S(1)} %reshape.13.listing, f32[16,128]{1,0:T(8,128)S(1)} %bitcast.13, s32[1]{0:T(128)} %bitcast.7.place_ref, s32[256,1]{1,0:T(8,128)S(1)} %copy.14.segc_ref, s32[1,256]{1,0:T(1,128)S(1)} %bitcast.18), custom_call_target="tpu_custom_call" | custom-call | tf_op jit(solution)/shard_map/seen_table/pallas_call | solution.py:238
  23.3 9.1 %local_scores.1 = (bf16[32,256,256]{2,1,0:T(8,128)(2,1)S(1)}, bf16[32,128,256]{2,1,0:T(8,128)(2,1)S(1)}, bf16[256,4096]{1,0:T(8,128)(2,1)S(1)}) custom-call(bf16[256,4096]{1,0:T(8,128)(2,1)} %q_ref, bf16[256,4096]{1,0:T(8,128)(2,1)} %k_ref, f32[32,256]{1,0:T(8,128)S(1)} %copy-done, s32[256,1]{1,0:T(8,128)S(1)} %copy.14.segc_ref, s32[1,256]{1,0:T(1,128)S(1)} %bitcast.19), custom_call_target="tpu_custom_call" | custom-call | flops 536870912 | bytes 12582912 | tf_op jit(solution)/shard_map/local_scores/pallas_call | solution.py:135
  32.4 3.0 %collective-permute-done.3.refs_7_ = bf16[256,1024]{1,0:T(8,128)(2,1)S(1)} collective-permute-done((bf16[256,1024]{1,0:T(8,128)(2,1)S(1)}, bf16[256,1024]{1,0:T(8,128)(2,1)S(1)}, u32[]{:S(2)}, u32[]{:S(2)}) %collective-permute-start.3) | collective-permute-done | bytes 524320 | tf_op jit(solution)/shard_map/ppermute | solution.py:531
  35.5 1.3 %collective-permute-start.4 = (bf16[256,512]{1,0:T(8,128)(2,1)S(1)}, bf16[256,512]{1,0:T(8,128)(2,1)S(1)}, u32[]{:S(2)}, u32[]{:S(2)}) collective-permute-start(bf16[256,512]{1,0:T(8,128)(2,1)S(1)} %slice.22), channel_id=1, source_target_pairs={{0,4},{2,6},{4,0},{6,2},{8,12},{10,14},{12,8},{14,10},{16,20},{18,... | collective-permute-start | bytes 786440 | tf_op jit(solution)/shard_map/ppermute | solution.py:531
  37.4 7.0 %collective-permute-done.5.refs_10_ = bf16[256,512]{1,0:T(8,128)(2,1)S(1)} collective-permute-done((bf16[256,512]{1,0:T(8,128)(2,1)S(1)}, bf16[256,512]{1,0:T(8,128)(2,1)S(1)}, u32[]{:S(2)}, u32[]{:S(2)}) %collective-permute-start.5) | collective-permute-done | bytes 262176 | tf_op jit(solution)/shard_map/ppermute | solution.py:531
  47.5 2.6 %attend.4 = (bf16[256,1024]{1,0:T(8,128)(2,1)S(1)}, f32[8,128,128]{2,1,0:T(8,128)S(1)}) custom-call(s32[2]{0:T(128)S(1)} %get-tuple-element.66.kv_head, s32[35]{0:T(128)S(1)} %get-tuple-element.69.table, bf16[256,4096]{1,0:T(8,128)(2,1)S(1)} %copy-done.2, bf16[256,1024]{1,0:T(8,128)(2,1)S(1)} %pad_maximum_fusion.refs_1_, ...), custom_call_target="tpu_custom_call" | custom-call | flops 10066329600 | bytes 15728640 | tf_op jit(solution)/shard_map/attend/pallas_call | solution.py:377
  50.6 2.8 %attend.5 = (bf16[256,1024]{1,0:T(8,128)(2,1)S(1)}, f32[8,128,128]{2,1,0:T(8,128)S(1)}) custom-call(s32[2]{0:T(128)S(1)} %get-tuple-element.85.kv_head, s32[35]{0:T(128)S(1)} %get-tuple-element.69.table, bf16[256,4096]{1,0:T(8,128)(2,1)S(1)} %copy-done.2, bf16[256,1024]{1,0:T(8,128)(2,1)S(1)} %pad_maximum_fusion.refs_1_, ...), custom_call_target="tpu_custom_call" | custom-call | flops 10066329600 | bytes 15728640 | tf_op jit(solution)/shard_map/attend/pallas_call | solution.py:377
  54.2 3.3 %collective-permute-start.14 = (bf16[4,128,128]{2,1,0:T(8,128)(2,1)S(1)}, bf16[4,128,128]{2,1,0:T(8,128)(2,1)S(1)}, u32[]{:S(2)}, u32[]{:S(2)}) collective-permute-start(bf16[4,128,128]{2,1,0:T(8,128)(2,1)S(1)} %get-tuple-element.88), channel_id=1, source_target_pairs={{0,4},{2,6},{4,0},{6,2},{8,12},{10,14},{12,8},{14,10},{16,20},{18,... | collective-permute-start | bytes 393224 | tf_op jit(solution)/shard_map/ppermute | solution.py:531
  57.4 2.6 %attend.6 = (bf16[256,1024]{1,0:T(8,128)(2,1)S(1)}, f32[8,128,128]{2,1,0:T(8,128)S(1)}) custom-call(s32[2]{0:T(128)S(1)} %get-tuple-element.89.kv_head, s32[35]{0:T(128)S(1)} %get-tuple-element.69.table, bf16[256,4096]{1,0:T(8,128)(2,1)S(1)} %copy-done.2, bf16[256,1024]{1,0:T(8,128)(2,1)S(1)} %pad_maximum_fusion.refs_1_, ...), custom_call_target="tpu_custom_call" | custom-call | flops 10066329600 | bytes 15728640 | tf_op jit(solution)/shard_map/attend/pallas_call | solution.py:377
  62.4 2.9 %attend.7 = (bf16[256,1024]{1,0:T(8,128)(2,1)S(1)}, f32[8,128,128]{2,1,0:T(8,128)S(1)}) custom-call(s32[2]{0:T(128)S(1)} %get-tuple-element.93.kv_head, s32[35]{0:T(128)S(1)} %get-tuple-element.69.table, bf16[256,4096]{1,0:T(8,128)(2,1)S(1)} %copy-done.2, bf16[256,1024]{1,0:T(8,128)(2,1)S(1)} %pad_maximum_fusion.refs_1_, ...), custom_call_target="tpu_custom_call" | custom-call | flops 10066329600 | bytes 15728640 | tf_op jit(solution)/shard_map/attend/pallas_call | solution.py:377
  65.3 7.8 %collective-permute-done.15.refs_2_ = bf16[4,128,128]{2,1,0:T(8,128)(2,1)S(1)} collective-permute-done((bf16[4,128,128]{2,1,0:T(8,128)(2,1)S(1)}, bf16[4,128,128]{2,1,0:T(8,128)(2,1)S(1)}, u32[]{:S(2)}, u32[]{:S(2)}) %collective-permute-start.15) | collective-permute-done | bytes 131104 | tf_op jit(solution)/shard_map/ppermute | solution.py:531
  74.7 3.3 %inside.1 = (f32[256,4096]{1,0:T(8,128)S(1)}, bf16[256,4096]{1,0:T(8,128)(2,1)}) custom-call(s32[4]{0:T(128)S(1)} %pad_add_fusion.4.order, bf16[32,256,256]{2,1,0:T(8,128)(2,1)S(1)} %get-tuple-element.99.w_ref, bf16[256,1024]{1,0:T(8,128)(2,1)S(1)} %get-tuple-element.84.refs_0_, bf16[256,1024]{1,0:T(8,128)(2,1)S(1)} %get-tuple-element.100.refs_1_, ...), custom_call_target="tpu_custom_call" | custom-call | flops 536870912 | bytes 10485760 | tf_op jit(solution)/shard_map/inside/pallas_call | solution.py:427
  80.2 1.3 %collective-permute-done.17.refs_3_ = bf16[4,128,128]{2,1,0:T(8,128)(2,1)S(1)} collective-permute-done((bf16[4,128,128]{2,1,0:T(8,128)(2,1)S(1)}, bf16[4,128,128]{2,1,0:T(8,128)(2,1)S(1)}, u32[]{:S(2)}, u32[]{:S(2)}) %collective-permute-start.17) | collective-permute-done | bytes 131104 | tf_op jit(solution)/shard_map/ppermute | solution.py:531
  83.5 3.1 %collective-permute-done.20.refs_2_ = bf16[4,128,128]{2,1,0:T(8,128)(2,1)S(1)} collective-permute-done((bf16[4,128,128]{2,1,0:T(8,128)(2,1)S(1)}, bf16[4,128,128]{2,1,0:T(8,128)(2,1)S(1)}, u32[]{:S(2)}, u32[]{:S(2)}) %collective-permute-start.20) | collective-permute-done | bytes 131104 | tf_op jit(solution)/shard_map/ppermute | solution.py:531
  87.3 6.1 %collective-permute-done.21.refs_3_ = bf16[4,128,128]{2,1,0:T(8,128)(2,1)S(1)} collective-permute-done((bf16[4,128,128]{2,1,0:T(8,128)(2,1)S(1)}, bf16[4,128,128]{2,1,0:T(8,128)(2,1)S(1)}, u32[]{:S(2)}, u32[]{:S(2)}) %collective-permute-start.21) | collective-permute-done | bytes 131104 | tf_op jit(solution)/shard_map/ppermute | solution.py:531
  96.1 3.2 %collective-permute-done.22.refs_3_ = bf16[4,128,128]{2,1,0:T(8,128)(2,1)S(1)} collective-permute-done((bf16[4,128,128]{2,1,0:T(8,128)(2,1)S(1)}, bf16[4,128,128]{2,1,0:T(8,128)(2,1)S(1)}, u32[]{:S(2)}, u32[]{:S(2)}) %collective-permute-start.22) | collective-permute-done | bytes 131104 | tf_op jit(solution)/shard_map/ppermute | solution.py:531
  100.2 1.5 %collective-permute-done.24.refs_3_ = bf16[8,128,128]{2,1,0:T(8,128)(2,1)S(1)} collective-permute-done((bf16[8,128,128]{2,1,0:T(8,128)(2,1)S(1)}, bf16[8,128,128]{2,1,0:T(8,128)(2,1)S(1)}, u32[]{:S(2)}, u32[]{:S(2)}) %collective-permute-start.24) | collective-permute-done | bytes 262176 | tf_op jit(solution)/shard_map/ppermute | solution.py:531
  101.7 1.5 %outputs.1 = (f32[256,4096]{1,0:T(8,128)S(1)}, f32[1,256]{1,0:T(1,128)S(1)}) custom-call(s32[1]{0:T(128)} %bitcast.7.place_ref, bf16[256,4096]{1,0:T(8,128)(2,1)S(1)} %get-tuple-element.103.q_ref, f32[256,4096]{1,0:T(8,128)S(1)} %get-tuple-element.104.inside_ref, ...), custom_call_target="tpu_custom_call", output_to_operand_aliasing={{0}: (2, {})} | custom-call | flops 268435456 | bytes 11534336 | tf_op jit(solution)/shard_map/outputs/pallas_call | solution.py:477
  103.2 1.6 %collective-permute-start.25 = (f32[1,256]{1,0:T(1,128)S(1)}, f32[1,256]{1,0:T(1,128)S(1)}, u32[]{:S(2)}, u32[]{:S(2)}) collective-permute-start(f32[1,256]{1,0:T(1,128)S(1)} %get-tuple-element.116), channel_id=1, source_target_pairs={{0,1},{1,0},{2,3},{3,2},{4,5},{5,4},{6,7},{7,6},{8,9},{9,8},{10,11... | collective-permute-start | bytes 3080 | tf_op jit(solution)/shard_map/ppermute | solution.py:777
  104.8 2.0 %collective-permute-done.25 = f32[1,256]{1,0:T(1,128)S(1)} collective-permute-done((f32[1,256]{1,0:T(1,128)S(1)}, f32[1,256]{1,0:T(1,128)S(1)}, u32[]{:S(2)}, u32[]{:S(2)}) %collective-permute-start.25) | collective-permute-done | bytes 1056 | tf_op jit(solution)/shard_map/ppermute | solution.py:777
  106.8 1.7 %scaled.1 = bf16[256,4096]{1,0:T(8,128)(2,1)} custom-call(f32[1,256]{1,0:T(1,128)S(1)} %add.21.squares_ref, f32[256,4096]{1,0:T(8,128)S(1)} %get-tuple-element.117.value_ref), custom_call_target="tpu_custom_call" | custom-call | tf_op jit(solution)/shard_map/scaled/pallas_call | solution.py:519
  (66 shorter events, 20.7 us)
Async XLA Ops:
  1.9 18.1 %collective-permute-start.1 = (bf16[256,1024]{1,0:T(8,128)(2,1)S(1)}, bf16[256,1024]{1,0:T(8,128)(2,1)S(1)}, u32[]{:S(2)}, u32[]{:S(2)}) collective-permute-start(bf16[256,1024]{1,0:T(8,128)(2,1)S(1)} %pad_maximum_fusion.refs_1_), channel_id=1, source_target_pairs={{0,8},{2,10},{4,12},{6,14},{8,16},{10,18},{12,20},{14,22},{16,24},... | collective-permute-start | bytes 1572872 | tf_op jit(solution)/shard_map/ppermute | solution.py:531
  5.0 15.0 %collective-permute-start = (bf16[256,1024]{1,0:T(8,128)(2,1)S(1)}, bf16[256,1024]{1,0:T(8,128)(2,1)S(1)}, u32[]{:S(2)}, u32[]{:S(2)}) collective-permute-start(bf16[256,1024]{1,0:T(8,128)(2,1)S(1)} %pad_maximum_fusion.refs_1_), channel_id=1, source_target_pairs={{0,4},{2,6},{4,0},{6,2},{8,12},{10,14},{12,8},{14,10},{16,20},{18,... | collective-permute-start | bytes 1572872 | tf_op jit(solution)/shard_map/ppermute | solution.py:531
  20.0 15.4 %collective-permute-start.3 = (bf16[256,1024]{1,0:T(8,128)(2,1)S(1)}, bf16[256,1024]{1,0:T(8,128)(2,1)S(1)}, u32[]{:S(2)}, u32[]{:S(2)}) collective-permute-start(bf16[256,1024]{1,0:T(8,128)(2,1)S(1)} %collective-permute-done.1.refs_6_), channel_id=1, source_target_pairs={{0,8},{2,10},{4,12},{6,14},{8,16},{10,18},{12,20},{14,22},{16,24},... | collective-permute-start | bytes 1572872 | tf_op jit(solution)/shard_map/ppermute | solution.py:531
  20.5 14.9 %collective-permute-start.2 = (bf16[256,1024]{1,0:T(8,128)(2,1)S(1)}, bf16[256,1024]{1,0:T(8,128)(2,1)S(1)}, u32[]{:S(2)}, u32[]{:S(2)}) collective-permute-start(bf16[256,1024]{1,0:T(8,128)(2,1)S(1)} %collective-permute-done.1.refs_6_), channel_id=1, source_target_pairs={{0,4},{2,6},{4,0},{6,2},{8,12},{10,14},{12,8},{14,10},{16,20},{18,... | collective-permute-start | bytes 1572872 | tf_op jit(solution)/shard_map/ppermute | solution.py:531
  21.6 23.4 %collective-permute-start.6 = (bf16[256,1024]{1,0:T(8,128)(2,1)S(1)}, bf16[256,1024]{1,0:T(8,128)(2,1)S(1)}, u32[]{:S(2)}, u32[]{:S(2)}) collective-permute-start(bf16[256,1024]{1,0:T(8,128)(2,1)S(1)} %pad_maximum_fusion.refs_1_), channel_id=1, source_target_pairs={{0,2},{2,0},{4,6},{6,4},{8,10},{10,8},{12,14},{14,12},{16,18},{18,... | collective-permute-start | bytes 1572872 | tf_op jit(solution)/shard_map/ppermute | solution.py:531
  35.4 9.0 %collective-permute-start.5 = (bf16[256,512]{1,0:T(8,128)(2,1)S(1)}, bf16[256,512]{1,0:T(8,128)(2,1)S(1)}, u32[]{:S(2)}, u32[]{:S(2)}) collective-permute-start(bf16[256,512]{1,0:T(8,128)(2,1)S(1)} %slice.23), channel_id=1, source_target_pairs={{0,8},{2,10},{4,12},{6,14},{8,16},{10,18},{12,20},{14,22},{16,24},... | collective-permute-start | bytes 786440 | tf_op jit(solution)/shard_map/ppermute | solution.py:531
  35.5 8.9 %collective-permute-start.4 = (bf16[256,512]{1,0:T(8,128)(2,1)S(1)}, bf16[256,512]{1,0:T(8,128)(2,1)S(1)}, u32[]{:S(2)}, u32[]{:S(2)}) collective-permute-start(bf16[256,512]{1,0:T(8,128)(2,1)S(1)} %slice.22), channel_id=1, source_target_pairs={{0,4},{2,6},{4,0},{6,2},{8,12},{10,14},{12,8},{14,10},{16,20},{18,... | collective-permute-start | bytes 786440 | tf_op jit(solution)/shard_map/ppermute | solution.py:531
  36.9 8.3 %collective-permute-start.9 = (bf16[256,1024]{1,0:T(8,128)(2,1)S(1)}, bf16[256,1024]{1,0:T(8,128)(2,1)S(1)}, u32[]{:S(2)}, u32[]{:S(2)}) collective-permute-start(bf16[256,1024]{1,0:T(8,128)(2,1)S(1)} %collective-permute-done.refs_8_), channel_id=1, source_target_pairs={{0,2},{2,0},{4,6},{6,4},{8,10},{10,8},{12,14},{14,12},{16,18},{18,... | collective-permute-start | bytes 1572872 | tf_op jit(solution)/shard_map/ppermute | solution.py:531
  36.9 8.7 %collective-permute-start.7 = (bf16[256,1024]{1,0:T(8,128)(2,1)S(1)}, bf16[256,1024]{1,0:T(8,128)(2,1)S(1)}, u32[]{:S(2)}, u32[]{:S(2)}) collective-permute-start(bf16[256,1024]{1,0:T(8,128)(2,1)S(1)} %collective-permute-done.1.refs_6_), channel_id=1, source_target_pairs={{0,2},{2,0},{4,6},{6,4},{8,10},{10,8},{12,14},{14,12},{16,18},{18,... | collective-permute-start | bytes 1572872 | tf_op jit(solution)/shard_map/ppermute | solution.py:531
  44.4 2.7 %collective-permute-start.10 = (bf16[256,1024]{1,0:T(8,128)(2,1)S(1)}, bf16[256,1024]{1,0:T(8,128)(2,1)S(1)}, u32[]{:S(2)}, u32[]{:S(2)}) collective-permute-start(bf16[256,1024]{1,0:T(8,128)(2,1)S(1)} %collective-permute-done.2.refs_9_), channel_id=1, source_target_pairs={{0,2},{2,0},{4,6},{6,4},{8,10},{10,8},{12,14},{14,12},{16,18},{18,... | collective-permute-start | bytes 1572872 | tf_op jit(solution)/shard_map/ppermute | solution.py:531
  44.9 2.5 %collective-permute-start.11 = (bf16[256,512]{1,0:T(8,128)(2,1)S(1)}, bf16[256,512]{1,0:T(8,128)(2,1)S(1)}, u32[]{:S(2)}, u32[]{:S(2)}) collective-permute-start(bf16[256,512]{1,0:T(8,128)(2,1)S(1)} %collective-permute-done.4.refs_10_), channel_id=1, source_target_pairs={{0,2},{2,0},{4,6},{6,4},{8,10},{10,8},{12,14},{14,12},{16,18},{18,... | collective-permute-start | bytes 786440 | tf_op jit(solution)/shard_map/ppermute | solution.py:531
  45.2 12.3 %collective-permute-start.13 = (bf16[256,512]{1,0:T(8,128)(2,1)S(1)}, bf16[256,512]{1,0:T(8,128)(2,1)S(1)}, u32[]{:S(2)}, u32[]{:S(2)}) collective-permute-start(bf16[256,512]{1,0:T(8,128)(2,1)S(1)} %collective-permute-done.5.refs_10_), channel_id=1, source_target_pairs={{0,2},{2,0},{4,6},{6,4},{8,10},{10,8},{12,14},{14,12},{16,18},{18,... | collective-permute-start | bytes 786440 | tf_op jit(solution)/shard_map/ppermute | solution.py:531
  50.1 3.3 %collective-permute-start.12 = (f32[8,128,128]{2,1,0:T(8,128)S(1)}, f32[8,128,128]{2,1,0:T(8,128)S(1)}, u32[]{:S(2)}, u32[]{:S(2)}) collective-permute-start(f32[8,128,128]{2,1,0:T(8,128)S(1)} %get-tuple-element.87), channel_id=1, source_target_pairs={{0,2},{2,0},{4,6},{6,4},{8,10},{10,8},{12,14},{14,12},{16,18},{18,... | collective-permute-start | bytes 1572872 | tf_op jit(solution)/shard_map/ppermute | solution.py:531
  54.2 7.5 %collective-permute-start.14 = (bf16[4,128,128]{2,1,0:T(8,128)(2,1)S(1)}, bf16[4,128,128]{2,1,0:T(8,128)(2,1)S(1)}, u32[]{:S(2)}, u32[]{:S(2)}) collective-permute-start(bf16[4,128,128]{2,1,0:T(8,128)(2,1)S(1)} %get-tuple-element.88), channel_id=1, source_target_pairs={{0,4},{2,6},{4,0},{6,2},{8,12},{10,14},{12,8},{14,10},{16,20},{18,... | collective-permute-start | bytes 393224 | tf_op jit(solution)/shard_map/ppermute | solution.py:531
  60.1 13.0 %collective-permute-start.16 = (f32[8,128,128]{2,1,0:T(8,128)S(1)}, f32[8,128,128]{2,1,0:T(8,128)S(1)}, u32[]{:S(2)}, u32[]{:S(2)}) collective-permute-start(f32[8,128,128]{2,1,0:T(8,128)S(1)} %get-tuple-element.96), channel_id=1, source_target_pairs={{0,2},{2,0},{4,6},{6,4},{8,10},{10,8},{12,14},{14,12},{16,18},{18,... | collective-permute-start | bytes 1572872 | tf_op jit(solution)/shard_map/ppermute | solution.py:531
  62.3 10.7 %collective-permute-start.15 = (bf16[4,128,128]{2,1,0:T(8,128)(2,1)S(1)}, bf16[4,128,128]{2,1,0:T(8,128)(2,1)S(1)}, u32[]{:S(2)}, u32[]{:S(2)}) collective-permute-start(bf16[4,128,128]{2,1,0:T(8,128)(2,1)S(1)} %mix_plane.2), channel_id=1, source_target_pairs={{0,8},{2,10},{4,12},{6,14},{8,16},{10,18},{12,20},{14,22},{16,24},... | collective-permute-start | bytes 393224 | tf_op jit(solution)/shard_map/ppermute | solution.py:531
  73.8 5.4 %collective-permute-start.19 = (bf16[4,128,128]{2,1,0:T(8,128)(2,1)S(1)}, bf16[4,128,128]{2,1,0:T(8,128)(2,1)S(1)}, u32[]{:S(2)}, u32[]{:S(2)}) collective-permute-start(bf16[4,128,128]{2,1,0:T(8,128)(2,1)S(1)} %get-tuple-element.97), channel_id=1, source_target_pairs={{0,4},{2,6},{4,0},{6,2},{8,12},{10,14},{12,8},{14,10},{16,20},{18,... | collective-permute-start | bytes 393224 | tf_op jit(solution)/shard_map/ppermute | solution.py:531
  74.7 6.8 %collective-permute-start.17 = (bf16[4,128,128]{2,1,0:T(8,128)(2,1)S(1)}, bf16[4,128,128]{2,1,0:T(8,128)(2,1)S(1)}, u32[]{:S(2)}, u32[]{:S(2)}) collective-permute-start(bf16[4,128,128]{2,1,0:T(8,128)(2,1)S(1)} %collective-permute-done.15.refs_2_), channel_id=1, source_target_pairs={{0,8},{2,10},{4,12},{6,14},{8,16},{10,18},{12,20},{14,22},{16,24},... | collective-permute-start | bytes 393224 | tf_op jit(solution)/shard_map/ppermute | solution.py:531
  79.9 6.8 %collective-permute-start.20 = (bf16[4,128,128]{2,1,0:T(8,128)(2,1)S(1)}, bf16[4,128,128]{2,1,0:T(8,128)(2,1)S(1)}, u32[]{:S(2)}, u32[]{:S(2)}) collective-permute-start(bf16[4,128,128]{2,1,0:T(8,128)(2,1)S(1)} %mix_plane.3), channel_id=1, source_target_pairs={{0,8},{2,10},{4,12},{6,14},{8,16},{10,18},{12,20},{14,22},{16,24},... | collective-permute-start | bytes 393224 | tf_op jit(solution)/shard_map/ppermute | solution.py:531
  82.3 5.0 %collective-permute-start.18 = (bf16[4,128,128]{2,1,0:T(8,128)(2,1)S(1)}, bf16[4,128,128]{2,1,0:T(8,128)(2,1)S(1)}, u32[]{:S(2)}, u32[]{:S(2)}) collective-permute-start(bf16[4,128,128]{2,1,0:T(8,128)(2,1)S(1)} %get-tuple-element.106), channel_id=1, source_target_pairs={{0,4},{2,6},{4,0},{6,2},{8,12},{10,14},{12,8},{14,10},{16,20},{18,... | collective-permute-start | bytes 393224 | tf_op jit(solution)/shard_map/ppermute | solution.py:531
  86.7 6.8 %collective-permute-start.21 = (bf16[4,128,128]{2,1,0:T(8,128)(2,1)S(1)}, bf16[4,128,128]{2,1,0:T(8,128)(2,1)S(1)}, u32[]{:S(2)}, u32[]{:S(2)}) collective-permute-start(bf16[4,128,128]{2,1,0:T(8,128)(2,1)S(1)} %collective-permute-done.20.refs_2_), channel_id=1, source_target_pairs={{0,8},{2,10},{4,12},{6,14},{8,16},{10,18},{12,20},{14,22},{16,24},... | collective-permute-start | bytes 393224 | tf_op jit(solution)/shard_map/ppermute | solution.py:531
  94.2 5.0 %collective-permute-start.22 = (bf16[4,128,128]{2,1,0:T(8,128)(2,1)S(1)}, bf16[4,128,128]{2,1,0:T(8,128)(2,1)S(1)}, u32[]{:S(2)}, u32[]{:S(2)}) collective-permute-start(bf16[4,128,128]{2,1,0:T(8,128)(2,1)S(1)} %get-tuple-element.112), channel_id=1, source_target_pairs={{0,4},{2,6},{4,0},{6,2},{8,12},{10,14},{12,8},{14,10},{16,20},{18,... | collective-permute-start | bytes 393224 | tf_op jit(solution)/shard_map/ppermute | solution.py:531
  96.0 4.2 %collective-permute-start.23 = (bf16[8,128,128]{2,1,0:T(8,128)(2,1)S(1)}, bf16[8,128,128]{2,1,0:T(8,128)(2,1)S(1)}, u32[]{:S(2)}, u32[]{:S(2)}) collective-permute-start(bf16[8,128,128]{2,1,0:T(8,128)(2,1)S(1)} %get-tuple-element.114), channel_id=1, source_target_pairs={{0,2},{2,0},{4,6},{6,4},{8,10},{10,8},{12,14},{14,12},{16,18},{18,... | collective-permute-start | bytes 786440 | tf_op jit(solution)/shard_map/ppermute | solution.py:531
  103.2 3.6 %collective-permute-start.25 = (f32[1,256]{1,0:T(1,128)S(1)}, f32[1,256]{1,0:T(1,128)S(1)}, u32[]{:S(2)}, u32[]{:S(2)}) collective-permute-start(f32[1,256]{1,0:T(1,128)S(1)} %get-tuple-element.116), channel_id=1, source_target_pairs={{0,1},{1,0},{2,3},{3,2},{4,5},{5,4},{6,7},{7,6},{8,9},{9,8},{10,11... | collective-permute-start | bytes 3080 | tf_op jit(solution)/shard_map/ppermute | solution.py:777
  (6 other events, 45.2 us)

commit v5 on v4

--- a/solution.py
+++ b/solution.py
@@ -732,7 +732,6 @@
         span = own.shape[1] // 2
         lasts = [moved(below_beside[:, span:], up(shards))]
         lasts.insert(0, moved(second[:, :span], cross(shards)))
-        lasts = after(lasts)
         second_far, below_beside_far = (
             moved(part, core(shards)) for part in (second, below_beside)
         )

time: 109 us -> 109 us (level)
  waiting for transfers between devices: 39.4 us -> 35 us
  starting transfers between devices: 19 us -> 22.7 us
    ppermute x25, waiting for transfers between devices: 37.4 us -> 33 us  [moved(): return lax.ppermute(value, 'seq', pairs)]
    ppermute x25, starting transfers between devices: 17.4 us -> 21.1 us  [moved(): return lax.ppermute(value, 'seq', pairs)]
  transfers between devices with their start and end apart: 26 -> 26, of which waited for: 15 -> 11; matrix products, arithmetic and copies ran while one was open for 0% -> 0% of each run, Pallas kernels for 27% -> 28%
where the time goes in v5:
time: 109 us; the launch traced here: 108 us
  waiting for transfers between devices  35 us (32%)
  Pallas kernels  34.4 us (32%)
  starting transfers between devices  22.7 us (21%)
  blocking collectives  13.1 us (12%)
  local copies, waits for them, and re-layouts  1.41 us (1%)
  between operations  1.1 us (1%)
    ppermute x25, waiting for transfers between devices, moved(): return lax.ppermute(value, 'seq', pairs)  33 us
    ppermute x25, starting transfers between devices, moved(): return lax.ppermute(value, 'seq', pairs)  21.1 us
    all_to_all x1, blocking collectives, body(): known = lax.all_to_all(info, 'seq', 0, 0, tiled=True)  13.1 us
    pallas_call x4, Pallas kernels, attend_part(): pl.pallas_call(functools.partial(attend_kernel, sizes, shifts, kv_step, g...  10.9 us
    pallas_call x1, Pallas kernels, local_part(): pl.pallas_call(local_kernel, grid=(steps,), in_specs=[wide, wide, pl.Bloc...  9.07 us
    pallas_call x8, Pallas kernels, mixing(): pl.pallas_call(functools.partial(mixing_kernel, body), in_specs=[smem, sm...  6.14 us
    pallas_call x1, Pallas kernels, inside_part(): pl.pallas_call(functools.partial(inside_kernel, len(parts)), in_specs=[pl...  3.25 us
  transfers between devices with their start and end apart: 26, of which 11 were waited for; matrix products, arithmetic and copies ran while one was open for 0% of the time, Pallas kernels for 28%

profile of v5, /device:TPU:0, one launch (start us, length us, event | category | flops | bytes accessed | tf_op | source)
XLA Modules:
  0.0 108.0 jit_solution(4021605764941742372)
XLA Ops:
  1.9 3.1 %collective-permute-start.1 = (bf16[256,1024]{1,0:T(8,128)(2,1)S(1)}, bf16[256,1024]{1,0:T(8,128)(2,1)S(1)}, u32[]{:S(2)}, u32[]{:S(2)}) collective-permute-start(bf16[256,1024]{1,0:T(8,128)(2,1)S(1)} %pad_maximum_fusion.refs_1_), channel_id=1, source_target_pairs={{0,8},{2,10},{4,12},{6,14},{8,16},{10,18},{12,20},{14,22},{16,24},... | collective-permute-start | bytes 1572872 | tf_op jit(solution)/shard_map/ppermute | solution.py:531
  6.9 13.1 %all_to_all.11 = f32[16,1,128]{2,1,0:T(1,128)S(1)} all-to-all(f32[16,1,128]{2,1,0:T(1,128)S(1)} %bitcast.15), channel_id=1, replica_groups=mesh['seq'=16,'head'=2] {'seq'}, dimensions={0} | all-to-all | bytes 16384 | tf_op jit(solution)/shard_map/all_to_all | solution.py:713
  22.2 1.6 %seen_table.1 = (f32[2,128,128]{2,1,0:T(8,128)S(1)}, f32[2,128,128]{2,1,0:T(8,128)S(1)}, f32[26,8,128]{2,1,0:T(8,128)S(1)}, s32[35]{0:T(128)S(1)}) custom-call(s32[24]{0:T(128)S(1)} %reshape.13.listing, f32[16,128]{1,0:T(8,128)S(1)} %bitcast.13, s32[1]{0:T(128)} %bitcast.7.place_ref, s32[256,1]{1,0:T(8,128)S(1)} %copy.14.segc_ref, s32[1,256]{1,0:T(1,128)S(1)} %bitcast.18), custom_call_target="tpu_custom_call" | custom-call | tf_op jit(solution)/shard_map/seen_table/pallas_call | solution.py:238
  23.8 9.1 %local_scores.1 = (bf16[32,256,256]{2,1,0:T(8,128)(2,1)S(1)}, bf16[32,128,256]{2,1,0:T(8,128)(2,1)S(1)}, bf16[256,4096]{1,0:T(8,128)(2,1)S(1)}) custom-call(bf16[256,4096]{1,0:T(8,128)(2,1)} %q_ref, bf16[256,4096]{1,0:T(8,128)(2,1)} %k_ref, f32[32,256]{1,0:T(8,128)S(1)} %copy-done, s32[256,1]{1,0:T(8,128)S(1)} %copy.14.segc_ref, s32[1,256]{1,0:T(1,128)S(1)} %bitcast.19), custom_call_target="tpu_custom_call" | custom-call | flops 536870912 | bytes 12582912 | tf_op jit(solution)/shard_map/local_scores/pallas_call | solution.py:135
  33.0 2.4 %collective-permute-done.3.refs_7_ = bf16[256,1024]{1,0:T(8,128)(2,1)S(1)} collective-permute-done((bf16[256,1024]{1,0:T(8,128)(2,1)S(1)}, bf16[256,1024]{1,0:T(8,128)(2,1)S(1)}, u32[]{:S(2)}, u32[]{:S(2)}) %collective-permute-start.3) | collective-permute-done | bytes 524320 | tf_op jit(solution)/shard_map/ppermute | solution.py:531
  37.1 7.1 %collective-permute-done.4.refs_10_ = bf16[256,512]{1,0:T(8,128)(2,1)S(1)} collective-permute-done((bf16[256,512]{1,0:T(8,128)(2,1)S(1)}, bf16[256,512]{1,0:T(8,128)(2,1)S(1)}, u32[]{:S(2)}, u32[]{:S(2)}) %collective-permute-start.4) | collective-permute-done | bytes 262176 | tf_op jit(solution)/shard_map/ppermute | solution.py:531
  44.4 2.6 %collective-permute-done.12.refs_10_ = bf16[256,512]{1,0:T(8,128)(2,1)S(1)} collective-permute-done((bf16[256,512]{1,0:T(8,128)(2,1)S(1)}, bf16[256,512]{1,0:T(8,128)(2,1)S(1)}, u32[]{:S(2)}, u32[]{:S(2)}) %collective-permute-start.12) | collective-permute-done | bytes 262176 | tf_op jit(solution)/shard_map/ppermute | solution.py:531
  47.1 2.6 %attend.4 = (bf16[256,1024]{1,0:T(8,128)(2,1)S(1)}, f32[8,128,128]{2,1,0:T(8,128)S(1)}) custom-call(s32[2]{0:T(128)S(1)} %get-tuple-element.64.kv_head, s32[35]{0:T(128)S(1)} %get-tuple-element.67.table, bf16[256,4096]{1,0:T(8,128)(2,1)S(1)} %copy-done.2, bf16[256,1024]{1,0:T(8,128)(2,1)S(1)} %pad_maximum_fusion.refs_1_, ...), custom_call_target="tpu_custom_call" | custom-call | flops 10066329600 | bytes 15728640 | tf_op jit(solution)/shard_map/attend/pallas_call | solution.py:377
  50.6 2.8 %attend.5 = (bf16[256,1024]{1,0:T(8,128)(2,1)S(1)}, f32[8,128,128]{2,1,0:T(8,128)S(1)}) custom-call(s32[2]{0:T(128)S(1)} %get-tuple-element.82.kv_head, s32[35]{0:T(128)S(1)} %get-tuple-element.67.table, bf16[256,4096]{1,0:T(8,128)(2,1)S(1)} %copy-done.2, bf16[256,1024]{1,0:T(8,128)(2,1)S(1)} %pad_maximum_fusion.refs_1_, ...), custom_call_target="tpu_custom_call" | custom-call | flops 10066329600 | bytes 15728640 | tf_op jit(solution)/shard_map/attend/pallas_call | solution.py:377
  54.1 4.4 %collective-permute-start.14 = (bf16[4,128,128]{2,1,0:T(8,128)(2,1)S(1)}, bf16[4,128,128]{2,1,0:T(8,128)(2,1)S(1)}, u32[]{:S(2)}, u32[]{:S(2)}) collective-permute-start(bf16[4,128,128]{2,1,0:T(8,128)(2,1)S(1)} %get-tuple-element.85), channel_id=1, source_target_pairs={{0,4},{2,6},{4,0},{6,2},{8,12},{10,14},{12,8},{14,10},{16,20},{18,... | collective-permute-start | bytes 393224 | tf_op jit(solution)/shard_map/ppermute | solution.py:531
  58.6 2.6 %attend.6 = (bf16[256,1024]{1,0:T(8,128)(2,1)S(1)}, f32[8,128,128]{2,1,0:T(8,128)S(1)}) custom-call(s32[2]{0:T(128)S(1)} %get-tuple-element.86.kv_head, s32[35]{0:T(128)S(1)} %get-tuple-element.67.table, bf16[256,4096]{1,0:T(8,128)(2,1)S(1)} %copy-done.2, bf16[256,1024]{1,0:T(8,128)(2,1)S(1)} %pad_maximum_fusion.refs_1_, ...), custom_call_target="tpu_custom_call" | custom-call | flops 10066329600 | bytes 15728640 | tf_op jit(solution)/shard_map/attend/pallas_call | solution.py:377
  63.6 2.9 %attend.7 = (bf16[256,1024]{1,0:T(8,128)(2,1)S(1)}, f32[8,128,128]{2,1,0:T(8,128)S(1)}) custom-call(s32[2]{0:T(128)S(1)} %get-tuple-element.89.kv_head, s32[35]{0:T(128)S(1)} %get-tuple-element.67.table, bf16[256,4096]{1,0:T(8,128)(2,1)S(1)} %copy-done.2, bf16[256,1024]{1,0:T(8,128)(2,1)S(1)} %pad_maximum_fusion.refs_1_, ...), custom_call_target="tpu_custom_call" | custom-call | flops 10066329600 | bytes 15728640 | tf_op jit(solution)/shard_map/attend/pallas_call | solution.py:377
  66.4 4.4 %collective-permute-done.15.refs_2_ = bf16[4,128,128]{2,1,0:T(8,128)(2,1)S(1)} collective-permute-done((bf16[4,128,128]{2,1,0:T(8,128)(2,1)S(1)}, bf16[4,128,128]{2,1,0:T(8,128)(2,1)S(1)}, u32[]{:S(2)}, u32[]{:S(2)}) %collective-permute-start.15) | collective-permute-done | bytes 131104 | tf_op jit(solution)/shard_map/ppermute | solution.py:531
  71.6 2.0 %collective-permute-start.19 = (bf16[4,128,128]{2,1,0:T(8,128)(2,1)S(1)}, bf16[4,128,128]{2,1,0:T(8,128)(2,1)S(1)}, u32[]{:S(2)}, u32[]{:S(2)}) collective-permute-start(bf16[4,128,128]{2,1,0:T(8,128)(2,1)S(1)} %get-tuple-element.93), channel_id=1, source_target_pairs={{0,4},{2,6},{4,0},{6,2},{8,12},{10,14},{12,8},{14,10},{16,20},{18,... | collective-permute-start | bytes 393224 | tf_op jit(solution)/shard_map/ppermute | solution.py:531
  73.6 1.6 %collective-permute-start.17 = (bf16[4,128,128]{2,1,0:T(8,128)(2,1)S(1)}, bf16[4,128,128]{2,1,0:T(8,128)(2,1)S(1)}, u32[]{:S(2)}, u32[]{:S(2)}) collective-permute-start(bf16[4,128,128]{2,1,0:T(8,128)(2,1)S(1)} %collective-permute-done.15.refs_2_), channel_id=1, source_target_pairs={{0,8},{2,10},{4,12},{6,14},{8,16},{10,18},{12,20},{14,22},{16,24},... | collective-permute-start | bytes 393224 | tf_op jit(solution)/shard_map/ppermute | solution.py:531
  75.2 3.3 %inside.1 = (f32[256,4096]{1,0:T(8,128)S(1)}, bf16[256,4096]{1,0:T(8,128)(2,1)}) custom-call(s32[4]{0:T(128)S(1)} %pad_add_fusion.4.order, bf16[32,256,256]{2,1,0:T(8,128)(2,1)S(1)} %get-tuple-element.95.w_ref, bf16[256,1024]{1,0:T(8,128)(2,1)S(1)} %get-tuple-element.81.refs_0_, bf16[256,1024]{1,0:T(8,128)(2,1)S(1)} %get-tuple-element.96.refs_1_, ...), custom_call_target="tpu_custom_call" | custom-call | flops 536870912 | bytes 10485760 | tf_op jit(solution)/shard_map/inside/pallas_call | solution.py:427
  79.2 1.8 %collective-permute-start.20 = (bf16[4,128,128]{2,1,0:T(8,128)(2,1)S(1)}, bf16[4,128,128]{2,1,0:T(8,128)(2,1)S(1)}, u32[]{:S(2)}, u32[]{:S(2)}) collective-permute-start(bf16[4,128,128]{2,1,0:T(8,128)(2,1)S(1)} %mix_plane.3), channel_id=1, source_target_pairs={{0,8},{2,10},{4,12},{6,14},{8,16},{10,18},{12,20},{14,22},{16,24},... | collective-permute-start | bytes 393224 | tf_op jit(solution)/shard_map/ppermute | solution.py:531
  82.2 3.8 %collective-permute-done.20.refs_2_ = bf16[4,128,128]{2,1,0:T(8,128)(2,1)S(1)} collective-permute-done((bf16[4,128,128]{2,1,0:T(8,128)(2,1)S(1)}, bf16[4,128,128]{2,1,0:T(8,128)(2,1)S(1)}, u32[]{:S(2)}, u32[]{:S(2)}) %collective-permute-start.20) | collective-permute-done | bytes 131104 | tf_op jit(solution)/shard_map/ppermute | solution.py:531
  86.8 5.9 %collective-permute-done.21.refs_3_ = bf16[4,128,128]{2,1,0:T(8,128)(2,1)S(1)} collective-permute-done((bf16[4,128,128]{2,1,0:T(8,128)(2,1)S(1)}, bf16[4,128,128]{2,1,0:T(8,128)(2,1)S(1)}, u32[]{:S(2)}, u32[]{:S(2)}) %collective-permute-start.21) | collective-permute-done | bytes 131104 | tf_op jit(solution)/shard_map/ppermute | solution.py:531
  94.8 3.8 %collective-permute-done.22.refs_3_ = bf16[4,128,128]{2,1,0:T(8,128)(2,1)S(1)} collective-permute-done((bf16[4,128,128]{2,1,0:T(8,128)(2,1)S(1)}, bf16[4,128,128]{2,1,0:T(8,128)(2,1)S(1)}, u32[]{:S(2)}, u32[]{:S(2)}) %collective-permute-start.22) | collective-permute-done | bytes 131104 | tf_op jit(solution)/shard_map/ppermute | solution.py:531
  99.5 1.5 %collective-permute-done.24.refs_3_ = bf16[8,128,128]{2,1,0:T(8,128)(2,1)S(1)} collective-permute-done((bf16[8,128,128]{2,1,0:T(8,128)(2,1)S(1)}, bf16[8,128,128]{2,1,0:T(8,128)(2,1)S(1)}, u32[]{:S(2)}, u32[]{:S(2)}) %collective-permute-start.24) | collective-permute-done | bytes 262176 | tf_op jit(solution)/shard_map/ppermute | solution.py:531
  102.5 1.6 %collective-permute-start.25 = (f32[1,256]{1,0:T(1,128)S(1)}, f32[1,256]{1,0:T(1,128)S(1)}, u32[]{:S(2)}, u32[]{:S(2)}) collective-permute-start(f32[1,256]{1,0:T(1,128)S(1)} %get-tuple-element.112), channel_id=1, source_target_pairs={{0,1},{1,0},{2,3},{3,2},{4,5},{5,4},{6,7},{7,6},{8,9},{9,8},{10,11... | collective-permute-start | bytes 3080 | tf_op jit(solution)/shard_map/ppermute | solution.py:776
  104.1 2.0 %collective-permute-done.25 = f32[1,256]{1,0:T(1,128)S(1)} collective-permute-done((f32[1,256]{1,0:T(1,128)S(1)}, f32[1,256]{1,0:T(1,128)S(1)}, u32[]{:S(2)}, u32[]{:S(2)}) %collective-permute-start.25) | collective-permute-done | bytes 1056 | tf_op jit(solution)/shard_map/ppermute | solution.py:776
  106.1 1.7 %scaled.1 = bf16[256,4096]{1,0:T(8,128)(2,1)} custom-call(f32[1,256]{1,0:T(1,128)S(1)} %add.21.squares_ref, f32[256,4096]{1,0:T(8,128)S(1)} %get-tuple-element.113.value_ref), custom_call_target="tpu_custom_call" | custom-call | tf_op jit(solution)/shard_map/scaled/pallas_call | solution.py:519
  (66 shorter events, 19.2 us)
Async XLA Ops:
  1.9 18.1 %collective-permute-start.1 = (bf16[256,1024]{1,0:T(8,128)(2,1)S(1)}, bf16[256,1024]{1,0:T(8,128)(2,1)S(1)}, u32[]{:S(2)}, u32[]{:S(2)}) collective-permute-start(bf16[256,1024]{1,0:T(8,128)(2,1)S(1)} %pad_maximum_fusion.refs_1_), channel_id=1, source_target_pairs={{0,8},{2,10},{4,12},{6,14},{8,16},{10,18},{12,20},{14,22},{16,24},... | collective-permute-start | bytes 1572872 | tf_op jit(solution)/shard_map/ppermute | solution.py:531
  5.0 15.0 %collective-permute-start = (bf16[256,1024]{1,0:T(8,128)(2,1)S(1)}, bf16[256,1024]{1,0:T(8,128)(2,1)S(1)}, u32[]{:S(2)}, u32[]{:S(2)}) collective-permute-start(bf16[256,1024]{1,0:T(8,128)(2,1)S(1)} %pad_maximum_fusion.refs_1_), channel_id=1, source_target_pairs={{0,4},{2,6},{4,0},{6,2},{8,12},{10,14},{12,8},{14,10},{16,20},{18,... | collective-permute-start | bytes 1572872 | tf_op jit(solution)/shard_map/ppermute | solution.py:531
  20.0 15.4 %collective-permute-start.3 = (bf16[256,1024]{1,0:T(8,128)(2,1)S(1)}, bf16[256,1024]{1,0:T(8,128)(2,1)S(1)}, u32[]{:S(2)}, u32[]{:S(2)}) collective-permute-start(bf16[256,1024]{1,0:T(8,128)(2,1)S(1)} %collective-permute-done.1.refs_6_), channel_id=1, source_target_pairs={{0,8},{2,10},{4,12},{6,14},{8,16},{10,18},{12,20},{14,22},{16,24},... | collective-permute-start | bytes 1572872 | tf_op jit(solution)/shard_map/ppermute | solution.py:531
  20.5 14.9 %collective-permute-start.2 = (bf16[256,1024]{1,0:T(8,128)(2,1)S(1)}, bf16[256,1024]{1,0:T(8,128)(2,1)S(1)}, u32[]{:S(2)}, u32[]{:S(2)}) collective-permute-start(bf16[256,1024]{1,0:T(8,128)(2,1)S(1)} %collective-permute-done.1.refs_6_), channel_id=1, source_target_pairs={{0,4},{2,6},{4,0},{6,2},{8,12},{10,14},{12,8},{14,10},{16,20},{18,... | collective-permute-start | bytes 1572872 | tf_op jit(solution)/shard_map/ppermute | solution.py:531
  21.6 14.9 %collective-permute-start.5 = (bf16[256,1024]{1,0:T(8,128)(2,1)S(1)}, bf16[256,1024]{1,0:T(8,128)(2,1)S(1)}, u32[]{:S(2)}, u32[]{:S(2)}) collective-permute-start(bf16[256,1024]{1,0:T(8,128)(2,1)S(1)} %pad_maximum_fusion.refs_1_), channel_id=1, source_target_pairs={{0,2},{2,0},{4,6},{6,4},{8,10},{10,8},{12,14},{14,12},{16,18},{18,... | collective-permute-start | bytes 1572872 | tf_op jit(solution)/shard_map/ppermute | solution.py:531
  21.6 15.0 %collective-permute-start.8 = (bf16[256,1024]{1,0:T(8,128)(2,1)S(1)}, bf16[256,1024]{1,0:T(8,128)(2,1)}, u32[]{:S(2)}, u32[]{:S(2)}) collective-permute-start(bf16[256,1024]{1,0:T(8,128)(2,1)S(1)} %collective-permute-done.refs_8_), channel_id=1, source_target_pairs={{0,2},{2,0},{4,6},{6,4},{8,10},{10,8},{12,14},{14,12},{16,18},{18,... | collective-permute-start | bytes 1572872 | tf_op jit(solution)/shard_map/ppermute | solution.py:531
  32.9 14.1 %collective-permute-start.6 = (bf16[256,1024]{1,0:T(8,128)(2,1)S(1)}, bf16[256,1024]{1,0:T(8,128)(2,1)S(1)}, u32[]{:S(2)}, u32[]{:S(2)}) collective-permute-start(bf16[256,1024]{1,0:T(8,128)(2,1)S(1)} %collective-permute-done.1.refs_6_), channel_id=1, source_target_pairs={{0,2},{2,0},{4,6},{6,4},{8,10},{10,8},{12,14},{14,12},{16,18},{18,... | collective-permute-start | bytes 1572872 | tf_op jit(solution)/shard_map/ppermute | solution.py:531
  35.4 11.6 %collective-permute-start.7 = (bf16[256,1024]{1,0:T(8,128)(2,1)S(1)}, bf16[256,1024]{1,0:T(8,128)(2,1)S(1)}, u32[]{:S(2)}, u32[]{:S(2)}) collective-permute-start(bf16[256,1024]{1,0:T(8,128)(2,1)S(1)} %collective-permute-done.3.refs_7_), channel_id=1, source_target_pairs={{0,2},{2,0},{4,6},{6,4},{8,10},{10,8},{12,14},{14,12},{16,18},{18,... | collective-permute-start | bytes 1572872 | tf_op jit(solution)/shard_map/ppermute | solution.py:531
  35.5 8.7 %collective-permute-start.4 = (bf16[256,512]{1,0:T(8,128)(2,1)S(1)}, bf16[256,512]{1,0:T(8,128)(2,1)S(1)}, u32[]{:S(2)}, u32[]{:S(2)}) collective-permute-start(bf16[256,512]{1,0:T(8,128)(2,1)S(1)} %slice.22), channel_id=1, source_target_pairs={{0,4},{2,6},{4,0},{6,2},{8,12},{10,14},{12,8},{14,10},{16,20},{18,... | collective-permute-start | bytes 786440 | tf_op jit(solution)/shard_map/ppermute | solution.py:531
  36.4 10.6 %collective-permute-start.9 = (bf16[256,1024]{1,0:T(8,128)(2,1)S(1)}, bf16[256,1024]{1,0:T(8,128)(2,1)S(1)}, u32[]{:S(2)}, u32[]{:S(2)}) collective-permute-start(bf16[256,1024]{1,0:T(8,128)(2,1)S(1)} %collective-permute-done.2.refs_9_), channel_id=1, source_target_pairs={{0,2},{2,0},{4,6},{6,4},{8,10},{10,8},{12,14},{14,12},{16,18},{18,... | collective-permute-start | bytes 1572872 | tf_op jit(solution)/shard_map/ppermute | solution.py:531
  36.6 10.4 %collective-permute-start.12 = (bf16[256,512]{1,0:T(8,128)(2,1)S(1)}, bf16[256,512]{1,0:T(8,128)(2,1)S(1)}, u32[]{:S(2)}, u32[]{:S(2)}) collective-permute-start(bf16[256,512]{1,0:T(8,128)(2,1)S(1)} %slice.23), channel_id=1, source_target_pairs={{0,8},{2,10},{4,12},{6,14},{8,16},{10,18},{12,20},{14,22},{16,24},... | collective-permute-start | bytes 786440 | tf_op jit(solution)/shard_map/ppermute | solution.py:531
  47.0 11.6 %collective-permute-start.13 = (bf16[256,512]{1,0:T(8,128)(2,1)S(1)}, bf16[256,512]{1,0:T(8,128)(2,1)S(1)}, u32[]{:S(2)}, u32[]{:S(2)}) collective-permute-start(bf16[256,512]{1,0:T(8,128)(2,1)S(1)} %collective-permute-done.12.refs_10_), channel_id=1, source_target_pairs={{0,2},{2,0},{4,6},{6,4},{8,10},{10,8},{12,14},{14,12},{16,18},{18,... | collective-permute-start | bytes 786440 | tf_op jit(solution)/shard_map/ppermute | solution.py:531
  49.7 3.7 %collective-permute-start.11 = (f32[8,128,128]{2,1,0:T(8,128)S(1)}, f32[8,128,128]{2,1,0:T(8,128)S(1)}, u32[]{:S(2)}, u32[]{:S(2)}) collective-permute-start(f32[8,128,128]{2,1,0:T(8,128)S(1)} %get-tuple-element.84), channel_id=1, source_target_pairs={{0,2},{2,0},{4,6},{6,4},{8,10},{10,8},{12,14},{14,12},{16,18},{18,... | collective-permute-start | bytes 1572872 | tf_op jit(solution)/shard_map/ppermute | solution.py:531
  54.1 8.6 %collective-permute-start.14 = (bf16[4,128,128]{2,1,0:T(8,128)(2,1)S(1)}, bf16[4,128,128]{2,1,0:T(8,128)(2,1)S(1)}, u32[]{:S(2)}, u32[]{:S(2)}) collective-permute-start(bf16[4,128,128]{2,1,0:T(8,128)(2,1)S(1)} %get-tuple-element.85), channel_id=1, source_target_pairs={{0,4},{2,6},{4,0},{6,2},{8,12},{10,14},{12,8},{14,10},{16,20},{18,... | collective-permute-start | bytes 393224 | tf_op jit(solution)/shard_map/ppermute | solution.py:531
  61.2 9.7 %collective-permute-start.16 = (f32[8,128,128]{2,1,0:T(8,128)S(1)}, f32[8,128,128]{2,1,0:T(8,128)S(1)}, u32[]{:S(2)}, u32[]{:S(2)}) collective-permute-start(f32[8,128,128]{2,1,0:T(8,128)S(1)} %get-tuple-element.92), channel_id=1, source_target_pairs={{0,2},{2,0},{4,6},{6,4},{8,10},{10,8},{12,14},{14,12},{16,18},{18,... | collective-permute-start | bytes 1572872 | tf_op jit(solution)/shard_map/ppermute | solution.py:531
  63.5 7.4 %collective-permute-start.15 = (bf16[4,128,128]{2,1,0:T(8,128)(2,1)S(1)}, bf16[4,128,128]{2,1,0:T(8,128)(2,1)S(1)}, u32[]{:S(2)}, u32[]{:S(2)}) collective-permute-start(bf16[4,128,128]{2,1,0:T(8,128)(2,1)S(1)} %mix_plane.2), channel_id=1, source_target_pairs={{0,8},{2,10},{4,12},{6,14},{8,16},{10,18},{12,20},{14,22},{16,24},... | collective-permute-start | bytes 393224 | tf_op jit(solution)/shard_map/ppermute | solution.py:531
  71.6 6.8 %collective-permute-start.19 = (bf16[4,128,128]{2,1,0:T(8,128)(2,1)S(1)}, bf16[4,128,128]{2,1,0:T(8,128)(2,1)S(1)}, u32[]{:S(2)}, u32[]{:S(2)}) collective-permute-start(bf16[4,128,128]{2,1,0:T(8,128)(2,1)S(1)} %get-tuple-element.93), channel_id=1, source_target_pairs={{0,4},{2,6},{4,0},{6,2},{8,12},{10,14},{12,8},{14,10},{16,20},{18,... | collective-permute-start | bytes 393224 | tf_op jit(solution)/shard_map/ppermute | solution.py:531
  73.6 7.4 %collective-permute-start.17 = (bf16[4,128,128]{2,1,0:T(8,128)(2,1)S(1)}, bf16[4,128,128]{2,1,0:T(8,128)(2,1)S(1)}, u32[]{:S(2)}, u32[]{:S(2)}) collective-permute-start(bf16[4,128,128]{2,1,0:T(8,128)(2,1)S(1)} %collective-permute-done.15.refs_2_), channel_id=1, source_target_pairs={{0,8},{2,10},{4,12},{6,14},{8,16},{10,18},{12,20},{14,22},{16,24},... | collective-permute-start | bytes 393224 | tf_op jit(solution)/shard_map/ppermute | solution.py:531
  79.2 6.8 %collective-permute-start.20 = (bf16[4,128,128]{2,1,0:T(8,128)(2,1)S(1)}, bf16[4,128,128]{2,1,0:T(8,128)(2,1)S(1)}, u32[]{:S(2)}, u32[]{:S(2)}) collective-permute-start(bf16[4,128,128]{2,1,0:T(8,128)(2,1)S(1)} %mix_plane.3), channel_id=1, source_target_pairs={{0,8},{2,10},{4,12},{6,14},{8,16},{10,18},{12,20},{14,22},{16,24},... | collective-permute-start | bytes 393224 | tf_op jit(solution)/shard_map/ppermute | solution.py:531
  81.8 5.0 %collective-permute-start.18 = (bf16[4,128,128]{2,1,0:T(8,128)(2,1)S(1)}, bf16[4,128,128]{2,1,0:T(8,128)(2,1)S(1)}, u32[]{:S(2)}, u32[]{:S(2)}) collective-permute-start(bf16[4,128,128]{2,1,0:T(8,128)(2,1)S(1)} %get-tuple-element.102), channel_id=1, source_target_pairs={{0,4},{2,6},{4,0},{6,2},{8,12},{10,14},{12,8},{14,10},{16,20},{18,... | collective-permute-start | bytes 393224 | tf_op jit(solution)/shard_map/ppermute | solution.py:531
  86.0 6.8 %collective-permute-start.21 = (bf16[4,128,128]{2,1,0:T(8,128)(2,1)S(1)}, bf16[4,128,128]{2,1,0:T(8,128)(2,1)S(1)}, u32[]{:S(2)}, u32[]{:S(2)}) collective-permute-start(bf16[4,128,128]{2,1,0:T(8,128)(2,1)S(1)} %collective-permute-done.20.refs_2_), channel_id=1, source_target_pairs={{0,8},{2,10},{4,12},{6,14},{8,16},{10,18},{12,20},{14,22},{16,24},... | collective-permute-start | bytes 393224 | tf_op jit(solution)/shard_map/ppermute | solution.py:531
  93.5 5.0 %collective-permute-start.22 = (bf16[4,128,128]{2,1,0:T(8,128)(2,1)S(1)}, bf16[4,128,128]{2,1,0:T(8,128)(2,1)S(1)}, u32[]{:S(2)}, u32[]{:S(2)}) collective-permute-start(bf16[4,128,128]{2,1,0:T(8,128)(2,1)S(1)} %get-tuple-element.108), channel_id=1, source_target_pairs={{0,4},{2,6},{4,0},{6,2},{8,12},{10,14},{12,8},{14,10},{16,20},{18,... | collective-permute-start | bytes 393224 | tf_op jit(solution)/shard_map/ppermute | solution.py:531
  94.7 4.8 %collective-permute-start.23 = (bf16[8,128,128]{2,1,0:T(8,128)(2,1)S(1)}, bf16[8,128,128]{2,1,0:T(8,128)(2,1)S(1)}, u32[]{:S(2)}, u32[]{:S(2)}) collective-permute-start(bf16[8,128,128]{2,1,0:T(8,128)(2,1)S(1)} %get-tuple-element.110), channel_id=1, source_target_pairs={{0,2},{2,0},{4,6},{6,4},{8,10},{10,8},{12,14},{14,12},{16,18},{18,... | collective-permute-start | bytes 786440 | tf_op jit(solution)/shard_map/ppermute | solution.py:531
  102.5 3.6 %collective-permute-start.25 = (f32[1,256]{1,0:T(1,128)S(1)}, f32[1,256]{1,0:T(1,128)S(1)}, u32[]{:S(2)}, u32[]{:S(2)}) collective-permute-start(f32[1,256]{1,0:T(1,128)S(1)} %get-tuple-element.112), channel_id=1, source_target_pairs={{0,1},{1,0},{2,3},{3,2},{4,5},{5,4},{6,7},{7,6},{8,9},{9,8},{10,11... | collective-permute-start | bytes 3080 | tf_op jit(solution)/shard_map/ppermute | solution.py:776
  (6 other events, 45.2 us)
